TPU v7x, 32 devices: a whole 2x2x4 slice. The times are simulated.
32 devices in a mesh: dp: 16 (over z, y, x), mp: 2 (over core).
Axes of the slice: x: 2, y: 2, z: 4, core: 2. Of those that a mesh axis runs over, the one named last changes fastest.
Arguments:
- tokens: bfloat16 [36864, 768], P(('dp', 'mp')), may hold values from -6 to 6
- lengths: int32 [64], P('dp'), may hold values from 256 to 576, as said below
- gain_attn: float32 [768], replicated, may hold values from 0.5 to 1.5
- w_query: bfloat16 [768, 768], P(None, 'mp'), may hold values from -0.21875 to 0.21875
- w_key: bfloat16 [768, 768], P(None, 'mp'), may hold values from -0.21875 to 0.21875
- w_value: bfloat16 [768, 768], P(None, 'mp'), may hold values from -0.21875 to 0.21875
- w_out: bfloat16 [768, 768], P('mp'), may hold values from -1.75 to 1.75
- gain_ffn: float32 [768], replicated, may hold values from 0.5 to 1.5
- w_gate: bfloat16 [768, 2048], P(None, 'mp'), may hold values from -0.21875 to 0.21875
- w_up: bfloat16 [768, 2048], P(None, 'mp'), may hold values from -0.21875 to 0.21875
- w_down: bfloat16 [2048, 768], P('mp'), may hold values from -0.125 to 0.125
- cotangent: bfloat16 [36864, 768], P(('dp', 'mp')), may hold values from -6 to 6
Outputs:
- output: bfloat16 [36864, 768], P(('dp', 'mp'))
- grad_input: float32 [36864, 768], P(('dp', 'mp'))
- grad_gain_attn: float32 [768], replicated
- grad_query: float32 [768, 768], P('dp', 'mp')
- grad_key: float32 [768, 768], P('dp', 'mp')
- grad_value: float32 [768, 768], P('dp', 'mp')
- grad_out: float32 [768, 768], P('mp', 'dp')
- grad_gain_ffn: float32 [768], replicated
- grad_gate: float32 [768, 2048], P('dp', 'mp')
- grad_up: float32 [768, 2048], P('dp', 'mp')
- grad_down: float32 [2048, 768], P('mp', 'dp')
Inputs may be any that keep to these rules, and one draw needn't show every extreme that they name: `lengths`: each item's count of valid tokens, the class token first; exactly half of the 64 items have 576 and the other half 256.
All inputs are finite; a program needn't handle non-finite values.
Results may differ from a plain program's by a relative error of at most 0.013.
Values may be sent and summed in bfloat16 or wider, within the bound.
No kernel may reach another device: no remote copies, remote signals or barrier semaphores. Data moves between devices by JAX's collectives and lax.ppermute only.
A program may use at most 192 MiB of HBM per device.

v0:
```python
import jax
import jax.numpy as jnp
from jax import lax
from jax.sharding import PartitionSpec as P

HEAD = 64
SLOTS = 576


EPS = 1e-05
THETA = 10000.0


def tables(row_count):
    places = (jnp.arange(row_count) % SLOTS).astype(jnp.float32)
    inv_freq = THETA ** (-(2.0 * jnp.arange(HEAD // 2).astype(jnp.float32)) / HEAD)
    angles = places[:, None] * inv_freq[None, :]
    return (jnp.cos(angles), jnp.sin(angles))


def rotate(values, cosine, sine):
    half_width = values.shape[-1] // 2
    first_half = values[..., :half_width]
    second = values[..., half_width:]
    cos_b = cosine[:, None, :]
    sin_b = sine[:, None, :]
    return jnp.concatenate(
        [first_half * cos_b - second * sin_b, second * cos_b + first_half * sin_b], -1
    )


def unrotate(values, cosine, sine):
    half_width = values.shape[-1] // 2
    first_half = values[..., :half_width]
    second = values[..., half_width:]
    cos_b = cosine[:, None, :]
    sin_b = sine[:, None, :]
    return jnp.concatenate(
        [first_half * cos_b + second * sin_b, second * cos_b - first_half * sin_b], -1
    )


def contract_rows(left, right):
    return lax.dot_general(
        left, right, (((0,), (0,)), ((), ())), preferred_element_type=jnp.float32
    )


def contract_cols(left, right):
    return lax.dot_general(
        left, right, (((1,), (1,)), ((), ())), preferred_element_type=jnp.float32
    )


def norm_back(inputs, inv_rms, gain, d_normed):
    weighted = d_normed * gain
    d_inputs = inv_rms * weighted - inputs * inv_rms**3 * jnp.mean(
        weighted * inputs, -1, keepdims=True
    )
    d_gain = jnp.sum(d_normed * inputs * inv_rms, 0)
    return (d_inputs, d_gain)


def local(
    tokens,
    lengths,
    gain_attn,
    w_query,
    w_key,
    w_value,
    w_out,
    gain_ffn,
    w_gate,
    w_up,
    w_down,
    cotangent,
):
    half_rows = tokens.shape[0]
    score_scale = HEAD ** (-0.5)
    q_weight, k_weight, v_weight, o_weight = (w_query, w_key, w_value, w_out)
    g_weight, u_weight, d_weight = (w_gate, w_up, w_down)
    local_cols = q_weight.shape[1]
    head_count = local_cols // HEAD
    resid_in = tokens.astype(jnp.float32)
    inv_rms_a = lax.rsqrt(jnp.mean(resid_in * resid_in, -1, keepdims=True) + EPS)
    normed_a = (resid_in * inv_rms_a * gain_attn).astype(jnp.bfloat16)
    gathered_a = lax.all_gather(normed_a, "mp", axis=0, tiled=True)
    all_rows = gathered_a.shape[0]
    item_count = all_rows // SLOTS
    item_shape = (item_count, SLOTS, head_count, HEAD)
    cosine, sine = tables(all_rows)
    queries = rotate(
        jnp.dot(gathered_a, q_weight, preferred_element_type=jnp.float32).reshape(
            all_rows, head_count, HEAD
        ),
        cosine,
        sine,
    ).astype(jnp.bfloat16)
    key_heads = rotate(
        jnp.dot(gathered_a, k_weight, preferred_element_type=jnp.float32).reshape(
            all_rows, head_count, HEAD
        ),
        cosine,
        sine,
    ).astype(jnp.bfloat16)
    value_heads = jnp.dot(gathered_a, v_weight, preferred_element_type=jnp.float32).astype(
        jnp.bfloat16
    )
    q_items = queries.reshape(item_shape)
    k_items = key_heads.reshape(item_shape)
    v_items = value_heads.reshape(item_shape)
    places = jnp.arange(SLOTS)

    def masked_scores(q_item, k_item, length):
        scores = (
            jnp.einsum("qhd,khd->hqk", q_item, k_item, preferred_element_type=jnp.float32)
            * score_scale
        )
        allowed = (places[None, :] <= places[:, None]) & (places[None, :] < length)
        return jnp.where(allowed[None], scores, -1e30)

    def attend(item_args):
        q_item, k_item, v_item, length = item_args
        scores = masked_scores(q_item, k_item, length)
        top_score = jnp.max(scores, -1, keepdims=True)
        expo = jnp.exp(scores - top_score)
        total = jnp.sum(expo, -1, keepdims=True)
        soft_probs = (expo / total).astype(jnp.bfloat16)
        mixed_item = jnp.einsum(
            "hqk,khd->qhd", soft_probs, v_item, preferred_element_type=jnp.float32
        )
        return (mixed_item.astype(jnp.bfloat16), (top_score + jnp.log(total))[..., 0])

    mixed_heads, log_norm = lax.map(attend, (q_items, k_items, v_items, lengths))
    attn_rows = mixed_heads.reshape(all_rows, local_cols)
    attn_branch = lax.psum_scatter(
        jnp.dot(attn_rows, o_weight, preferred_element_type=jnp.float32),
        "mp",
        scatter_dimension=0,
        tiled=True,
    )
    middle = resid_in + attn_branch
    inv_rms_f = lax.rsqrt(jnp.mean(middle * middle, -1, keepdims=True) + EPS)
    normed_f = (middle * inv_rms_f * gain_ffn).astype(jnp.bfloat16)
    gathered_f = lax.all_gather(normed_f, "mp", axis=0, tiled=True)
    gate_pre = jnp.dot(gathered_f, g_weight, preferred_element_type=jnp.float32)
    up_pre = jnp.dot(gathered_f, u_weight, preferred_element_type=jnp.float32)
    sigmoid_g = jax.nn.sigmoid(gate_pre)
    silu_g = gate_pre * sigmoid_g
    hidden = (silu_g * up_pre).astype(jnp.bfloat16)
    ffn_branch = lax.psum_scatter(
        jnp.dot(hidden, d_weight, preferred_element_type=jnp.float32).astype(jnp.bfloat16),
        "mp",
        scatter_dimension=0,
        tiled=True,
    ).astype(jnp.float32)
    row_index = lax.axis_index("mp") * half_rows + jnp.arange(half_rows)
    final_rows = middle + ffn_branch
    owner = (row_index // SLOTS)[:, None] == jnp.arange(item_count)[None, :]
    limit = jnp.sum(jnp.where(owner, lengths[None, :], 0), 1)
    valid_rows = (row_index % SLOTS < limit).astype(jnp.float32)[:, None]
    output = (valid_rows * final_rows).astype(jnp.bfloat16)
    d_final = valid_rows * cotangent.astype(jnp.float32)
    d_ffn_all = lax.all_gather(d_final.astype(jnp.bfloat16), "mp", axis=0, tiled=True)
    grad_down = contract_rows(hidden, d_ffn_all)
    d_hidden = contract_cols(d_ffn_all, d_weight)
    d_gate = (d_hidden * up_pre * (sigmoid_g * (1.0 + gate_pre * (1.0 - sigmoid_g)))).astype(
        jnp.bfloat16
    )
    d_up = (d_hidden * silu_g).astype(jnp.bfloat16)
    grad_gate = contract_rows(gathered_f, d_gate)
    grad_up = contract_rows(gathered_f, d_up)
    ffn_sums = (
        lax.psum_scatter(grad_gate, "dp", scatter_dimension=0, tiled=True),
        lax.psum_scatter(grad_up, "dp", scatter_dimension=0, tiled=True),
        lax.psum_scatter(grad_down, "dp", scatter_dimension=1, tiled=True),
    )
    d_normed_f = lax.psum_scatter(
        contract_cols(d_gate, g_weight) + contract_cols(d_up, u_weight),
        "mp",
        scatter_dimension=0,
        tiled=True,
    )
    d_middle_norm, d_gain_ffn = norm_back(middle, inv_rms_f, gain_ffn, d_normed_f)
    d_middle = d_final + d_middle_norm
    d_attn_all = lax.all_gather(d_middle.astype(jnp.bfloat16), "mp", axis=0, tiled=True)
    grad_out = contract_rows(attn_rows, d_attn_all)
    d_mixed = contract_cols(d_attn_all, o_weight).astype(jnp.bfloat16).reshape(item_shape)

    def attend_back(item_args):
        q_item, k_item, v_item, length, norm_item, d_item = item_args
        scores = masked_scores(q_item, k_item, length)
        soft_probs = jnp.exp(scores - norm_item[..., None])
        d_value = jnp.einsum(
            "hqk,qhd->khd",
            soft_probs.astype(jnp.bfloat16),
            d_item,
            preferred_element_type=jnp.float32,
        )
        d_soft = jnp.einsum("qhd,khd->hqk", d_item, v_item, preferred_element_type=jnp.float32)
        d_scores = (soft_probs * (d_soft - jnp.sum(soft_probs * d_soft, -1, keepdims=True))).astype(
            jnp.bfloat16
        )
        d_query = (
            jnp.einsum("hqk,khd->qhd", d_scores, k_item, preferred_element_type=jnp.float32)
            * score_scale
        )
        d_key = (
            jnp.einsum("hqk,qhd->khd", d_scores, q_item, preferred_element_type=jnp.float32)
            * score_scale
        )
        return (d_query, d_key, d_value)

    d_queries, d_keys, d_values = lax.map(
        attend_back, (q_items, k_items, v_items, lengths, log_norm, d_mixed)
    )
    d_q_rows = (
        unrotate(d_queries.reshape(all_rows, head_count, HEAD), cosine, sine)
        .astype(jnp.bfloat16)
        .reshape(all_rows, local_cols)
    )
    d_k_rows = (
        unrotate(d_keys.reshape(all_rows, head_count, HEAD), cosine, sine)
        .astype(jnp.bfloat16)
        .reshape(all_rows, local_cols)
    )
    d_v_rows = d_values.astype(jnp.bfloat16).reshape(all_rows, local_cols)
    grad_query = contract_rows(gathered_a, d_q_rows)
    grad_key = contract_rows(gathered_a, d_k_rows)
    grad_value = contract_rows(gathered_a, d_v_rows)
    d_normed_a = lax.psum_scatter(
        contract_cols(d_q_rows, q_weight)
        + contract_cols(d_k_rows, k_weight)
        + contract_cols(d_v_rows, v_weight),
        "mp",
        scatter_dimension=0,
        tiled=True,
    )
    d_input_norm, d_gain_attn = norm_back(resid_in, inv_rms_a, gain_attn, d_normed_a)
    grad_input = d_middle + d_input_norm
    gain_grads = lax.psum((d_gain_attn, d_gain_ffn), ("dp", "mp"))
    attn_sums = (
        lax.psum_scatter(grad_query, "dp", scatter_dimension=0, tiled=True),
        lax.psum_scatter(grad_key, "dp", scatter_dimension=0, tiled=True),
        lax.psum_scatter(grad_value, "dp", scatter_dimension=0, tiled=True),
        lax.psum_scatter(grad_out, "dp", scatter_dimension=1, tiled=True),
    )
    summed = (
        attn_sums[0],
        attn_sums[1],
        attn_sums[2],
        attn_sums[3],
        ffn_sums[0],
        ffn_sums[1],
        ffn_sums[2],
    )
    return (
        output,
        grad_input,
        gain_grads[0],
        summed[0],
        summed[1],
        summed[2],
        summed[3],
        gain_grads[1],
        summed[4],
        summed[5],
        summed[6],
    )


def solution(mesh):
    in_specs = (
        P(("dp", "mp"), None),
        P("dp"),
        P(),
        P(None, "mp"),
        P(None, "mp"),
        P(None, "mp"),
        P("mp", None),
        P(),
        P(None, "mp"),
        P(None, "mp"),
        P("mp", None),
        P(("dp", "mp"), None),
    )
    out_specs = (
        P(("dp", "mp"), None),
        P(("dp", "mp"), None),
        P(),
        P("dp", "mp"),
        P("dp", "mp"),
        P("dp", "mp"),
        P("mp", "dp"),
        P(),
        P("dp", "mp"),
        P("dp", "mp"),
        P("mp", "dp"),
    )
    return jax.shard_map(local, mesh=mesh, in_specs=in_specs, out_specs=out_specs, check_vma=False)
```

profile of v0, /device:TPU:0, one launch (start us, length us, event | category | flops | bytes accessed | tf_op | source)
XLA Modules:
  0.0 1483.8 jit_solution(9570107461674244627)
XLA Ops:
  15.7 13.5 all-gather.5.cloned.1.call-done
  63.9 42.3 %while.30 = (s32[]{:T(128)}, bf16[4,576,6,64]{1,3,2,0:T(8,128)(2,1)S(1)}, f32[4,6,576]{2,1,0:T(8,128)}, bf16[4,576,6,64]{1,3,2,0:T(8,128)(2,1)}, s32[4]{0:T(128)...) while((s32[]{:T(128)}, ...), condition=%wide.region_5.6_spmd.clone.clone, body=%wide.region_2.5_spmd.clone.clone.sunk | while | flops 534377664 | bytes 28236528 | solution.py:134
  112.5 6.4 fusion.83
  119.0 16.7 %reduce-scatter.12.cloned.1.call-done = f32[1152,768]{1,0:T(8,128)} async-done(((f32[2304,768]{1,0:T(8,128)}), f32[1152,768]{1,0:T(8,128)}) %reduce-scatter.12.cloned.1.call-update) | async-done | bytes 3538960 | tf_op jit(solution)/shard_map/reduce_scatter | solution.py:136
  143.7 11.9 all-gather.7.cloned.1.call-done
  155.6 10.5 fusion.85
  172.4 14.8 multiply_convert_fusion.1
  187.2 7.5 fusion.86
  201.1 7.7 convolution_convert_fusion
  208.8 8.7 reduce-scatter.16.cloned.1.call-done
  221.6 10.8 reduce-scatter.14.cloned.1.call-done
  238.3 13.9 all-gather.11.cloned.1.call-done
  264.7 246.6 %while.31 = (s32[]{:T(128)}, f32[4,576,6,64]{1,0,3,2:T(4,128)}, f32[4,576,6,64]{1,0,3,2:T(4,128)}, bf16[4,576,6,64]{1,3,2,0:T(8,128)(2,1)}, bf16[4,576,6,64]{1,3...) while((s32[]{:T(128)}, f32[4,576,6,64]{1,0,3,2:T(4,128)}, ...), condition=%wide.region_13.14_spmd.clone.clone, body=%wide.region_11.13_spmd.clone.clone.sunk | while | flops 1304982784 | bytes 89503072 | solution.py:214
  287.4 19.6 %dynamic_update_slice.40 = f32[4,576,6,64]{1,0,3,2:T(4,128)} dynamic-update-slice(f32[4,576,6,64]{1,0,3,2:T(4,128)} %get-tuple-element.481, f32[1,576,6,64]{1,0,3,2:T(1,128)S(1)} %copy.81, s32[]{:T(128)S(6)} %copy.100, s32[]{:T(128)} %constant.88.clone.1..sunk, s32[]{:T(128)} %constant.88.clone.1..sunk, s32[]{:T(128)} %constant.88.clone.1..sunk) | dynamic-update-slice | bytes 1769476 | tf_op jit(solution)/shard_map/while/body/jit(dynamic_update_index_in_dim)/dynamic_update_slice | solution.py:214
  307.1 19.6 %dynamic_update_slice.39 = f32[4,576,6,64]{1,0,3,2:T(4,128)} dynamic-update-slice(f32[4,576,6,64]{1,0,3,2:T(4,128)} %get-tuple-element.480, f32[1,576,6,64]{1,0,3,2:T(1,128)S(1)} %copy.80, s32[]{:T(128)S(6)} %copy.100, s32[]{:T(128)} %constant.88.clone.1..sunk, s32[]{:T(128)} %constant.88.clone.1..sunk, s32[]{:T(128)} %constant.88.clone.1..sunk) | dynamic-update-slice | bytes 1769476 | tf_op jit(solution)/shard_map/while/body/jit(dynamic_update_index_in_dim)/dynamic_update_slice | solution.py:214
  348.9 19.6 %dynamic_update_slice.40 = f32[4,576,6,64]{1,0,3,2:T(4,128)} dynamic-update-slice(f32[4,576,6,64]{1,0,3,2:T(4,128)} %get-tuple-element.481, f32[1,576,6,64]{1,0,3,2:T(1,128)S(1)} %copy.81, s32[]{:T(128)S(6)} %copy.100, s32[]{:T(128)} %constant.88.clone.1..sunk, s32[]{:T(128)} %constant.88.clone.1..sunk, s32[]{:T(128)} %constant.88.clone.1..sunk) | dynamic-update-slice | bytes 1769476 | tf_op jit(solution)/shard_map/while/body/jit(dynamic_update_index_in_dim)/dynamic_update_slice | solution.py:214
  368.6 19.6 %dynamic_update_slice.39 = f32[4,576,6,64]{1,0,3,2:T(4,128)} dynamic-update-slice(f32[4,576,6,64]{1,0,3,2:T(4,128)} %get-tuple-element.480, f32[1,576,6,64]{1,0,3,2:T(1,128)S(1)} %copy.80, s32[]{:T(128)S(6)} %copy.100, s32[]{:T(128)} %constant.88.clone.1..sunk, s32[]{:T(128)} %constant.88.clone.1..sunk, s32[]{:T(128)} %constant.88.clone.1..sunk) | dynamic-update-slice | bytes 1769476 | tf_op jit(solution)/shard_map/while/body/jit(dynamic_update_index_in_dim)/dynamic_update_slice | solution.py:214
  410.4 19.6 %dynamic_update_slice.40 = f32[4,576,6,64]{1,0,3,2:T(4,128)} dynamic-update-slice(f32[4,576,6,64]{1,0,3,2:T(4,128)} %get-tuple-element.481, f32[1,576,6,64]{1,0,3,2:T(1,128)S(1)} %copy.81, s32[]{:T(128)S(6)} %copy.100, s32[]{:T(128)} %constant.88.clone.1..sunk, s32[]{:T(128)} %constant.88.clone.1..sunk, s32[]{:T(128)} %constant.88.clone.1..sunk) | dynamic-update-slice | bytes 1769476 | tf_op jit(solution)/shard_map/while/body/jit(dynamic_update_index_in_dim)/dynamic_update_slice | solution.py:214
  430.1 19.6 %dynamic_update_slice.39 = f32[4,576,6,64]{1,0,3,2:T(4,128)} dynamic-update-slice(f32[4,576,6,64]{1,0,3,2:T(4,128)} %get-tuple-element.480, f32[1,576,6,64]{1,0,3,2:T(1,128)S(1)} %copy.80, s32[]{:T(128)S(6)} %copy.100, s32[]{:T(128)} %constant.88.clone.1..sunk, s32[]{:T(128)} %constant.88.clone.1..sunk, s32[]{:T(128)} %constant.88.clone.1..sunk) | dynamic-update-slice | bytes 1769476 | tf_op jit(solution)/shard_map/while/body/jit(dynamic_update_index_in_dim)/dynamic_update_slice | solution.py:214
  471.9 19.6 %dynamic_update_slice.40 = f32[4,576,6,64]{1,0,3,2:T(4,128)} dynamic-update-slice(f32[4,576,6,64]{1,0,3,2:T(4,128)} %get-tuple-element.481, f32[1,576,6,64]{1,0,3,2:T(1,128)S(1)} %copy.81, s32[]{:T(128)S(6)} %copy.100, s32[]{:T(128)} %constant.88.clone.1..sunk, s32[]{:T(128)} %constant.88.clone.1..sunk, s32[]{:T(128)} %constant.88.clone.1..sunk) | dynamic-update-slice | bytes 1769476 | tf_op jit(solution)/shard_map/while/body/jit(dynamic_update_index_in_dim)/dynamic_update_slice | solution.py:214
  491.6 19.6 %dynamic_update_slice.39 = f32[4,576,6,64]{1,0,3,2:T(4,128)} dynamic-update-slice(f32[4,576,6,64]{1,0,3,2:T(4,128)} %get-tuple-element.480, f32[1,576,6,64]{1,0,3,2:T(1,128)S(1)} %copy.80, s32[]{:T(128)S(6)} %copy.100, s32[]{:T(128)} %constant.88.clone.1..sunk, s32[]{:T(128)} %constant.88.clone.1..sunk, s32[]{:T(128)} %constant.88.clone.1..sunk) | dynamic-update-slice | bytes 1769476 | tf_op jit(solution)/shard_map/while/body/jit(dynamic_update_index_in_dim)/dynamic_update_slice | solution.py:214
  540.3 9.0 fusion.95
  549.4 10.8 fusion.93
  560.3 9.1 fusion.94
  595.1 40.7 %all-reduce = (f32[768]{0:T(1024)}, f32[768]{0:T(1024)}) all-reduce(f32[768]{0:T(1024)S(1)} %get-tuple-element.261, f32[768]{0:T(1024)S(1)} %copy-done.27), channel_id=1, replica_groups=mesh['dp'=16,'mp'=2] {'dp','mp'}, use_global_device_ids=true, to_apply=%region_17.18 | all-reduce | flops 1536 | bytes 12288 | tf_op jit(solution)/shard_map/psum | solution.py:241
  640.7 53.7 %reduce-scatter.32.cloned.1.call-done = f32[1024,48]{0,1:T(8,128)} async-done(((f32[1024,768]{0,1:T(8,128)}), f32[1024,48]{0,1:T(8,128)}) %reduce-scatter.32.cloned.1.call-update) | async-done | bytes 196624 | tf_op jit(solution)/shard_map/reduce_scatter | solution.py:176
  694.4 135.5 %reduce-scatter.28.cloned.1.call-done = f32[48,1024]{1,0:T(8,128)} async-done(((f32[768,1024]{1,0:T(8,128)}), f32[48,1024]{1,0:T(8,128)}) %reduce-scatter.28.cloned.1.call-update) | async-done | bytes 196624 | tf_op jit(solution)/shard_map/reduce_scatter | solution.py:174
  829.8 135.5 %reduce-scatter.30.cloned.1.call-done = f32[48,1024]{1,0:T(8,128)} async-done(((f32[768,1024]{1,0:T(8,128)}), f32[48,1024]{1,0:T(8,128)}) %reduce-scatter.30.cloned.1.call-update) | async-done | bytes 196624 | tf_op jit(solution)/shard_map/reduce_scatter | solution.py:175
  965.4 128.0 %reduce-scatter.26.cloned.1.call-done = f32[384,48]{0,1:T(8,128)} async-done(((f32[384,768]{0,1:T(8,128)}), f32[384,48]{0,1:T(8,128)}) %reduce-scatter.26.cloned.1.call-update) | async-done | bytes 73744 | tf_op jit(solution)/shard_map/reduce_scatter | solution.py:246
  1093.4 128.0 %reduce-scatter.24.cloned.1.call-done = f32[48,384]{1,0:T(8,128)} async-done(((f32[768,384]{1,0:T(8,128)}), f32[48,384]{1,0:T(8,128)}) %reduce-scatter.24.cloned.1.call-update) | async-done | bytes 73744 | tf_op jit(solution)/shard_map/reduce_scatter | solution.py:245
  1221.4 127.7 %reduce-scatter.20.cloned.1.call-done = f32[48,384]{1,0:T(8,128)} async-done(((f32[768,384]{1,0:T(8,128)}), f32[48,384]{1,0:T(8,128)}) %reduce-scatter.20.cloned.1.call-update) | async-done | bytes 73744 | tf_op jit(solution)/shard_map/reduce_scatter | solution.py:243
  1349.1 127.7 %reduce-scatter.22.cloned.1.call-done = f32[48,384]{1,0:T(8,128)} async-done(((f32[768,384]{1,0:T(8,128)}), f32[48,384]{1,0:T(8,128)}) %reduce-scatter.22.cloned.1.call-update) | async-done | bytes 73744 | tf_op jit(solution)/shard_map/reduce_scatter | solution.py:244
  (250 shorter events, 282.9 us)
Async XLA Ops:
  7.2 165.2 %copy-start = (bf16[1024,768]{1,0:T(8,128)(2,1)S(1)}, bf16[1024,768]{1,0:T(8,128)(2,1)}, u32[]{:S(2)}) copy-start(bf16[1024,768]{1,0:T(8,128)(2,1)} %param.26) | copy-start | bytes 4718596
  7.2 22.0 %all-gather.5.cloned.1.call-start = ((), (), s32[]{:S(2)}) async-start(), calls=%async_computation.11 | async-start | bytes 5308416 | tf_op jit(solution)/shard_map/all_gather | solution.py:87
  13.6 122.1 %reduce-scatter.12.cloned.1.call-start = ((), (), s32[]{:S(2)}) async-start(), calls=%async_computation.12 | async-start | bytes 10616832 | tf_op jit(solution)/shard_map/reduce_scatter | solution.py:136
  112.5 6.4 copy-start.6
  118.9 16.8 %copy-start.4 = (bf16[1152,768]{1,0:T(8,128)(2,1)S(1)}, bf16[1152,768]{1,0:T(8,128)(2,1)}, u32[]{:S(2)}) copy-start(bf16[1152,768]{1,0:T(8,128)(2,1)} %param.16) | copy-start | bytes 5308420
  118.9 21.1 %copy-start.24 = (f32[768]{0:T(1024)S(1)}, f32[768]{0:T(1024)}, u32[]{:S(2)}) copy-start(f32[768]{0:T(1024)} %param.23) | copy-start | bytes 9220
  118.9 36.7 %all-gather.7.cloned.1.call-start = ((), (), s32[]{:S(2)}) async-start(), calls=%async_computation.13 | async-start | bytes 5308416 | tf_op jit(solution)/shard_map/all_gather | solution.py:145
  141.6 30.8 %all-gather.9.cloned.1.call-start = ((), (), s32[]{:S(2)}) async-start(), calls=%async_computation.15 | async-start | bytes 5308416 | tf_op jit(solution)/shard_map/all_gather | solution.py:164
  143.5 22.7 %copy-start.32 = (bf16[768,1024]{1,0:T(8,128)(2,1)S(1)}, bf16[768,1024]{1,0:T(8,128)(2,1)}, u32[]{:S(2)}) copy-start(bf16[768,1024]{1,0:T(8,128)(2,1)} %param.24) | copy-start | bytes 4718596
  143.5 74.0 %reduce-scatter.16.cloned.1.call-start = ((), (), s32[]{:S(2)}) async-start(), calls=%async_computation.16 | async-start | bytes 10616832 | tf_op jit(solution)/shard_map/reduce_scatter | solution.py:178
  155.6 10.5 copy-start.31
  187.2 7.5 copy-start.34
  187.2 7.5 copy-start.33
  200.8 31.5 %reduce-scatter.14.cloned.1.call-start = ((), (), s32[]{:S(2)}) async-start(), calls=%async_computation.14 | async-start | bytes 5308416 | tf_op jit(solution)/shard_map/reduce_scatter | solution.py:151
  208.8 8.8 copy-start.3
  208.8 43.5 %all-gather.11.cloned.1.call-start = ((), (), s32[]{:S(2)}) async-start(), calls=%async_computation.17 | async-start | bytes 5308416 | tf_op jit(solution)/shard_map/all_gather | solution.py:186
  238.3 353.4 %reduce-scatter.18.cloned.1.call-start = ((), (), s32[]{:S(2)}) async-start(), calls=%async_computation.18 | async-start | bytes 10616832 | tf_op jit(solution)/shard_map/reduce_scatter | solution.py:231
  258.8 6.0 copy-start.29
  273.5 5.0 copy-start.16
  540.0 154.3 %reduce-scatter.32.cloned.1.call-start = ((), (), s32[]{:S(2)}) async-start(), calls=%async_computation.25 | async-start | bytes 3342336 | tf_op jit(solution)/shard_map/reduce_scatter | solution.py:176
  549.3 280.5 %reduce-scatter.28.cloned.1.call-start = ((), (), s32[]{:S(2)}) async-start(), calls=%async_computation.23 | async-start | bytes 3342336 | tf_op jit(solution)/shard_map/reduce_scatter | solution.py:174
  560.2 9.5 copy-start.7
  560.2 405.2 %reduce-scatter.30.cloned.1.call-start = ((), (), s32[]{:S(2)}) async-start(), calls=%async_computation.24 | async-start | bytes 3342336 | tf_op jit(solution)/shard_map/reduce_scatter | solution.py:175
  569.3 524.0 %reduce-scatter.26.cloned.1.call-start = ((), (), s32[]{:S(2)}) async-start(), calls=%async_computation.22 | async-start | bytes 1253376 | tf_op jit(solution)/shard_map/reduce_scatter | solution.py:246
  574.8 646.5 %reduce-scatter.24.cloned.1.call-start = ((), (), s32[]{:S(2)}) async-start(), calls=%async_computation.21 | async-start | bytes 1253376 | tf_op jit(solution)/shard_map/reduce_scatter | solution.py:245
  580.5 768.6 %reduce-scatter.20.cloned.1.call-start = ((), (), s32[]{:S(2)}) async-start(), calls=%async_computation.19 | async-start | bytes 1253376 | tf_op jit(solution)/shard_map/reduce_scatter | solution.py:243
  585.7 5.9 copy-start.5
  585.7 5.9 copy-start.23
  585.7 5.9 copy-start.25
  585.7 891.1 %reduce-scatter.22.cloned.1.call-start = ((), (), s32[]{:S(2)}) async-start(), calls=%async_computation.20 | async-start | bytes 1253376 | tf_op jit(solution)/shard_map/reduce_scatter | solution.py:244
  591.6 44.2 %copy-start.26 = (f32[1152]{0:T(1024)S(1)}, f32[1152]{0:T(1024)}, u32[]{:S(2)}) copy-start(f32[1152]{0:T(1024)} %get-tuple-element.325) | copy-start | bytes 13828
  635.7 841.1 %copy-start.1 = (bf16[1024,768]{1,0:T(8,128)(2,1)S(1)}, bf16[1024,768]{1,0:T(8,128)(2,1)}, u32[]{:S(2)}) copy-start(bf16[1024,768]{1,0:T(8,128)(2,1)} %param.26) | copy-start | bytes 4718596
  (24 other events, 63.0 us)
Sparse Core Ops, SparseCore 0:
  13.7 15.3 all-gather.4
  119.0 16.6 reduce-scatter.11
  141.8 13.8 all-gather.6
  157.1 13.8 all-gather.8
  200.9 16.5 reduce-scatter.15
  219.6 12.6 reduce-scatter.13
  238.4 13.8 all-gather.10
  540.2 16.6 reduce-scatter.17
  562.4 131.9 reduce-scatter.31
  699.8 130.0 reduce-scatter.27
  835.4 129.9 reduce-scatter.29
  970.5 122.7 reduce-scatter.25
  1098.7 122.5 reduce-scatter.23
  1226.5 122.5 reduce-scatter.19
  1354.3 122.5 reduce-scatter.21
where the time goes:
time: 1500 us; the launch traced here: 1480 us
  waiting for transfers between devices  912 us (61%)
  local copies, waits for them, and re-layouts  225 us (15%)
  matrix products  221 us (15%)
  other arithmetic  67.5 us (4%)
  blocking collectives  40.7 us (3%)
    dynamic_update_slice x16, local copies, waits for them, and re-layouts, local(): lax.map(attend_back, (q_items, k_items, v_items, lengths, log_norm, d_mix...  165 us
    reduce_scatter x1, waiting for transfers between devices, local(): lax.psum_scatter(grad_up, 'dp', scatter_dimension=0, tiled=True)  136 us
    reduce_scatter x1, waiting for transfers between devices, local(): lax.psum_scatter(grad_gate, 'dp', scatter_dimension=0, tiled=True)  135 us
    reduce_scatter x1, waiting for transfers between devices, local(): lax.psum_scatter(grad_out, 'dp', scatter_dimension=1, tiled=True)  128 us
    reduce_scatter x1, waiting for transfers between devices, local(): lax.psum_scatter(grad_value, 'dp', scatter_dimension=0, tiled=True)  128 us
    reduce_scatter x1, waiting for transfers between devices, local(): lax.psum_scatter(grad_query, 'dp', scatter_dimension=0, tiled=True)  128 us
    reduce_scatter x1, waiting for transfers between devices, local(): lax.psum_scatter(grad_key, 'dp', scatter_dimension=0, tiled=True)  128 us
    reduce_scatter x1, waiting for transfers between devices, local(): lax.psum_scatter(grad_down, 'dp', scatter_dimension=1, tiled=True)  53.7 us
  transfers between devices with their start and end apart: 15, of which 13 were waited for; matrix products, arithmetic and copies ran while one was open for 6% of the time, Pallas kernels for 0%

commit v1 on v0

v1 whole, which is shorter than its diff:
```python
import functools

import jax
import jax.numpy as jnp
import numpy as np
from jax import lax
from jax.experimental import pallas as pl
from jax.experimental.pallas import tpu as pltpu
from jax.sharding import PartitionSpec as P

HEAD = 64
PAIR = 2 * HEAD
SLOTS = 576
EPS = 1e-05
THETA = 10000.0
ROWS = 384
CHUNK = 512
F32 = jnp.float32
BF16 = jnp.bfloat16
NEG = -1e30
BLOCKS = ((512, 64), (256, 256), (0, 256))
MIB = 1 << 20


def hbm(shape, dtype):
    return pltpu.HBM(shape, dtype)


def vmem(shape, dtype):
    return pltpu.VMEM(shape, dtype)


def on_chip(tree):
    return jax.tree.map(lambda a: pltpu.with_memory_space_constraint(a, pltpu.VMEM), tree)


def off_chip(tree):
    return jax.tree.map(lambda a: pltpu.with_memory_space_constraint(a, pltpu.HBM), tree)


def copy(source, target, sem):
    made = pltpu.make_async_copy(source, target, sem)
    made.start()
    return made


ANY = pl.BlockSpec(memory_space=pl.ANY)
CHIP = pl.BlockSpec(memory_space=pltpu.VMEM)
SCALAR = pl.BlockSpec(memory_space=pltpu.SMEM)


def dot(left, right):
    return jnp.dot(left, right, preferred_element_type=F32)


def dot_nt(left, right):
    return lax.dot_general(left, right, (((1,), (1,)), ((), ())), preferred_element_type=F32)


def params(mib):
    return pltpu.CompilerParams(vmem_limit_bytes=mib * MIB)


def cost(flops, moved, special=0):
    return pl.CostEstimate(flops=int(flops), bytes_accessed=int(moved), transcendentals=int(special))


def sds(shape, dtype):
    return jax.ShapeDtypeStruct(shape, dtype)


def position_tables(row_count):
    inv_freq = np.float32(THETA) ** (
        -(np.float32(2.0) * np.arange(HEAD // 2, dtype=np.float32)) / np.float32(HEAD)
    )
    places = (np.arange(row_count) % SLOTS).astype(np.float32)
    angles = (places[:, None] * inv_freq[None, :].astype(np.float32)).astype(np.float32)
    cosine, sine = np.cos(angles), np.sin(angles)
    cos_t = np.tile(cosine, (1, PAIR // cosine.shape[1]))
    sin_t = np.tile(np.concatenate([-sine, sine], 1), (1, 2))
    return cos_t.astype(np.float32), sin_t.astype(np.float32)


def swap_halves(values):
    lane = lax.broadcasted_iota(jnp.int32, values.shape, 1)
    return jnp.where(
        lane % HEAD < HEAD // 2,
        pltpu.roll(values, PAIR - HEAD // 2, 1),
        pltpu.roll(values, HEAD // 2, 1),
    )


def relative_order(dp):
    return [b0 + 2 * b1 + 4 * z for b0 in range(2) for b1 in range(2) for z in range(dp // 4)]


def store_transposed(value, scratch, out_ref, me_ref, dp):
    width = value.shape[1]
    group = width // dp
    if group % 16:
        out_ref[...] = value.T
        return
    scratch[...] = value.T
    for place, relative in enumerate(relative_order(dp)):
        start = pl.multiple_of(group * jnp.bitwise_xor(me_ref[0], relative), 16)
        out_ref[group * place : group * place + group, :] = scratch[pl.ds(start, group), :]


def finish_transposed(array, me, dp):
    group = array.shape[0] // dp
    if group % 16 == 0:
        return array
    index = jnp.bitwise_xor(me[0], jnp.asarray(relative_order(dp), jnp.int32))
    return jnp.take(array.reshape(dp, group, -1), index, axis=0).reshape(array.shape)


class Copies:
    def __init__(self, sems):
        self.sems, self.made = sems, []

    def start(self, source, target):
        self.made.append(copy(source, target, self.sems.at[len(self.made)]))
        return self.made[-1]

    def wait(self):
        for c in self.made:
            c.wait()


def row_blocks(count):
    return [slice(start, start + ROWS) for start in range(0, count, ROWS)]


def prepare_kernel(
    items, dp, me_ref, lens_ref, gain_ref, x_hbm, cot_hbm, na_ref, nat_ref, eb_ref, ebt_ref, x, cot, turn, sems
):
    arrive = Copies(sems)
    blocks = row_blocks(x.shape[0])
    inputs = [
        (arrive.start(x_hbm.at[own, :], x.at[own, :]), arrive.start(cot_hbm.at[own, :], cot.at[own, :]))
        for own in blocks
    ]
    for own, (x_in, cot_in) in zip(blocks, inputs):
        x_in.wait()
        rows = x[own, :].astype(F32)
        inv = lax.rsqrt(jnp.mean(rows * rows, -1, keepdims=True) + EPS)
        normed = (rows * inv * gain_ref[...][None, :]).astype(BF16)
        na_ref[own, :] = normed
        store_transposed(normed, turn.at[0], nat_ref.at[:, own], me_ref, dp)
        cot_in.wait()
        valid = row_is_valid(me_ref, lens_ref, items, own.start)
        e = jnp.where(valid, cot[own, :].astype(F32), 0.0).astype(BF16)
        eb_ref[own, :] = e
        store_transposed(e, turn.at[1], ebt_ref.at[:, own], me_ref, dp)


def prepare(dp, me, lens, x, cot, gain):
    count, width = x.shape
    return pl.pallas_call(
        functools.partial(prepare_kernel, count // SLOTS, dp),
        in_specs=[SCALAR, SCALAR, CHIP, ANY, ANY],
        out_specs=[CHIP] * 4,
        out_shape=[vmem((count, width), BF16), vmem((width, count), BF16)] * 2,
        scratch_shapes=[
            pltpu.VMEM((count, width), BF16),
            pltpu.VMEM((count, width), BF16),
            pltpu.VMEM((2, width, ROWS), BF16),
            pltpu.SemaphoreType.DMA((2 * (count // ROWS),)),
        ],
        compiler_params=params(24),
        cost_estimate=cost(10 * count * width, 12 * count * width),
        name="prepare",
    )(me, lens, on_chip(gain), *off_chip((x, cot)))


def attention_tasks(items):
    return [(i, h, q0, qb) for i in range(items) for q0, qb in BLOCKS for h in range(2)]


def pipelined(tasks, first, second, third):
    made, ready = {}, {}
    for step in range(len(tasks) + 2):
        if step < len(tasks):
            made[step] = first(tasks[step])
        if 0 <= step - 1 < len(tasks):
            ready[step - 1] = second(tasks[step - 1], made.pop(step - 1))
        if 0 <= step - 2 < len(tasks):
            third(tasks[step - 2], ready.pop(step - 2))


def causal(shape):
    key = lax.broadcasted_iota(jnp.int32, shape, 0)
    query = lax.broadcasted_iota(jnp.int32, shape, 1)
    return key <= query


def attend(items, q_ref, k_ref, v_ref, own_cols, o_ref, lse_ref, pair, acc):
    side = lax.broadcasted_iota(jnp.int32, (SLOTS, PAIR), 1) // HEAD
    v_t = {}

    def scores(task):
        i, h, q0, qb = task
        base = i * SLOTS
        q = jnp.where(side[:qb] == h, q_ref[base + q0 : base + q0 + qb, own_cols], 0).astype(BF16)
        diag = dot_nt(k_ref[base + q0 : base + q0 + qb, own_cols], q)
        return diag, (dot_nt(k_ref[base : base + q0, own_cols], q) if q0 else None)

    def soften(task, made):
        i, h, q0, qb = task
        diag, past = made
        diag = jnp.where(causal(diag.shape), diag, NEG)
        top = jnp.max(diag, 0, keepdims=True)
        if q0:
            top = jnp.maximum(top, jnp.max(past, 0, keepdims=True))
        diag = jnp.exp(diag - top)
        total = jnp.sum(diag, 0, keepdims=True)
        if q0:
            past = jnp.exp(past - top)
            total = total + jnp.sum(past, 0, keepdims=True)
            past = past.astype(BF16)
        lse_ref[pair, 2 * i + h : 2 * i + h + 1, q0 : q0 + qb] = top + jnp.log(total)
        return diag.astype(BF16), past, total

    def mix(task, made):
        i, h, q0, qb = task
        diag, past, total = made
        if i not in v_t:
            v_t[i] = v_ref[i * SLOTS : (i + 1) * SLOTS, own_cols].T
        own = v_t[i][HEAD * h : HEAD * h + HEAD]
        out = dot(own[:, q0 : q0 + qb], diag)
        if q0:
            out = out + dot(own[:, :q0], past)
        acc[i, HEAD * h : HEAD * h + HEAD, q0 : q0 + qb] = out * (1.0 / total)

    pipelined(attention_tasks(items), scores, soften, mix)
    for i in range(items):
        o_ref[i * SLOTS : (i + 1) * SLOTS, own_cols] = acc[i].T.astype(BF16)


def front_kernel(
    dp, me_ref, gain_ref, na_ref, cos_hbm, sin_hbm, w_hbm, wo_hbm, x_hbm,
    q_hbm, k_hbm, v_hbm, h1_hbm, o_ref, lse_ref, nf_ref, nft_ref,
    q_ref, k_ref, v_ref, h1_ref, acc, weights, wo, x, cosine, sine, turn, sems, out_sems,
):
    arrive = Copies(sems)
    leaving = ((q_ref, q_hbm), (k_ref, k_hbm), (v_ref, v_hbm))
    count, width = na_ref.shape
    items, cols = count // SLOTS, wo_hbm[0].shape[0]
    half = cols // PAIR
    early = [arrive.start(cos_hbm, cosine), arrive.start(sin_hbm, sine)]
    for p in range(2 * half):
        for j in range(3):
            source = w_hbm[p // half][j].at[:, (p % half) * PAIR : (p % half + 1) * PAIR]
            early.append(arrive.start(source, weights.at[:, (3 * p + j) * PAIR : (3 * p + j + 1) * PAIR]))
    late = [arrive.start(w, wo.at[i * cols : (i + 1) * cols, :]) for i, w in enumerate(wo_hbm)]
    late.append(arrive.start(x_hbm, x))
    for c in early:
        c.wait()

    @pl.loop(0, 2 * half)
    def _(pair):
        own_cols = pl.ds(pl.multiple_of(pair * PAIR, PAIR), PAIR)
        own_weights = weights[:, pl.ds(pl.multiple_of(pair * 3 * PAIR, PAIR), 3 * PAIR)]
        for own in row_blocks(count):
            qkv = dot(na_ref[own, :], own_weights)
            cos_v, sin_v = cosine[own, :], sine[own, :]
            q, k = qkv[:, :PAIR], qkv[:, PAIR : 2 * PAIR]
            q_ref[own, own_cols] = ((q * cos_v + swap_halves(q) * sin_v) * HEAD**-0.5).astype(BF16)
            k_ref[own, own_cols] = (k * cos_v + swap_halves(k) * sin_v).astype(BF16)
            v_ref[own, own_cols] = qkv[:, 2 * PAIR :].astype(BF16)
        for j, (source, target) in enumerate(leaving):
            copy(source.at[:, own_cols], target.at[:, own_cols], out_sems.at[3 * pair + j])
        attend(items, q_ref, k_ref, v_ref, own_cols, o_ref, lse_ref, pair, acc)

    for c in late:
        c.wait()
    blocks = row_blocks(count)
    branch = dot(o_ref[blocks[0], :], wo[...])
    for i, own in enumerate(blocks):
        upcoming = dot(o_ref[blocks[i + 1], :], wo[...]) if i + 1 < len(blocks) else None
        rows = x[own, :].astype(F32) + branch
        h1_ref[own, :] = rows
        inv = lax.rsqrt(jnp.mean(rows * rows, -1, keepdims=True) + EPS)
        normed = (rows * inv * gain_ref[...][None, :]).astype(BF16)
        nf_ref[own, :] = normed
        store_transposed(normed, turn, nft_ref.at[:, own], me_ref, dp)
        branch = upcoming
        copy(h1_ref.at[own, :], h1_hbm.at[own, :], out_sems.at[6 * half + i])
    for p in range(2 * half):
        own_cols = slice(p * PAIR, (p + 1) * PAIR)
        for j, (source, target) in enumerate(leaving):
            pltpu.make_async_copy(source.at[:, own_cols], target.at[:, own_cols], out_sems.at[3 * p + j]).wait()
    for i, own in enumerate(blocks):
        pltpu.make_async_copy(h1_ref.at[own, :], h1_hbm.at[own, :], out_sems.at[6 * half + i]).wait()


def front(dp, me, na, tables, gain, w, wo, x):
    count, width = na.shape
    items, cols = count // SLOTS, wo[0].shape[0]
    half = cols // PAIR
    area = 2 * half * items * 2 * SLOTS * SLOTS
    return pl.pallas_call(
        functools.partial(front_kernel, dp),
        in_specs=[SCALAR, CHIP, CHIP, ANY, ANY, [[ANY] * 3] * 2, [ANY] * 2, ANY],
        out_specs=[ANY] * 4 + [CHIP] * 4,
        out_shape=[hbm((count, width), BF16)] * 3
        + [
            hbm((count, width), F32), vmem((count, width), BF16),
            vmem((2 * half, 2 * items, SLOTS), F32),
            vmem((count, width), BF16), vmem((width, count), BF16),
        ],
        scratch_shapes=[pltpu.VMEM((count, width), BF16)] * 3
        + [
            pltpu.VMEM((count, width), F32),
            pltpu.VMEM((items, PAIR, SLOTS), F32),
            pltpu.VMEM((width, 6 * cols), BF16),
            pltpu.VMEM((2 * cols, width), BF16),
            pltpu.VMEM((count, width), BF16),
            pltpu.VMEM((count, PAIR), F32),
            pltpu.VMEM((count, PAIR), F32),
            pltpu.VMEM((width, ROWS), BF16),
            pltpu.SemaphoreType.DMA((6 * half + 8,)),
            pltpu.SemaphoreType.DMA((6 * half + count // ROWS,)),
        ],
        compiler_params=params(34),
        cost_estimate=cost(8 * count * width * width + 8 * area * PAIR, 24 * count * width, area),
        name="front",
    )(me, *on_chip((gain, na)), *off_chip(tables), [list(off_chip(w[0])), list(w[1])], [off_chip(wo[0]), wo[1]], off_chip(x))


def attention_back_kernel(
    final, first, d_ref, lse_ref, nat_ref, cos_hbm, sin_hbm, q_hbm, k_hbm, v_hbm, *rest
):
    q_ref, k_ref, v_ref, dq_t, dk_acc, dv_acc, cosine, sine, right, sems, row_sems = rest[-11:]
    if final:
        recv_ref, dq_ref, dk_ref, dv_ref, *outs = rest[:-11]
    else:
        dq_ref, dk_ref, dv_ref, out_ref = rest[:-11]
    count, cols = dq_ref.shape
    items = count // SLOTS
    arrive = Copies(sems)
    arrive.start(cos_hbm.at[:SLOTS, :], cosine)
    arrive.start(sin_hbm.at[:SLOTS, :], sine)
    arriving = ((q_hbm, q_ref), (k_hbm, k_ref), (v_hbm, v_ref))
    for p in range(cols // PAIR):
        source_cols = slice((p + first) * PAIR, (p + first + 1) * PAIR)
        for j, (source, target) in enumerate(arriving):
            copy(source.at[:, source_cols], target.at[:, p * PAIR : (p + 1) * PAIR], row_sems.at[3 * p + j])
    arrive.wait()
    side = lax.broadcasted_iota(jnp.int32, (SLOTS, PAIR), 1) // HEAD
    quarter = nat_ref.shape[0] // 4

    @pl.loop(0, cols // PAIR)
    def _(pair):
        own_cols = pl.ds(pl.multiple_of(pair * PAIR, PAIR), PAIR)
        from_cols = pl.ds(pl.multiple_of((pair + first) * PAIR, PAIR), PAIR)
        for j, (source, target) in enumerate(arriving):
            pltpu.make_async_copy(source.at[:, from_cols], target.at[:, own_cols], row_sems.at[3 * pair + j]).wait()
        k_t = {}

        def scores(task):
            i, h, q0, qb = task
            base, end = i * SLOTS, i * SLOTS + q0 + qb
            q = jnp.where(side[:qb] == h, q_ref[base + q0 : end, own_cols], 0).astype(BF16)
            d = jnp.where(side[:qb] == h, d_ref[base + q0 : end, from_cols], 0).astype(BF16)
            return q, d, dot_nt(k_ref[base:end, own_cols], q), dot_nt(v_ref[base:end, own_cols], d)

        def soften(task, made):
            i, h, q0, qb = task
            q, d, s, dp = made
            lse = lse_ref[pair + first, 2 * i + h : 2 * i + h + 1, q0 : q0 + qb]
            p = jnp.exp(s[q0:] - lse)
            p = jnp.where(causal(p.shape), p, 0.0)
            if q0:
                p = jnp.concatenate([jnp.exp(s[:q0] - lse), p], 0)
            ds = (p * (dp - jnp.sum(p * dp, 0, keepdims=True))).astype(BF16)
            return q, d, p.astype(BF16), ds

        def mix(task, made):
            i, h, q0, qb = task
            q, d, p, ds = made
            end = q0 + qb
            if i not in k_t:
                k_t[i] = k_ref[i * SLOTS : (i + 1) * SLOTS, own_cols].T
            dv, dk = dot(p, d), dot(ds, q)
            if end == SLOTS and h == 0:
                dv_acc[i] = dv
                dk_acc[i] = dk
            else:
                dv_acc[i, :end, :] += dv
                dk_acc[i, :end, :] += dk
            dq_t[i, HEAD * h : HEAD * h + HEAD, q0:end] = dot(k_t[i][HEAD * h : HEAD * h + HEAD, :end], ds)

        pipelined(attention_tasks(items), scores, soften, mix)
        cos_v, sin_v = cosine[...], sine[...]
        for i in range(items):
            own = slice(i * SLOTS, (i + 1) * SLOTS)
            dq = dq_t[i].T * HEAD**-0.5
            dq = (dq * cos_v - swap_halves(dq) * sin_v).astype(BF16)
            dk = dk_acc[i]
            dk = (dk * cos_v - swap_halves(dk) * sin_v).astype(BF16)
            dv = dv_acc[i].astype(BF16)
            for j, (ref, value) in enumerate(((dq_ref, dq), (dk_ref, dk), (dv_ref, dv))):
                ref[own, own_cols] = value
                right[own, j * PAIR : (j + 1) * PAIR] = value
        wide = pl.ds(pl.multiple_of(pair * 3 * PAIR, PAIR), 3 * PAIR)
        for place in range(4):
            own = slice(place * quarter, place * quarter + quarter)
            values = dot(nat_ref[own, :], right[...])
            if final:
                outs[place][:, wide] = (values + recv_ref[own, wide].astype(F32)).astype(BF16)
            else:
                out_ref[own, wide] = values.astype(BF16)


def attention_back(q, k, v, d, lse, tables, nat, first, recv=None):
    count, width = q.shape
    cols = width // 2
    items, pairs = count // SLOTS, cols // PAIR
    area = pairs * items * 2 * SLOTS * SLOTS
    final = recv is not None
    args = [*on_chip((d, lse, nat)), *off_chip((*tables, q, k, v))]
    out_shape = [vmem((count, cols), BF16)] * 3
    if final:
        args.append(on_chip(recv))
        out_shape += [vmem((width // 4, 3 * cols), BF16)] * 4
    else:
        out_shape.append(vmem((width, 3 * cols), BF16))
    return pl.pallas_call(
        functools.partial(attention_back_kernel, final, first),
        in_specs=[CHIP] * 3 + [ANY] * 5 + [CHIP] * (len(args) - 8),
        out_specs=[CHIP] * len(out_shape),
        out_shape=out_shape,
        scratch_shapes=[pltpu.VMEM((count, cols), BF16)] * 3
        + [pltpu.VMEM((items, PAIR, SLOTS), F32)]
        + [pltpu.VMEM((items, SLOTS, PAIR), F32)] * 2
        + [pltpu.VMEM((SLOTS, PAIR), F32)] * 2
        + [pltpu.VMEM((count, 3 * PAIR), BF16), pltpu.SemaphoreType.DMA((2,)), pltpu.SemaphoreType.DMA((3 * pairs,))],
        compiler_params=params(28),
        cost_estimate=cost(20 * area * PAIR + 6 * count * width * cols, 16 * count * cols, area),
        name="attention_back_final" if final else "attention_back_other",
    )(*args)


def row_is_valid(me_ref, lens_ref, items, start):
    row = start + lax.broadcasted_iota(jnp.int32, (ROWS, 1), 0)
    valid = row < 0
    for i in range(items):
        valid = valid | ((row >= i * SLOTS) & (row < i * SLOTS + lens_ref[me_ref[1] * items + i]))
    return valid


def split_store(values, cols, total, b0, b1, outs):
    send_a, keep_a, send_b, keep_b = outs
    cut = total // 2
    if cols.start < cut:
        part = values[:, : min(cols.stop, cut) - cols.start].astype(BF16)
        (send_a if b0 else keep_a)[b1, :, cols.start : min(cols.stop, cut)] = part
    if cols.stop > cut:
        start = max(cols.start, cut)
        part = values[:, start - cols.start :].astype(BF16)
        (send_b if b1 else keep_b)[b0, :, start - cut : cols.stop - cut] = part


def ffn_kernel(final, column, blocks, nf_ref, nft_ref, eb_ref, ebt_ref, wg_hbm, wu_hbm, wd_hbm, *rest):
    wg, wu, wd, hid, in_sems, out_sems = rest[-6:]
    if final:
        recv_ref, hid_hbm, dg_ref, du_ref, *outs = rest[:-6]
    else:
        hid_hbm, dg_ref, du_ref, out_ref = rest[:-6]
    width = nft_ref.shape[0]
    chunk = pl.ds(column, CHUNK)
    arrive, sent = Copies(in_sems), Copies(out_sems)
    waits = [
        arrive.start(wg_hbm.at[:, chunk], wg),
        arrive.start(wu_hbm.at[:, chunk], wu),
        arrive.start(wd_hbm.at[chunk, :], wd),
    ]

    def products(own):
        made = []
        for ref, weight, multiply in ((nf_ref, wg, dot), (nf_ref, wu, dot), (eb_ref, wd, dot_nt)):
            if waits:
                waits.pop(0).wait()
            made.append(multiply(ref[own, :], weight[...]))
        return made

    def point(own, made):
        g, u, dh = made
        sig = 0.5 * jnp.tanh(0.5 * g) + 0.5
        silu = g * sig
        hid[own, :] = (silu * u).astype(BF16)
        sent.start(hid.at[own, :], hid_hbm.at[own, :])
        du_ref[own, :] = (dh * silu).astype(BF16)
        dg_ref[own, :] = (dh * u * (sig + silu * (1.0 - sig))).astype(BF16)

    made = None
    for i in range(len(blocks) + 1):
        upcoming = products(blocks[i]) if i < len(blocks) else None
        if made is not None:
            point(blocks[i - 1], made)
        made = upcoming
    quarter = width // 4
    for place in range(4):
        own = slice(place * quarter, place * quarter + quarter)
        grads = [dot(nft_ref[own, :], dg_ref[...]), dot(nft_ref[own, :], du_ref[...]), dot(ebt_ref[own, :], hid[...])]
        for j, values in enumerate(grads):
            cols = slice(j * CHUNK, (j + 1) * CHUNK)
            if final:
                split_store(values + recv_ref[own, cols].astype(F32), cols, 3 * CHUNK, place // 2, place % 2, outs)
            else:
                out_ref[own, cols] = values.astype(BF16)
    sent.wait()


def ffn(nf, nft, eb, ebt, wg, wu, wd, chunk, recv=None, spare=0):
    count, width = nf.shape
    final = recv is not None
    wide = 3 * CHUNK
    sizes = [512 * count // 1152, 384 * count // 1152]
    edges = [0, sizes[0], sum(sizes), count]
    blocks = [slice(i, j) for i, j in zip(edges, edges[1:])]
    weights = off_chip((wg, wu, wd)) if final else (wg, wu, wd)
    args = [*on_chip((nf, nft, eb, ebt)), *weights]
    out_shape = [hbm((count, CHUNK), BF16)] + [vmem((count, CHUNK), BF16)] * 2
    if final:
        args.append(on_chip(recv))
        out_shape += [vmem((2, width // 4, wide // 2 + spare), BF16)] * 4
    else:
        out_shape.append(vmem((width, wide), BF16))
    return pl.pallas_call(
        functools.partial(ffn_kernel, final, chunk * CHUNK, blocks),
        in_specs=[CHIP] * 4 + [ANY] * 3 + [CHIP] * (len(args) - 7),
        out_specs=[ANY] + [CHIP] * (len(out_shape) - 1),
        out_shape=out_shape,
        scratch_shapes=[pltpu.VMEM((width, CHUNK), BF16)] * 2
        + [
            pltpu.VMEM((CHUNK, width), BF16),
            pltpu.VMEM((count, CHUNK), BF16),
            pltpu.SemaphoreType.DMA((3,)),
            pltpu.SemaphoreType.DMA((3,)),
        ],
        compiler_params=params(24),
        cost_estimate=cost(12 * count * width * CHUNK, 8 * count * width + 12 * width * CHUNK),
        name="ffn_final" if final else "ffn_other",
    )(*args)


def norm_back_rows(rows, d_normed, gain):
    inv = lax.rsqrt(jnp.mean(rows * rows, -1, keepdims=True) + EPS)
    unit = rows * inv
    weighted = d_normed * gain
    d_rows = inv * (weighted - unit * jnp.mean(weighted * unit, -1, keepdims=True))
    return d_rows, jnp.sum(d_normed * unit, 0, keepdims=True)


def ffn_back_kernel(
    dp, me_ref, gain_ref, h1_hbm, eb_ref, o_ref, d_refs, wg_hbm, wu_hbm, wo_hbm,
    dh1_ref, do_ref, dgain_ref, there_ref, here_ref, h1_ref, weights, wo, turn, abt, in_sems,
):
    count, width = h1_ref.shape
    cols, half = wo_hbm[0].shape[0], wg_hbm[0].shape[1]
    arrive = Copies(in_sems)
    w_in = [arrive.start(w, weights.at[i]) for i, w in enumerate((*wg_hbm, *wu_hbm))]
    wo_in = [arrive.start(w, wo.at[i * cols : (i + 1) * cols, :]) for i, w in enumerate(wo_hbm)]
    blocks = row_blocks(count)
    h1_in = [arrive.start(h1_hbm.at[own, :], h1_ref.at[own, :]) for own in blocks]
    per = len(d_refs) // len(w_in)

    def product(i):
        total = None
        for j, w in enumerate(w_in):
            if i == 0:
                w.wait()
            left = jnp.concatenate([d[blocks[i], :] for d in d_refs[j * per : (j + 1) * per]], 1)
            term = dot_nt(left, weights[j])
            total = term if total is None else total + term
        return total

    dnf, gain_total = product(0), None
    for c in wo_in:
        c.wait()
    for i, own in enumerate(blocks):
        upcoming = product(i + 1) if i + 1 < len(blocks) else None
        h1_in[i].wait()
        d_rows, gain_part = norm_back_rows(h1_ref[own, :], dnf, gain_ref[...][None, :])
        gain_total = gain_part if gain_total is None else gain_total + gain_part
        back = eb_ref[own, :].astype(F32) + d_rows
        dh1_ref[own, :] = back
        rounded = back.astype(BF16)
        do_ref[own, :] = dot_nt(rounded, wo[...]).astype(BF16)
        store_transposed(rounded, turn, abt.at[:, own], me_ref, dp)
        dnf = upcoming
    dgain_ref[...] = gain_total
    quarter = width // 4
    for start in range(0, width, quarter):
        own = slice(start, start + quarter)
        total = dot(abt[own, :], o_ref[...])
        there_ref[own, :] = total[:, cols:].astype(BF16)
        here_ref[own, :] = total[:, :cols].astype(BF16)


def ffn_back(dp, me, h1, eb, gain, wg, wu, wo, o, d):
    count, width = h1.shape
    half, cols = wg[0].shape[1], wo[0].shape[0]
    return pl.pallas_call(
        functools.partial(ffn_back_kernel, dp),
        in_specs=[SCALAR, CHIP, ANY, CHIP, CHIP, [CHIP] * len(d), [ANY] * 2, [ANY] * 2, [ANY] * 2],
        out_specs=[CHIP] * 5,
        out_shape=[
            vmem((count, width), F32),
            vmem((count, 2 * cols), BF16),
            vmem((1, width), F32),
            vmem((width, cols), BF16),
            vmem((width, cols), BF16),
        ],
        scratch_shapes=[
            pltpu.VMEM((count, width), F32),
            pltpu.VMEM((4, width, half), BF16),
            pltpu.VMEM((2 * cols, width), BF16),
            pltpu.VMEM((width, ROWS), BF16),
            pltpu.VMEM((width, count), BF16),
            pltpu.SemaphoreType.DMA((6 + count // ROWS,)),
        ],
        compiler_params=params(26),
        cost_estimate=cost(4 * count * width * (2 * half + 2 * cols), 20 * count * width + 8 * count * half),
        name="ffn_back",
    )(
        me, on_chip(gain), off_chip(h1), *on_chip((eb, o)), list(on_chip(d)),
        [off_chip(wg[0]), wg[1]], [off_chip(wu[0]), wu[1]], [off_chip(wo[0]), wo[1]],
    )


def join_kernel(here_ref, recv_ref, *rest):
    outs = rest[4:8]
    quarter, cut = here_ref.shape[0] // 4, here_ref.shape[1] // 2
    spare = slice(outs[0].shape[2] - cut, outs[0].shape[2])
    for place in range(4):
        own = slice(place * quarter, place * quarter + quarter)
        values = here_ref[own, :].astype(F32) + recv_ref[own, :].astype(F32)
        b0, b1 = place // 2, place % 2
        (outs[0] if b0 else outs[1])[b1, :, spare] = values[:, :cut].astype(BF16)
        (outs[2] if b1 else outs[3])[b0, :, spare] = values[:, cut:].astype(BF16)


def join(here, recv, pieces):
    return pl.pallas_call(
        join_kernel,
        in_specs=[CHIP] * 2 + [CHIP] * 4,
        out_specs=[CHIP] * 4,
        out_shape=[vmem(p.shape, BF16) for p in pieces],
        input_output_aliases={2 + i: i for i in range(4)},
        compiler_params=params(16),
        cost_estimate=cost(here.size, 6 * here.size),
        name="join",
    )(*on_chip((here, recv)), *on_chip(pieces))


def finish_kernel(
    items, me_ref, lens_ref, gain_ref, dh1_ref, d_refs, x_hbm, w_hbm, h1_hbm, wd_hbm, hid_hbm,
    gin_hbm, out_hbm, dgain_ref, weights, x, gin, h1, wd, hid, out, in_sems, out_sems
):
    arrive, sent = Copies(in_sems), Copies(out_sems)
    cols, per = w_hbm[0].shape[1], 3
    w_in = [
        arrive.start(w, weights.at[i // per, :, (i % per) * cols : (i % per + 1) * cols]) for i, w in enumerate(w_hbm)
    ]
    blocks = row_blocks(x.shape[0])
    x_in = [arrive.start(x_hbm.at[own, :], x.at[own, :]) for own in blocks]
    half, size = wd_hbm[0].shape[0], hid_hbm[0].shape[1]
    wd_in = [arrive.start(w, wd.at[i * half : (i + 1) * half, :]) for i, w in enumerate(wd_hbm)]
    row_in = [
        [arrive.start(h.at[own, :], hid.at[own, j * size : (j + 1) * size]) for j, h in enumerate(hid_hbm)]
        + [arrive.start(h1_hbm.at[own, :], h1.at[own, :])]
        for own in blocks
    ]

    def product(i):
        total = None
        for j in range(len(w_in) // per):
            if i == 0:
                for c in w_in[j * per : (j + 1) * per]:
                    c.wait()
            left = jnp.concatenate([d[blocks[i], :] for d in d_refs[j * per : (j + 1) * per]], 1)
            term = dot_nt(left, weights[j])
            total = term if total is None else total + term
        return total

    def down(i):
        if i == 0:
            for c in wd_in:
                c.wait()
        for c in row_in[i]:
            c.wait()
        return dot(hid[blocks[i], :], wd[...])

    dna, gain_total, total = product(0), None, None
    for i, own in enumerate(blocks):
        upcoming = product(i + 1) if i + 1 < len(blocks) else None
        if i + 1 == len(blocks):
            total = down(0)
        x_in[i].wait()
        d_rows, gain_part = norm_back_rows(x[own, :].astype(F32), dna, gain_ref[...][None, :])
        gain_total = gain_part if gain_total is None else gain_total + gain_part
        gin[own, :] = dh1_ref[own, :] + d_rows
        sent.start(gin.at[own, :], gin_hbm.at[own, :])
        dna = upcoming
    dgain_ref[...] = gain_total
    for i, own in enumerate(blocks):
        upcoming = down(i + 1) if i + 1 < len(blocks) else None
        total = total + h1[own, :]
        out[own, :] = jnp.where(row_is_valid(me_ref, lens_ref, items, own.start), total, 0.0).astype(BF16)
        sent.start(out.at[own, :], out_hbm.at[own, :])
        total = upcoming
    sent.wait()


def finish(me, lens, x, dh1, gain, weights, grads, h1, wd, hid):
    count, width = x.shape
    cols, half = weights[0].shape[1], wd[0].shape[0]
    deep, mine, steps = cols * len(weights), len(weights) // 2, count // ROWS
    return pl.pallas_call(
        functools.partial(finish_kernel, count // SLOTS),
        in_specs=[SCALAR, SCALAR, CHIP, CHIP, [CHIP] * len(grads), ANY, [ANY] * len(weights), ANY, [ANY] * 2, [ANY] * len(hid)],
        out_specs=[ANY, ANY, CHIP],
        out_shape=[hbm((count, width), F32), hbm((count, width), BF16), vmem((1, width), F32)],
        scratch_shapes=[
            pltpu.VMEM((2, width, deep // 2), BF16),
            pltpu.VMEM((count, width), BF16),
            pltpu.VMEM((count, width), F32),
            pltpu.VMEM((count, width), F32),
            pltpu.VMEM((2 * half, width), BF16),
            pltpu.VMEM((count, 2 * half), BF16),
            pltpu.VMEM((count, width), BF16),
            pltpu.SemaphoreType.DMA((len(weights) + 2 + steps * (2 + len(hid)),)),
            pltpu.SemaphoreType.DMA((2 * steps,)),
        ],
        compiler_params=params(40),
        cost_estimate=cost(2 * count * width * (deep + 2 * half), 16 * count * width + 2 * count * (deep + 2 * half)),
        name="finish",
    )(
        me, lens, *on_chip((gain, dh1)), list(on_chip(grads)), off_chip(x),
        [*off_chip(weights[:mine]), *weights[mine:]], off_chip(h1), [off_chip(wd[0]), wd[1]], list(off_chip(hid)),
    )


def second_kernel(keep_a, recv_a, keep_b, recv_b, send_a, send_b):
    send_a[...] = (keep_a[1].astype(F32) + recv_a[1].astype(F32)).astype(BF16)
    send_b[...] = (keep_b[1].astype(F32) + recv_b[1].astype(F32)).astype(BF16)


def third_kernel(keep_a, recv_a, last_a, keep_b, recv_b, last_b, keep_ref, send_refs):
    group, cut = keep_ref.shape[0], keep_a.shape[2]
    for z in range(len(send_refs) + 1):
        own = slice(z * group, z * group + group)
        for cols, keep, recv, last in (
            (slice(0, cut), keep_a, recv_a, last_a),
            (slice(cut, 2 * cut), keep_b, recv_b, last_b),
        ):
            total = keep[0, own, :].astype(F32) + recv[0, own, :].astype(F32) + last[own, :].astype(F32)
            if z:
                send_refs[z - 1][:, cols] = total.astype(BF16)
            else:
                keep_ref[:, cols] = total


def swap_dp(array, dp, relative):
    return lax.ppermute(array, "dp", [(i, i ^ relative) for i in range(dp)])


def first_swaps(pieces, dp):
    return swap_dp(pieces[0], dp, 1), swap_dp(pieces[2], dp, 2)


def second_swaps(pieces, recv, dp):
    _, keep_a, _, keep_b = pieces
    _, quarter, cut = keep_a.shape
    next_a, next_b = pl.pallas_call(
        second_kernel,
        out_shape=[sds((quarter, cut), BF16)] * 2,
        compiler_params=params(24),
        cost_estimate=cost(quarter * cut * 2, quarter * cut * 12),
        name="second_sum",
    )(keep_a, recv[0], keep_b, recv[1])
    return swap_dp(next_a, dp, 2), swap_dp(next_b, dp, 1)


def third_swaps(pieces, recv, last, dp):
    _, keep_a, _, keep_b = pieces
    _, quarter, cut = keep_a.shape
    far = dp // 4
    group = quarter // far
    kept, sends = pl.pallas_call(
        third_kernel,
        out_shape=[sds((group, 2 * cut), F32), [sds((group, 2 * cut), BF16)] * (far - 1)],
        compiler_params=params(24),
        cost_estimate=cost(quarter * cut * 4, quarter * cut * 16),
        name="third_sum",
    )(keep_a, recv[0], last[0], keep_b, recv[1], last[1])
    return kept, tuple(swap_dp(send, dp, 4 * (z + 1)) for z, send in enumerate(sends))


def direct_kernel(keep, recv_refs, keep_ref, send_refs):
    group = keep_ref.shape[0]
    for z in range(len(send_refs) + 1):
        own = slice(z * group, z * group + group)
        total = keep[own, :].astype(F32)
        for recv in recv_refs:
            total = total + recv[own, :].astype(F32)
        if z:
            send_refs[z - 1][...] = total.astype(BF16)
        else:
            keep_ref[...] = total


def direct_swaps(pieces, dp):
    return tuple(swap_dp(piece, dp, relative) for piece, relative in zip(pieces[1:], (2, 1, 3)))


def direct_far_swaps(keep, recv, dp):
    quarter, cols = keep.shape
    far = dp // 4
    group = quarter // far
    kept, sends = pl.pallas_call(
        direct_kernel,
        out_shape=[sds((group, cols), F32), [sds((group, cols), BF16)] * (far - 1)],
        compiler_params=params(24),
        cost_estimate=cost(quarter * cols * 4, quarter * cols * 10),
        name="direct_sum",
    )(keep, list(recv))
    return kept, tuple(swap_dp(send, dp, 4 * (z + 1)) for z, send in enumerate(sends))


def last_kernel(kept, far_refs, outs):
    for p in range(kept.shape[1] // (3 * PAIR)):
        for j, out in enumerate(outs):
            own = slice((3 * p + j) * PAIR, (3 * p + j + 1) * PAIR)
            total = kept[:, own]
            for far in far_refs:
                total = total + far[:, own].astype(F32)
            out[:, p * PAIR : (p + 1) * PAIR] = total


def last_sum(kept, far):
    group, cols = kept.shape
    return pl.pallas_call(
        lambda kept, far_refs, *outs: last_kernel(kept, far_refs, outs),
        out_shape=[sds((group, cols // 3), F32)] * 3,
        compiler_params=params(16),
        name="last_sum",
    )(kept, list(far))


def total_of(kept, arrived):
    for part in arrived:
        kept = kept + part.astype(F32)
    return kept


fence = lax.optimization_barrier


def swap_sum(values, dp, relatives):
    count = 1 << len(relatives)
    terms = [values]
    for r in range(1, count):
        relative = sum(bit for i, bit in enumerate(relatives) if r >> i & 1)
        terms.append(swap_dp(values, dp, relative))
    while len(terms) > 1:
        terms = [terms[i] + terms[i + 1] for i in range(0, len(terms), 2)]
    return terms[0]


def local(
    dp, mp, tokens, lengths, gain_attn, w_query, w_key, w_value, w_out, gain_ffn, w_gate, w_up, w_down, cotangent
):
    count, width = tokens.shape
    me = jnp.stack([lax.axis_index("dp"), lax.axis_index("mp")]).astype(jnp.int32)
    gain_a, gain_f = gain_attn, gain_ffn

    def other(array):
        return lax.ppermute(array, "mp", [(0, 1), (1, 0)])

    wq, wk, wv, wo, wg, wu, wd = (
        (w, other(w)) for w in (w_query, w_key, w_value, w_out, w_gate, w_up, w_down)
    )
    tables = tuple(jnp.asarray(t) for t in position_tables(count))

    na, nat, eb, ebt = prepare(dp, me, lengths, tokens, cotangent, gain_a)
    na, wq, wk, wv = fence((na, wq, wk, wv))
    nat, ebt = finish_transposed(nat, me, dp), finish_transposed(ebt, me, dp)
    q, k, v, h1, o, lse, nf, nft = front(
        dp, me, na, tables, gain_f, ((wq[0], wk[0], wv[0]), (wq[1], wk[1], wv[1])), wo, tokens
    )
    nft = finish_transposed(nft, me, dp)

    half = w_gate.shape[1]
    chunks = half // CHUNK
    made, back = [], []
    for c in range(chunks):
        nf, made = fence((nf, made))
        *rest, there = ffn(nf, nft, eb, ebt, wg[1], wu[1], wd[1], c)
        made.append(rest)
        back.append(other(there))
    theirs = made
    made, pieces, recv = [], [], []
    for c in range(chunks):
        nf, here, theirs, made = fence((nf, back[c], theirs, made))
        spare = w_out.shape[0] // 2 if c == chunks - 1 else 0
        *rest, sa, ka, sb, kb = ffn(nf, nft, eb, ebt, wg[0], wu[0], wd[0], c, here, spare)
        made.append(rest)
        pieces.append((sa, ka, sb, kb))
        recv.append(first_swaps(pieces[-1], dp) if c < chunks - 1 else None)
    h1, recv, made, theirs = fence((h1, recv[:-1], made, theirs))
    last = [second_swaps(p, r, dp) for p, r in zip(pieces, recv)]
    parts = made + theirs
    hid = [p[0] for p in parts]
    dh1, do, dgain_f, out_there, out_here = ffn_back(
        dp, me, h1, eb, gain_f, wg, wu, wo, o, [p[1] for p in parts] + [p[2] for p in parts]
    )
    out_there, out_here, last, do = fence((out_there, out_here, last, do))
    back_out = other(out_there)
    third = [third_swaps(p, r, l, dp) for p, r, l in zip(pieces, recv, last)]
    pieces[-1] = join(out_here, back_out, pieces[-1])
    recv.append(first_swaps(pieces[-1], dp))
    heads = w_query.shape[1] // PAIR
    do, pieces = fence((do, pieces))
    *d1, qkv_there = attention_back(q, k, v, do, lse, tables, nat, heads)
    qkv_there, d1, recv, third, do = fence((qkv_there, d1, recv, third, do))
    back_qkv = other(qkv_there)
    last_last = second_swaps(pieces[-1], recv[-1], dp)
    *d0, keep_q, s1, s2, s3 = attention_back(q, k, v, do, lse, tables, nat, 0, back_qkv)
    d0, s1, s2, s3, last_last = fence((d0, s1, s2, s3, last_last))
    recv_q = direct_swaps((keep_q, s1, s2, s3), dp)
    third.append(third_swaps(pieces[-1], recv[-1], last_last, dp))
    grad_input, output, dgain_a = finish(
        me, lengths, tokens, dh1, gain_a, (wq[0], wk[0], wv[0], wq[1], wk[1], wv[1]), (*d0, *d1), h1, wd, hid
    )
    dgain_a, recv_q, third = fence((dgain_a, recv_q, third))
    kept_q, far_q = direct_far_swaps(keep_q, recv_q, dp)
    gains = jnp.concatenate([dgain_a, dgain_f], 0)
    gains = gains + other(gains)
    gains = swap_sum(gains, dp, (1, 2))
    gains = swap_sum(gains, dp, [1 << i for i in range(2, dp.bit_length() - 1)])
    gq, gk, gv = last_sum(kept_q, far_q)
    summed = [total_of(*t) for t in third]
    wide = 3 * CHUNK
    ffn_pieces, out_cols = [], []
    for p in summed:
        cut = p.shape[1] // 2
        ffn_pieces.append(jnp.concatenate([p[:, : wide // 2], p[:, cut : cut + wide // 2]], 1))
        if cut > wide // 2:
            out_cols = [p[:, wide // 2 : cut], p[:, cut + wide // 2 :]]
    out_piece = jnp.concatenate(out_cols, 1)

    g_gate, g_up, g_down = (
        jnp.concatenate([p[:, i * CHUNK : (i + 1) * CHUNK] for p in ffn_pieces], 1) for i in range(3)
    )
    return (
        output, grad_input, gains[0], gq, gk, gv, out_piece.T, gains[1], g_gate, g_up, g_down.T,
    )


def solution(mesh):
    in_specs = (
        P(("dp", "mp"), None),
        P("dp"),
        P(),
        P(None, "mp"),
        P(None, "mp"),
        P(None, "mp"),
        P("mp", None),
        P(),
        P(None, "mp"),
        P(None, "mp"),
        P("mp", None),
        P(("dp", "mp"), None),
    )
    out_specs = (
        P(("dp", "mp"), None),
        P(("dp", "mp"), None),
        P(),
        P("dp", "mp"),
        P("dp", "mp"),
        P("dp", "mp"),
        P("mp", "dp"),
        P(),
        P("dp", "mp"),
        P("dp", "mp"),
        P("mp", "dp"),
    )
    body = functools.partial(local, mesh.shape["dp"], mesh.shape["mp"])
    return jax.shard_map(body, mesh=mesh, in_specs=in_specs, out_specs=out_specs, check_vma=False)
```

time: 1500 us -> 208 us (0.14)
  waiting for transfers between devices: 912 us -> 22.7 us
  matrix products: 221 us -> 0 us
  local copies, waits for them, and re-layouts: 225 us -> 9.53 us
  Pallas kernels: 0 us -> 131 us
  other arithmetic: 67.5 us -> 2.46 us
  blocking collectives: 40.7 us -> 0 us
  starting transfers between devices: 1.47 us -> 37.2 us
    reduce_scatter x11 -> x0, waiting for transfers between devices: 872 us -> none  [the longest x1 136 us: local(): lax.psum_scatter(grad_up, 'dp', scatter_dimension=0, tiled=True)]
    dot_general x49 -> x0, matrix products: 221 us -> none  [the longest x7 50.5 us: contract_rows(): lax.dot_general(left, right, (((0,), (0,)), ((), ())), preferred_element_...]
    dynamic_update_slice x16 -> x0, local copies, waits for them, and re-layouts: 165 us -> none  [local(): lax.map(attend_back, (q_items, k_items, v_items, lengths, log_norm, d_mix...]
    pallas_call x0 -> x17, Pallas kernels: none -> 131 us  [the longest x4 33.4 us: ffn(): pl.pallas_call(functools.partial(ffn_kernel, final, chunk * CHUNK, blocks...]
    psum x1 -> x0, blocking collectives: 40.7 us -> none  [local(): gain_grads = lax.psum((d_gain_attn, d_gain_ffn), ('dp', 'mp'))]
    all_gather x4 -> x0, waiting for transfers between devices: 39.4 us -> none  [the longest x1 13.9 us: local(): lax.all_gather(d_middle.astype(jnp.bfloat16), 'mp', axis=0, tiled=True)]
    ppermute x0 -> x38, starting transfers between devices: none -> 37.2 us  [the longest x26 34.4 us: swap_dp(): return lax.ppermute(array, 'dp', [(i, i ^ relative) for i in range(dp)])]
    reshape x6 -> x0, local copies, waits for them, and re-layouts: 24.4 us -> none  [the longest x1 5.45 us: local(): d_keys.reshape(all_rows, head_count, HEAD)]
  transfers between devices with their start and end apart: 15 -> 38, of which waited for: 13 -> 13; matrix products, arithmetic and copies ran while one was open for 6% -> 1% of each run, Pallas kernels for 0% -> 59%
where the time goes in v1:
time: 208 us; the launch traced here: 204 us
  Pallas kernels  131 us (63%)
  starting transfers between devices  37.2 us (18%)
  waiting for transfers between devices  22.7 us (11%)
  local copies, waits for them, and re-layouts  9.53 us (5%)
  other arithmetic  2.46 us (1%)
    ppermute x26, starting transfers between devices, swap_dp(): return lax.ppermute(array, 'dp', [(i, i ^ relative) for i in range(dp)])  34.4 us
    pallas_call x4, Pallas kernels, ffn(): pl.pallas_call(functools.partial(ffn_kernel, final, chunk * CHUNK, blocks...  33.4 us
    pallas_call x2, Pallas kernels, attention_back(): pl.pallas_call(functools.partial(attention_back_kernel, final, first), in...  30.9 us
    pallas_call x1, Pallas kernels, front(): pl.pallas_call(functools.partial(front_kernel, dp), in_specs=[SCALAR, CHI...  23.8 us
    pallas_call x1, Pallas kernels, ffn_back(): pl.pallas_call(functools.partial(ffn_back_kernel, dp), in_specs=[SCALAR,...  22 us
    ppermute x26, waiting for transfers between devices, swap_dp(): return lax.ppermute(array, 'dp', [(i, i ^ relative) for i in range(dp)])  18.6 us
    pallas_call x1, Pallas kernels, finish(): pl.pallas_call(functools.partial(finish_kernel, count // SLOTS), in_specs...  15.3 us
    unnamed x42, local copies, waits for them, and re-layouts  8.63 us
  transfers between devices with their start and end apart: 38, of which 13 were waited for; matrix products, arithmetic and copies ran while one was open for 1% of the time, Pallas kernels for 59%

profile of v1, /device:TPU:0, one launch (start us, length us, event | category | flops | bytes accessed | tf_op | source)
XLA Modules:
  0.0 204.4 jit_solution(15589482209718619786)
XLA Ops:
  7.3 3.8 %prepare.1 = (bf16[1152,768]{1,0:T(8,128)(2,1)S(1)}, bf16[768,1152]{1,0:T(8,128)(2,1)S(1)}, bf16[1152,768]{1,0:T(8,128)(2,1)S(1)}, bf16[768,1152]{1,0:T(8,128)(2,1)S(1)}) custom-call(s32[2]{0:T(128)S(1)} %pad_add_fusion.me_ref, s32[4]{0:T(128)S(1)} %copy-done.2, f32[768]{0:T(1024)S(1)} %copy-done, bf16[1152,768]{1,0:T(8,128)(2,1)} %x_hbm.5, ...), custom_call_target="tpu_custom_call" | custom-call | flops 8847360 | bytes 10616832 | tf_op jit(solution)/shard_map/prepare/pallas_call | solution.py:159
  11.2 23.8 %front.1 = (bf16[1152,768]{1,0:T(8,128)(2,1)}, bf16[1152,768]{1,0:T(8,128)(2,1)}, bf16[1152,768]{1,0:T(8,128)(2,1)}, f32[1152,768]{1,0:T(8,128)}, bf16[1152,768]...) custom-call(s32[2]{0:T(128)S(1)} %pad_add_fusion.me_ref, ...), custom_call_target="tpu_custom_call" | custom-call | flops 13589544960 | bytes 21233664 | tf_op jit(solution)/shard_map/front/pallas_call | solution.py:302
  35.0 8.3 %ffn_other.2 = (bf16[1152,512]{1,0:T(8,128)(2,1)}, bf16[1152,512]{1,0:T(8,128)(2,1)S(1)}, bf16[1152,512]{1,0:T(8,128)(2,1)S(1)}, bf16[768,1536]{1,0:T(8,128)(2,1)S(1)}) custom-call(bf16[1152,768]{1,0:T(8,128)(2,1)S(1)} %get-tuple-element.212.nf_ref, bf16[768,1152]{1,0:T(8,128)(2,1)S(1)} %get-tuple-element.181.nft_ref, ...), custom_call_target="tpu_custom_call" | custom-call | flops 5435817984 | bytes 11796480 | tf_op jit(solution)/shard_map/ffn_other/pallas_call | solution.py:531
  44.4 8.0 %ffn_other.3 = (bf16[1152,512]{1,0:T(8,128)(2,1)}, bf16[1152,512]{1,0:T(8,128)(2,1)S(1)}, bf16[1152,512]{1,0:T(8,128)(2,1)S(1)}, bf16[768,1536]{1,0:T(8,128)(2,1)S(1)}) custom-call(bf16[1152,768]{1,0:T(8,128)(2,1)S(1)} %get-tuple-element.212.nf_ref, bf16[768,1152]{1,0:T(8,128)(2,1)S(1)} %get-tuple-element.181.nft_ref, ...), custom_call_target="tpu_custom_call" | custom-call | flops 5435817984 | bytes 11796480 | tf_op jit(solution)/shard_map/ffn_other/pallas_call | solution.py:531
  54.7 8.4 %ffn_final.2 = (bf16[1152,512]{1,0:T(8,128)(2,1)}, bf16[1152,512]{1,0:T(8,128)(2,1)S(1)}, bf16[1152,512]{1,0:T(8,128)(2,1)S(1)}, bf16[2,192,768]{2,1,0:T(8,128)(...) custom-call(bf16[1152,768]{1,0:T(8,128)(2,1)S(1)} %get-tuple-element., ...), custom_call_target="tpu_custom_call" | custom-call | flops 5435817984 | bytes 11796480 | tf_op jit(solution)/shard_map/ffn_final/pallas_call | solution.py:531
  63.2 2.8 %collective-permute-start.8 = (bf16[2,192,768]{2,1,0:T(8,128)(2,1)S(1)}, bf16[2,192,768]{2,1,0:T(8,128)(2,1)S(1)}, u32[]{:S(2)}, u32[]{:S(2)}) collective-permute-start(bf16[2,192,768]{2,1,0:T(8,128)(2,1)S(1)} %get-tuple-element.197), channel_id=1, source_target_pairs={{0,2},{2,0},{4,6},{6,4},{8,10},{10,8},{12,14},{14,12},{16,18},{18,... | collective-permute-start | bytes 1769480 | tf_op jit(solution)/shard_map/ppermute | solution.py:768
  66.0 1.5 collective-permute-start.9
  67.5 8.8 %ffn_final.3 = (bf16[1152,512]{1,0:T(8,128)(2,1)}, bf16[1152,512]{1,0:T(8,128)(2,1)S(1)}, bf16[1152,512]{1,0:T(8,128)(2,1)S(1)}, bf16[2,192,960]{2,1,0:T(8,128)(...) custom-call(bf16[1152,768]{1,0:T(8,128)(2,1)S(1)} %get-tuple-element., ...), custom_call_target="tpu_custom_call" | custom-call | flops 5435817984 | bytes 11796480 | tf_op jit(solution)/shard_map/ffn_final/pallas_call | solution.py:531
  76.3 3.5 %collective-permute-done.8.recv_a = bf16[2,192,768]{2,1,0:T(8,128)(2,1)S(1)} collective-permute-done((bf16[2,192,768]{2,1,0:T(8,128)(2,1)S(1)}, bf16[2,192,768]{2,1,0:T(8,128)(2,1)S(1)}, u32[]{:S(2)}, u32[]{:S(2)}) %collective-permute-start.8) | collective-permute-done | bytes 589856 | tf_op jit(solution)/shard_map/ppermute | solution.py:768
  79.7 1.5 collective-permute-done.9.recv_b
  81.3 1.6 collective-permute-start.11
  83.5 1.3 copy-done.16
  84.7 1.3 copy-done.18
  86.0 22.0 %ffn_back.1 = (f32[1152,768]{1,0:T(8,128)S(1)}, bf16[1152,768]{1,0:T(8,128)(2,1)S(1)}, f32[1,768]{1,0:T(1,128)S(1)}, bf16[768,384]{1,0:T(8,128)(2,1)S(1)}, bf16[768,384]{1,0:T(8,128)(2,1)S(1)}) custom-call(s32[2]{0:T(128)S(1)} %pad_add_fusion.me_ref, f32[768]{0:T(1024)S(1)} %copy-done.8, f32[1152,768]{1,0:T(8,128)} %get-tuple-element.223.h1_hbm, ...), custom_call_target="tpu_custom_call" | custom-call | flops 9965666304 | bytes 27131904 | tf_op jit(solution)/shard_map/ffn_back/pallas_call | solution.py:606
  108.4 1.7 collective-permute-start.16
  110.0 2.6 %collective-permute-start.17 = (bf16[48,1536]{1,0:T(8,128)(2,1)S(1)}, bf16[48,1536]{1,0:T(8,128)(2,1)S(1)}, u32[]{:S(2)}, u32[]{:S(2)}) collective-permute-start(bf16[48,1536]{1,0:T(8,128)(2,1)S(1)} %get-tuple-element.268), channel_id=1, source_target_pairs={{0,16},{2,18},{4,20},{6,22},{8,24},{10,26},{12,28},{14,30},{16,0},... | collective-permute-start | bytes 442376 | tf_op jit(solution)/shard_map/ppermute | solution.py:768
  113.5 1.6 collective-permute-start.14
  115.5 15.4 %attention_back_other.1 = (bf16[1152,384]{1,0:T(8,128)(2,1)S(1)}, bf16[1152,384]{1,0:T(8,128)(2,1)S(1)}, bf16[1152,384]{1,0:T(8,128)(2,1)S(1)}, bf16[768,1152]{1,0:T(8,128)(2,1)S(1)}) custom-call(bf16[1152,768]{1,0:T(8,128)(2,1)S(1)} %get-tuple-element.270.d_ref, f32[6,4,576]{2,1,0:T(4,128)S(1)} %get-tuple-element.255.lse_ref, ...), custom_call_target="tpu_custom_call" | custom-call | flops 12230590464 | bytes 7077888 | tf_op jit(solution)/shard_map/attention_back_other/pallas_call | solution.py:429
  131.0 1.7 collective-permute-done.14.recv_a
  132.7 1.2 collective-permute-done.15.recv_b
  135.3 2.4 %collective-permute-done.19.rest_0_ = bf16[768,1152]{1,0:T(8,128)(2,1)S(1)} collective-permute-done((bf16[768,1152]{1,0:T(8,128)(2,1)S(1)}, bf16[768,1152]{1,0:T(8,128)(2,1)S(1)}, u32[]{:S(2)}, u32[]{:S(2)}) %collective-permute-start.19) | collective-permute-done | bytes 1769504 | tf_op jit(solution)/shard_map/ppermute | solution.py:882
  137.6 15.5 %attention_back_final.1 = (bf16[1152,384]{1,0:T(8,128)(2,1)S(1)}, bf16[1152,384]{1,0:T(8,128)(2,1)S(1)}, bf16[1152,384]{1,0:T(8,128)(2,1)S(1)}, bf16[192,1152]{1...) custom-call(bf16[1152,768]{1,0:T(8,128)(2,1)S(1)} %get-tuple-element, ...), custom_call_target="tpu_custom_call" | custom-call | flops 12230590464 | bytes 7077888 | tf_op jit(solution)/shard_map/attention_back_final/pallas_call | solution.py:429
  154.2 3.5 %collective-permute-start.26 = (bf16[48,1920]{1,0:T(8,128)(2,1)S(1)}, bf16[48,1920]{1,0:T(8,128)(2,1)S(1)}, u32[]{:S(2)}, u32[]{:S(2)}) collective-permute-start(bf16[48,1920]{1,0:T(8,128)(2,1)S(1)} %get-tuple-element.308), channel_id=1, source_target_pairs={{0,16},{2,18},{4,20},{6,22},{8,24},{10,26},{12,28},{14,30},{16,0},... | collective-permute-start | bytes 552968 | tf_op jit(solution)/shard_map/ppermute | solution.py:768
  159.0 4.7 %collective-permute-done.25 = bf16[48,1920]{1,0:T(8,128)(2,1)S(1)} collective-permute-done((bf16[48,1920]{1,0:T(8,128)(2,1)S(1)}, bf16[48,1920]{1,0:T(8,128)(2,1)S(1)}, u32[]{:S(2)}, u32[]{:S(2)}) %collective-permute-start.25) | collective-permute-done | bytes 184352 | tf_op jit(solution)/shard_map/ppermute | solution.py:768
  164.2 15.3 %finish.1 = (f32[1152,768]{1,0:T(8,128)}, bf16[1152,768]{1,0:T(8,128)(2,1)}, f32[1,768]{1,0:T(1,128)S(1)}) custom-call(s32[2]{0:T(128)S(1)} %pad_add_fusion.me_ref, s32[4]{0:T(128)S(1)} %copy-done.3, f32[768]{0:T(1024)S(1)} %copy-done.1, f32[1152,768]{1,0:T(8,128)S(1)} %copy-done.10, bf16[1152,384]{1,0:T(8,128)(2,1)S(1)} %get-tuple-element.284.d_refs_0_, ...), custom_call_target="tpu_custom_call" | custom-call | flops 7700742144 | bytes 24182784 | tf_op jit(solution)/shard_map/finish/pallas_call | solution.py:722
  181.3 3.5 %collective-permute-start.36 = (bf16[48,1152]{1,0:T(8,128)(2,1)S(1)}, bf16[48,1152]{1,0:T(8,128)(2,1)S(1)}, u32[]{:S(2)}, u32[]{:S(2)}) collective-permute-start(bf16[48,1152]{1,0:T(8,128)(2,1)S(1)} %get-tuple-element.318), channel_id=1, source_target_pairs={{0,16},{2,18},{4,20},{6,22},{8,24},{10,26},{12,28},{14,30},{16,0},... | collective-permute-start | bytes 331784 | tf_op jit(solution)/shard_map/ppermute | solution.py:768
  187.2 2.4 %collective-permute-start.31 = (f32[2,768]{1,0:T(2,128)S(1)}, f32[2,768]{1,0:T(2,128)S(1)}, u32[]{:S(2)}, u32[]{:S(2)}) collective-permute-start(f32[2,768]{1,0:T(2,128)S(1)} %fusion.1), channel_id=1, source_target_pairs={{0,6},{2,4},{4,2},{6,0},{8,14},{10,12},{12,10},{14,8},{16,22},{18,... | collective-permute-start | bytes 18440 | tf_op jit(solution)/shard_map/ppermute | solution.py:768
  190.4 1.4 collective-permute-done.31
  191.9 2.3 %collective-permute-start.33 = (f32[2,768]{1,0:T(2,128)S(1)}, f32[2,768]{1,0:T(2,128)S(1)}, u32[]{:S(2)}, u32[]{:S(2)}) collective-permute-start(f32[2,768]{1,0:T(2,128)S(1)} %add_add_fusion.1), channel_id=1, source_target_pairs={{0,16},{2,18},{4,20},{6,22},{8,24},{10,26},{12,28},{14,30},{16,0},... | collective-permute-start | bytes 18440 | tf_op jit(solution)/shard_map/ppermute | solution.py:768
  194.2 2.1 %collective-permute-start.34 = (f32[2,768]{1,0:T(2,128)S(1)}, f32[2,768]{1,0:T(2,128)S(1)}, u32[]{:S(2)}, u32[]{:S(2)}) collective-permute-start(f32[2,768]{1,0:T(2,128)S(1)} %add_add_fusion.1), channel_id=1, source_target_pairs={{0,24},{2,26},{4,28},{6,30},{8,16},{10,18},{12,20},{14,22},{16,8},... | collective-permute-start | bytes 18440 | tf_op jit(solution)/shard_map/ppermute | solution.py:768
  197.0 1.8 collective-permute-start.37
  200.3 3.2 %collective-permute-done.37.far_refs_2_ = bf16[48,1152]{1,0:T(8,128)(2,1)S(1)} collective-permute-done((bf16[48,1152]{1,0:T(8,128)(2,1)S(1)}, bf16[48,1152]{1,0:T(8,128)(2,1)S(1)}, u32[]{:S(2)}, u32[]{:S(2)}) %collective-permute-start.37) | collective-permute-done | bytes 110624 | tf_op jit(solution)/shard_map/ppermute | solution.py:768
  (118 shorter events, 24.6 us)
Async XLA Ops:
  1.2 9.9 %collective-permute-start.2 = (bf16[768,384]{1,0:T(8,128)(2,1)}, bf16[768,384]{1,0:T(8,128)(2,1)}, u32[]{:S(2)}, u32[]{:S(2)}) collective-permute-start(bf16[768,384]{1,0:T(8,128)(2,1)} %w_hbm_2_), channel_id=1, source_target_pairs={{0,1},{1,0},{2,3},{3,2},{4,5},{5,4},{6,7},{7,6},{8,9},{9,8},{10,11... | collective-permute-start | bytes 1769480 | tf_op jit(solution)/shard_map/ppermute | solution.py:882
  1.7 9.5 %collective-permute-start.3 = (bf16[384,768]{1,0:T(8,128)(2,1)}, bf16[384,768]{1,0:T(8,128)(2,1)}, u32[]{:S(2)}, u32[]{:S(2)}) collective-permute-start(bf16[384,768]{1,0:T(8,128)(2,1)} %wo_hbm_0_.3), channel_id=1, source_target_pairs={{0,1},{1,0},{2,3},{3,2},{4,5},{5,4},{6,7},{7,6},{8,9},{9,8},{10,11... | collective-permute-start | bytes 1769480 | tf_op jit(solution)/shard_map/ppermute | solution.py:882
  1.8 33.2 %collective-permute-start.4 = (bf16[768,1024]{1,0:T(8,128)(2,1)}, bf16[768,1024]{1,0:T(8,128)(2,1)S(1)}, u32[]{:S(2)}, u32[]{:S(2)}) collective-permute-start(bf16[768,1024]{1,0:T(8,128)(2,1)} %wg_hbm_0_.1), channel_id=1, source_target_pairs={{0,1},{1,0},{2,3},{3,2},{4,5},{5,4},{6,7},{7,6},{8,9},{9,8},{10,11... | collective-permute-start | bytes 4718600 | tf_op jit(solution)/shard_map/ppermute | solution.py:882
  3.8 31.2 %collective-permute-start.5 = (bf16[768,1024]{1,0:T(8,128)(2,1)}, bf16[768,1024]{1,0:T(8,128)(2,1)}, u32[]{:S(2)}, u32[]{:S(2)}) collective-permute-start(bf16[768,1024]{1,0:T(8,128)(2,1)} %wu_hbm_0_.1), channel_id=1, source_target_pairs={{0,1},{1,0},{2,3},{3,2},{4,5},{5,4},{6,7},{7,6},{8,9},{9,8},{10,11... | collective-permute-start | bytes 4718600 | tf_op jit(solution)/shard_map/ppermute | solution.py:882
  5.5 29.5 %collective-permute-start.6 = (bf16[1024,768]{1,0:T(8,128)(2,1)}, bf16[1024,768]{1,0:T(8,128)(2,1)S(1)}, u32[]{:S(2)}, u32[]{:S(2)}) collective-permute-start(bf16[1024,768]{1,0:T(8,128)(2,1)} %wd_hbm_0_.1), channel_id=1, source_target_pairs={{0,1},{1,0},{2,3},{3,2},{4,5},{5,4},{6,7},{7,6},{8,9},{9,8},{10,11... | collective-permute-start | bytes 4718600 | tf_op jit(solution)/shard_map/ppermute | solution.py:882
  44.3 10.4 %collective-permute-start.7 = (bf16[768,1536]{1,0:T(8,128)(2,1)S(1)}, bf16[768,1536]{1,0:T(8,128)(2,1)S(1)}, u32[]{:S(2)}, u32[]{:S(2)}) collective-permute-start(bf16[768,1536]{1,0:T(8,128)(2,1)S(1)} %get-tuple-element.188), channel_id=1, source_target_pairs={{0,1},{1,0},{2,3},{3,2},{4,5},{5,4},{6,7},{7,6},{8,9},{9,8},{10,11... | collective-permute-start | bytes 7077896 | tf_op jit(solution)/shard_map/ppermute | solution.py:882
  54.5 13.0 %collective-permute-start.10 = (bf16[768,1536]{1,0:T(8,128)(2,1)S(1)}, bf16[768,1536]{1,0:T(8,128)(2,1)S(1)}, u32[]{:S(2)}, u32[]{:S(2)}) collective-permute-start(bf16[768,1536]{1,0:T(8,128)(2,1)S(1)} %get-tuple-element.199), channel_id=1, source_target_pairs={{0,1},{1,0},{2,3},{3,2},{4,5},{5,4},{6,7},{7,6},{8,9},{9,8},{10,11... | collective-permute-start | bytes 7077896 | tf_op jit(solution)/shard_map/ppermute | solution.py:882
  63.2 16.5 %collective-permute-start.8 = (bf16[2,192,768]{2,1,0:T(8,128)(2,1)S(1)}, bf16[2,192,768]{2,1,0:T(8,128)(2,1)S(1)}, u32[]{:S(2)}, u32[]{:S(2)}) collective-permute-start(bf16[2,192,768]{2,1,0:T(8,128)(2,1)S(1)} %get-tuple-element.197), channel_id=1, source_target_pairs={{0,2},{2,0},{4,6},{6,4},{8,10},{10,8},{12,14},{14,12},{16,18},{18,... | collective-permute-start | bytes 1769480 | tf_op jit(solution)/shard_map/ppermute | solution.py:768
  66.0 15.2 %collective-permute-start.9 = (bf16[2,192,768]{2,1,0:T(8,128)(2,1)S(1)}, bf16[2,192,768]{2,1,0:T(8,128)(2,1)S(1)}, u32[]{:S(2)}, u32[]{:S(2)}) collective-permute-start(bf16[2,192,768]{2,1,0:T(8,128)(2,1)S(1)} %get-tuple-element.198), channel_id=1, source_target_pairs={{0,4},{2,6},{4,0},{6,2},{8,12},{10,14},{12,8},{14,10},{16,20},{18,... | collective-permute-start | bytes 1769480 | tf_op jit(solution)/shard_map/ppermute | solution.py:768
  81.3 26.7 %collective-permute-start.11 = (bf16[192,768]{1,0:T(8,128)(2,1)S(1)}, bf16[192,768]{1,0:T(8,128)(2,1)S(1)}, u32[]{:S(2)}, u32[]{:S(2)}) collective-permute-start(bf16[192,768]{1,0:T(8,128)(2,1)S(1)} %get-tuple-element.240), channel_id=1, source_target_pairs={{0,4},{2,6},{4,0},{6,2},{8,12},{10,14},{12,8},{14,10},{16,20},{18,... | collective-permute-start | bytes 884744 | tf_op jit(solution)/shard_map/ppermute | solution.py:768
  82.9 25.1 %collective-permute-start.12 = (bf16[192,768]{1,0:T(8,128)(2,1)S(1)}, bf16[192,768]{1,0:T(8,128)(2,1)S(1)}, u32[]{:S(2)}, u32[]{:S(2)}) collective-permute-start(bf16[192,768]{1,0:T(8,128)(2,1)S(1)} %get-tuple-element.241), channel_id=1, source_target_pairs={{0,2},{2,0},{4,6},{6,4},{8,10},{10,8},{12,14},{14,12},{16,18},{18,... | collective-permute-start | bytes 884744 | tf_op jit(solution)/shard_map/ppermute | solution.py:768
  108.1 5.2 %collective-permute-start.13 = (bf16[768,384]{1,0:T(8,128)(2,1)S(1)}, bf16[768,384]{1,0:T(8,128)(2,1)S(1)}, u32[]{:S(2)}, u32[]{:S(2)}) collective-permute-start(bf16[768,384]{1,0:T(8,128)(2,1)S(1)} %get-tuple-element.245), channel_id=1, source_target_pairs={{0,1},{1,0},{2,3},{3,2},{4,5},{5,4},{6,7},{7,6},{8,9},{9,8},{10,11... | collective-permute-start | bytes 1769480 | tf_op jit(solution)/shard_map/ppermute | solution.py:882
  108.4 22.6 %collective-permute-start.16 = (bf16[48,1536]{1,0:T(8,128)(2,1)S(1)}, bf16[48,1536]{1,0:T(8,128)(2,1)S(1)}, u32[]{:S(2)}, u32[]{:S(2)}) collective-permute-start(bf16[48,1536]{1,0:T(8,128)(2,1)S(1)} %get-tuple-element.267), channel_id=1, source_target_pairs={{0,8},{2,10},{4,12},{6,14},{8,0},{10,2},{12,4},{14,6},{16,24},{18,... | collective-permute-start | bytes 442376 | tf_op jit(solution)/shard_map/ppermute | solution.py:768
  110.0 21.0 %collective-permute-start.17 = (bf16[48,1536]{1,0:T(8,128)(2,1)S(1)}, bf16[48,1536]{1,0:T(8,128)(2,1)S(1)}, u32[]{:S(2)}, u32[]{:S(2)}) collective-permute-start(bf16[48,1536]{1,0:T(8,128)(2,1)S(1)} %get-tuple-element.268), channel_id=1, source_target_pairs={{0,16},{2,18},{4,20},{6,22},{8,24},{10,26},{12,28},{14,30},{16,0},... | collective-permute-start | bytes 442376 | tf_op jit(solution)/shard_map/ppermute | solution.py:768
  112.6 18.4 %collective-permute-start.18 = (bf16[48,1536]{1,0:T(8,128)(2,1)S(1)}, bf16[48,1536]{1,0:T(8,128)(2,1)S(1)}, u32[]{:S(2)}, u32[]{:S(2)}) collective-permute-start(bf16[48,1536]{1,0:T(8,128)(2,1)S(1)} %get-tuple-element.269), channel_id=1, source_target_pairs={{0,24},{2,26},{4,28},{6,30},{8,16},{10,18},{12,20},{14,22},{16,8},... | collective-permute-start | bytes 442376 | tf_op jit(solution)/shard_map/ppermute | solution.py:768
  113.5 19.3 %collective-permute-start.14 = (bf16[2,192,960]{2,1,0:T(8,128)(2,1)S(1)}, bf16[2,192,960]{2,1,0:T(8,128)(2,1)S(1)}, u32[]{:S(2)}, u32[]{:S(2)}) collective-permute-start(bf16[2,192,960]{2,1,0:T(8,128)(2,1)S(1)} %get-tuple-element.250), channel_id=1, source_target_pairs={{0,2},{2,0},{4,6},{6,4},{8,10},{10,8},{12,14},{14,12},{16,18},{18,... | collective-permute-start | bytes 2211848 | tf_op jit(solution)/shard_map/ppermute | solution.py:768
  115.0 18.9 %collective-permute-start.15 = (bf16[2,192,960]{2,1,0:T(8,128)(2,1)S(1)}, bf16[2,192,960]{2,1,0:T(8,128)(2,1)S(1)}, u32[]{:S(2)}, u32[]{:S(2)}) collective-permute-start(bf16[2,192,960]{2,1,0:T(8,128)(2,1)S(1)} %get-tuple-element.252), channel_id=1, source_target_pairs={{0,4},{2,6},{4,0},{6,2},{8,12},{10,14},{12,8},{14,10},{16,20},{18,... | collective-permute-start | bytes 2211848 | tf_op jit(solution)/shard_map/ppermute | solution.py:768
  134.1 19.0 %collective-permute-start.20 = (bf16[192,960]{1,0:T(8,128)(2,1)S(1)}, bf16[192,960]{1,0:T(8,128)(2,1)S(1)}, u32[]{:S(2)}, u32[]{:S(2)}) collective-permute-start(bf16[192,960]{1,0:T(8,128)(2,1)S(1)} %get-tuple-element.282), channel_id=1, source_target_pairs={{0,4},{2,6},{4,0},{6,2},{8,12},{10,14},{12,8},{14,10},{16,20},{18,... | collective-permute-start | bytes 1105928 | tf_op jit(solution)/shard_map/ppermute | solution.py:768
  134.7 18.4 %collective-permute-start.21 = (bf16[192,960]{1,0:T(8,128)(2,1)S(1)}, bf16[192,960]{1,0:T(8,128)(2,1)S(1)}, u32[]{:S(2)}, u32[]{:S(2)}) collective-permute-start(bf16[192,960]{1,0:T(8,128)(2,1)S(1)} %get-tuple-element.283), channel_id=1, source_target_pairs={{0,2},{2,0},{4,6},{6,4},{8,10},{10,8},{12,14},{14,12},{16,18},{18,... | collective-permute-start | bytes 1105928 | tf_op jit(solution)/shard_map/ppermute | solution.py:768
  153.5 10.2 %collective-permute-start.25 = (bf16[48,1920]{1,0:T(8,128)(2,1)S(1)}, bf16[48,1920]{1,0:T(8,128)(2,1)S(1)}, u32[]{:S(2)}, u32[]{:S(2)}) collective-permute-start(bf16[48,1920]{1,0:T(8,128)(2,1)S(1)} %get-tuple-element.307), channel_id=1, source_target_pairs={{0,8},{2,10},{4,12},{6,14},{8,0},{10,2},{12,4},{14,6},{16,24},{18,... | collective-permute-start | bytes 552968 | tf_op jit(solution)/shard_map/ppermute | solution.py:768
  154.2 25.3 %collective-permute-start.26 = (bf16[48,1920]{1,0:T(8,128)(2,1)S(1)}, bf16[48,1920]{1,0:T(8,128)(2,1)S(1)}, u32[]{:S(2)}, u32[]{:S(2)}) collective-permute-start(bf16[48,1920]{1,0:T(8,128)(2,1)S(1)} %get-tuple-element.308), channel_id=1, source_target_pairs={{0,16},{2,18},{4,20},{6,22},{8,24},{10,26},{12,28},{14,30},{16,0},... | collective-permute-start | bytes 552968 | tf_op jit(solution)/shard_map/ppermute | solution.py:768
  157.7 21.8 %collective-permute-start.27 = (bf16[48,1920]{1,0:T(8,128)(2,1)S(1)}, bf16[48,1920]{1,0:T(8,128)(2,1)S(1)}, u32[]{:S(2)}, u32[]{:S(2)}) collective-permute-start(bf16[48,1920]{1,0:T(8,128)(2,1)S(1)} %get-tuple-element.309), channel_id=1, source_target_pairs={{0,24},{2,26},{4,28},{6,30},{8,16},{10,18},{12,20},{14,22},{16,8},... | collective-permute-start | bytes 552968 | tf_op jit(solution)/shard_map/ppermute | solution.py:768
  158.0 21.5 %collective-permute-start.22 = (bf16[192,1152]{1,0:T(8,128)(2,1)S(1)}, bf16[192,1152]{1,0:T(8,128)(2,1)S(1)}, u32[]{:S(2)}, u32[]{:S(2)}) collective-permute-start(bf16[192,1152]{1,0:T(8,128)(2,1)S(1)} %get-tuple-element.297), channel_id=1, source_target_pairs={{0,4},{2,6},{4,0},{6,2},{8,12},{10,14},{12,8},{14,10},{16,20},{18,... | collective-permute-start | bytes 1327112 | tf_op jit(solution)/shard_map/ppermute | solution.py:768
  158.5 21.0 %collective-permute-start.23 = (bf16[192,1152]{1,0:T(8,128)(2,1)S(1)}, bf16[192,1152]{1,0:T(8,128)(2,1)S(1)}, u32[]{:S(2)}, u32[]{:S(2)}) collective-permute-start(bf16[192,1152]{1,0:T(8,128)(2,1)S(1)} %get-tuple-element.298), channel_id=1, source_target_pairs={{0,2},{2,0},{4,6},{6,4},{8,10},{10,8},{12,14},{14,12},{16,18},{18,... | collective-permute-start | bytes 1327112 | tf_op jit(solution)/shard_map/ppermute | solution.py:768
  163.7 16.3 %collective-permute-start.24 = (bf16[192,1152]{1,0:T(8,128)(2,1)S(1)}, bf16[192,1152]{1,0:T(8,128)(2,1)S(1)}, u32[]{:S(2)}, u32[]{:S(2)}) collective-permute-start(bf16[192,1152]{1,0:T(8,128)(2,1)S(1)} %get-tuple-element.299), channel_id=1, source_target_pairs={{0,6},{2,4},{4,2},{6,0},{8,14},{10,12},{12,10},{14,8},{16,22},{18,... | collective-permute-start | bytes 1327112 | tf_op jit(solution)/shard_map/ppermute | solution.py:768
  180.7 19.6 %collective-permute-start.35 = (bf16[48,1152]{1,0:T(8,128)(2,1)S(1)}, bf16[48,1152]{1,0:T(8,128)(2,1)S(1)}, u32[]{:S(2)}, u32[]{:S(2)}) collective-permute-start(bf16[48,1152]{1,0:T(8,128)(2,1)S(1)} %get-tuple-element.317), channel_id=1, source_target_pairs={{0,8},{2,10},{4,12},{6,14},{8,0},{10,2},{12,4},{14,6},{16,24},{18,... | collective-permute-start | bytes 331784 | tf_op jit(solution)/shard_map/ppermute | solution.py:768
  181.3 19.0 %collective-permute-start.36 = (bf16[48,1152]{1,0:T(8,128)(2,1)S(1)}, bf16[48,1152]{1,0:T(8,128)(2,1)S(1)}, u32[]{:S(2)}, u32[]{:S(2)}) collective-permute-start(bf16[48,1152]{1,0:T(8,128)(2,1)S(1)} %get-tuple-element.318), channel_id=1, source_target_pairs={{0,16},{2,18},{4,20},{6,22},{8,24},{10,26},{12,28},{14,30},{16,0},... | collective-permute-start | bytes 331784 | tf_op jit(solution)/shard_map/ppermute | solution.py:768
  187.2 4.5 %collective-permute-start.31 = (f32[2,768]{1,0:T(2,128)S(1)}, f32[2,768]{1,0:T(2,128)S(1)}, u32[]{:S(2)}, u32[]{:S(2)}) collective-permute-start(f32[2,768]{1,0:T(2,128)S(1)} %fusion.1), channel_id=1, source_target_pairs={{0,6},{2,4},{4,2},{6,0},{8,14},{10,12},{12,10},{14,8},{16,22},{18,... | collective-permute-start | bytes 18440 | tf_op jit(solution)/shard_map/ppermute | solution.py:768
  191.8 5.2 %collective-permute-start.32 = (f32[2,768]{1,0:T(2,128)S(1)}, f32[2,768]{1,0:T(2,128)S(1)}, u32[]{:S(2)}, u32[]{:S(2)}) collective-permute-start(f32[2,768]{1,0:T(2,128)S(1)} %add_add_fusion.1), channel_id=1, source_target_pairs={{0,8},{2,10},{4,12},{6,14},{8,0},{10,2},{12,4},{14,6},{16,24},{18,... | collective-permute-start | bytes 18440 | tf_op jit(solution)/shard_map/ppermute | solution.py:768
  191.9 6.8 %collective-permute-start.33 = (f32[2,768]{1,0:T(2,128)S(1)}, f32[2,768]{1,0:T(2,128)S(1)}, u32[]{:S(2)}, u32[]{:S(2)}) collective-permute-start(f32[2,768]{1,0:T(2,128)S(1)} %add_add_fusion.1), channel_id=1, source_target_pairs={{0,16},{2,18},{4,20},{6,22},{8,24},{10,26},{12,28},{14,30},{16,0},... | collective-permute-start | bytes 18440 | tf_op jit(solution)/shard_map/ppermute | solution.py:768
  194.2 5.5 %collective-permute-start.34 = (f32[2,768]{1,0:T(2,128)S(1)}, f32[2,768]{1,0:T(2,128)S(1)}, u32[]{:S(2)}, u32[]{:S(2)}) collective-permute-start(f32[2,768]{1,0:T(2,128)S(1)} %add_add_fusion.1), channel_id=1, source_target_pairs={{0,24},{2,26},{4,28},{6,30},{8,16},{10,18},{12,20},{14,22},{16,8},... | collective-permute-start | bytes 18440 | tf_op jit(solution)/shard_map/ppermute | solution.py:768
  197.0 6.5 %collective-permute-start.37 = (bf16[48,1152]{1,0:T(8,128)(2,1)S(1)}, bf16[48,1152]{1,0:T(8,128)(2,1)S(1)}, u32[]{:S(2)}, u32[]{:S(2)}) collective-permute-start(bf16[48,1152]{1,0:T(8,128)(2,1)S(1)} %get-tuple-element.319), channel_id=1, source_target_pairs={{0,24},{2,26},{4,28},{6,30},{8,16},{10,18},{12,20},{14,22},{16,8},... | collective-permute-start | bytes 331784 | tf_op jit(solution)/shard_map/ppermute | solution.py:768
  (27 other events, 124.2 us)

commit v2 on v1

--- a/solution.py
+++ b/solution.py
@@ -132,14 +132,16 @@
 
 
 def prepare_kernel(
-    items, dp, me_ref, lens_ref, gain_ref, x_hbm, cot_hbm, na_ref, nat_ref, eb_ref, ebt_ref, x, cot, turn, sems
+    items, dp, me_ref, lens_ref, gain_hbm, x_hbm, cot_hbm, na_ref, nat_ref, eb_ref, ebt_ref, gain_ref, x, cot, turn, sems
 ):
     arrive = Copies(sems)
+    gain_in = arrive.start(gain_hbm, gain_ref)
     blocks = row_blocks(x.shape[0])
     inputs = [
         (arrive.start(x_hbm.at[own, :], x.at[own, :]), arrive.start(cot_hbm.at[own, :], cot.at[own, :]))
         for own in blocks
     ]
+    gain_in.wait()
     for own, (x_in, cot_in) in zip(blocks, inputs):
         x_in.wait()
         rows = x[own, :].astype(F32)
@@ -148,7 +150,7 @@
         na_ref[own, :] = normed
         store_transposed(normed, turn.at[0], nat_ref.at[:, own], me_ref, dp)
         cot_in.wait()
-        valid = row_is_valid(me_ref, lens_ref, items, own.start)
+        valid = row_is_valid(me_ref, lens_ref, items, own.start, own.stop - own.start)
         e = jnp.where(valid, cot[own, :].astype(F32), 0.0).astype(BF16)
         eb_ref[own, :] = e
         store_transposed(e, turn.at[1], ebt_ref.at[:, own], me_ref, dp)
@@ -158,19 +160,20 @@
     count, width = x.shape
     return pl.pallas_call(
         functools.partial(prepare_kernel, count // SLOTS, dp),
-        in_specs=[SCALAR, SCALAR, CHIP, ANY, ANY],
+        in_specs=[SCALAR, SCALAR, ANY, ANY, ANY],
         out_specs=[CHIP] * 4,
         out_shape=[vmem((count, width), BF16), vmem((width, count), BF16)] * 2,
         scratch_shapes=[
+            pltpu.VMEM((width,), F32),
             pltpu.VMEM((count, width), BF16),
             pltpu.VMEM((count, width), BF16),
             pltpu.VMEM((2, width, ROWS), BF16),
-            pltpu.SemaphoreType.DMA((2 * (count // ROWS),)),
+            pltpu.SemaphoreType.DMA((1 + 2 * (count // ROWS),)),
         ],
-        compiler_params=params(24),
+        compiler_params=params(14),
         cost_estimate=cost(10 * count * width, 12 * count * width),
         name="prepare",
-    )(me, lens, on_chip(gain), *off_chip((x, cot)))
+    )(me, lens, *off_chip((gain, x, cot)))
 
 
 def attention_tasks(items):
@@ -238,9 +241,9 @@
 
 
 def front_kernel(
-    dp, me_ref, gain_ref, na_ref, cos_hbm, sin_hbm, w_hbm, wo_hbm, x_hbm,
+    dp, me_ref, gain_hbm, na_ref, cos_hbm, sin_hbm, w_hbm, wo_hbm, x_hbm,
     q_hbm, k_hbm, v_hbm, h1_hbm, o_ref, lse_ref, nf_ref, nft_ref,
-    q_ref, k_ref, v_ref, h1_ref, acc, weights, wo, x, cosine, sine, turn, sems, out_sems,
+    gain_ref, q_ref, k_ref, v_ref, h1_ref, acc, weights, wo, x, cosine, sine, turn, sems, out_sems,
 ):
     arrive = Copies(sems)
     leaving = ((q_ref, q_hbm), (k_ref, k_hbm), (v_ref, v_hbm))
@@ -253,7 +256,7 @@
             source = w_hbm[p // half][j].at[:, (p % half) * PAIR : (p % half + 1) * PAIR]
             early.append(arrive.start(source, weights.at[:, (3 * p + j) * PAIR : (3 * p + j + 1) * PAIR]))
     late = [arrive.start(w, wo.at[i * cols : (i + 1) * cols, :]) for i, w in enumerate(wo_hbm)]
-    late.append(arrive.start(x_hbm, x))
+    late += [arrive.start(x_hbm, x), arrive.start(gain_hbm, gain_ref)]
     for c in early:
         c.wait()
 
@@ -301,7 +304,7 @@
     area = 2 * half * items * 2 * SLOTS * SLOTS
     return pl.pallas_call(
         functools.partial(front_kernel, dp),
-        in_specs=[SCALAR, CHIP, CHIP, ANY, ANY, [[ANY] * 3] * 2, [ANY] * 2, ANY],
+        in_specs=[SCALAR, ANY, CHIP, ANY, ANY, [[ANY] * 3] * 2, [ANY] * 2, ANY],
         out_specs=[ANY] * 4 + [CHIP] * 4,
         out_shape=[hbm((count, width), BF16)] * 3
         + [
@@ -309,7 +312,8 @@
             vmem((2 * half, 2 * items, SLOTS), F32),
             vmem((count, width), BF16), vmem((width, count), BF16),
         ],
-        scratch_shapes=[pltpu.VMEM((count, width), BF16)] * 3
+        scratch_shapes=[pltpu.VMEM((width,), F32)]
+        + [pltpu.VMEM((count, width), BF16)] * 3
         + [
             pltpu.VMEM((count, width), F32),
             pltpu.VMEM((items, PAIR, SLOTS), F32),
@@ -319,13 +323,13 @@
             pltpu.VMEM((count, PAIR), F32),
             pltpu.VMEM((count, PAIR), F32),
             pltpu.VMEM((width, ROWS), BF16),
-            pltpu.SemaphoreType.DMA((6 * half + 8,)),
+            pltpu.SemaphoreType.DMA((6 * half + 6,)),
             pltpu.SemaphoreType.DMA((6 * half + count // ROWS,)),
         ],
-        compiler_params=params(34),
+        compiler_params=params(28),
         cost_estimate=cost(8 * count * width * width + 8 * area * PAIR, 24 * count * width, area),
         name="front",
-    )(me, *on_chip((gain, na)), *off_chip(tables), [list(off_chip(w[0])), list(w[1])], [off_chip(wo[0]), wo[1]], off_chip(x))
+    )(me, off_chip(gain), on_chip(na), *off_chip(tables), [list(off_chip(w[0])), list(w[1])], [off_chip(wo[0]), wo[1]], off_chip(x))
 
 
 def attention_back_kernel(
@@ -333,7 +337,7 @@
 ):
     q_ref, k_ref, v_ref, dq_t, dk_acc, dv_acc, cosine, sine, right, sems, row_sems = rest[-11:]
     if final:
-        recv_ref, dq_ref, dk_ref, dv_ref, *outs = rest[:-11]
+        recv_ref, here_ref, there_ref, dq_ref, dk_ref, dv_ref, *outs = rest[:-11]
     else:
         dq_ref, dk_ref, dv_ref, out_ref = rest[:-11]
     count, cols = dq_ref.shape
@@ -349,6 +353,15 @@
     arrive.wait()
     side = lax.broadcasted_iota(jnp.int32, (SLOTS, PAIR), 1) // HEAD
     quarter = nat_ref.shape[0] // 4
+
+    if final:
+        send_a, keep_a, send_b, keep_b = outs
+        for place in range(4):
+            own = slice(place * quarter, place * quarter + quarter)
+            values = (here_ref[own, :].astype(F32) + there_ref[own, :].astype(F32)).astype(BF16)
+            b0, b1 = place // 2, place % 2
+            (send_a if b0 else keep_a)[b1, :, 3 * cols :] = values[: quarter // 2]
+            (send_b if b1 else keep_b)[b0, :, 3 * cols :] = values[quarter // 2 :]
 
     @pl.loop(0, cols // PAIR)
     def _(pair):
@@ -408,22 +421,26 @@
             own = slice(place * quarter, place * quarter + quarter)
             values = dot(nat_ref[own, :], right[...])
             if final:
-                outs[place][:, wide] = (values + recv_ref[own, wide].astype(F32)).astype(BF16)
+                send_a, keep_a, send_b, keep_b = outs
+                values = (values + recv_ref[own, wide].astype(F32)).astype(BF16)
+                b0, b1 = place // 2, place % 2
+                (send_a if b0 else keep_a)[b1, :, wide] = values[: quarter // 2]
+                (send_b if b1 else keep_b)[b0, :, wide] = values[quarter // 2 :]
             else:
                 out_ref[own, wide] = values.astype(BF16)
 
 
-def attention_back(q, k, v, d, lse, tables, nat, first, recv=None):
+def attention_back(q, k, v, d, lse, tables, nat, first, recv=()):
     count, width = q.shape
     cols = width // 2
     items, pairs = count // SLOTS, cols // PAIR
     area = pairs * items * 2 * SLOTS * SLOTS
-    final = recv is not None
+    final = bool(recv)
     args = [*on_chip((d, lse, nat)), *off_chip((*tables, q, k, v))]
     out_shape = [vmem((count, cols), BF16)] * 3
     if final:
-        args.append(on_chip(recv))
-        out_shape += [vmem((width // 4, 3 * cols), BF16)] * 4
+        args += on_chip(recv)
+        out_shape += [vmem((2, width // 8, 4 * cols), BF16)] * 4
     else:
         out_shape.append(vmem((width, 3 * cols), BF16))
     return pl.pallas_call(
@@ -436,36 +453,38 @@
         + [pltpu.VMEM((items, SLOTS, PAIR), F32)] * 2
         + [pltpu.VMEM((SLOTS, PAIR), F32)] * 2
         + [pltpu.VMEM((count, 3 * PAIR), BF16), pltpu.SemaphoreType.DMA((2,)), pltpu.SemaphoreType.DMA((3 * pairs,))],
-        compiler_params=params(28),
+        compiler_params=params(20),
         cost_estimate=cost(20 * area * PAIR + 6 * count * width * cols, 16 * count * cols, area),
         name="attention_back_final" if final else "attention_back_other",
     )(*args)
 
 
-def row_is_valid(me_ref, lens_ref, items, start):
-    row = start + lax.broadcasted_iota(jnp.int32, (ROWS, 1), 0)
+def row_is_valid(me_ref, lens_ref, items, start, size):
+    row = start + lax.broadcasted_iota(jnp.int32, (size, 1), 0)
     valid = row < 0
     for i in range(items):
         valid = valid | ((row >= i * SLOTS) & (row < i * SLOTS + lens_ref[me_ref[1] * items + i]))
     return valid
 
 
-def split_store(values, cols, total, b0, b1, outs):
+def split_store(values, cols, total, beside, b0, b1, outs):
     send_a, keep_a, send_b, keep_b = outs
     cut = total // 2
     if cols.start < cut:
-        part = values[:, : min(cols.stop, cut) - cols.start].astype(BF16)
-        (send_a if b0 else keep_a)[b1, :, cols.start : min(cols.stop, cut)] = part
+        stop = min(cols.stop, cut)
+        part = values[:, : stop - cols.start].astype(BF16)
+        (send_a if b0 else keep_a)[b1, :, beside + cols.start : beside + stop] = part
     if cols.stop > cut:
         start = max(cols.start, cut)
         part = values[:, start - cols.start :].astype(BF16)
-        (send_b if b1 else keep_b)[b0, :, start - cut : cols.stop - cut] = part
-
-
-def ffn_kernel(final, column, blocks, nf_ref, nft_ref, eb_ref, ebt_ref, wg_hbm, wu_hbm, wd_hbm, *rest):
+        (send_b if b1 else keep_b)[b0, :, beside + start - cut : beside + cols.stop - cut] = part
+
+
+def ffn_kernel(final, column, beside, blocks, nf_ref, nft_ref, eb_ref, ebt_ref, wg_hbm, wu_hbm, wd_hbm, *rest):
     wg, wu, wd, hid, in_sems, out_sems = rest[-6:]
     if final:
-        recv_ref, hid_hbm, dg_ref, du_ref, *outs = rest[:-6]
+        recv_ref, *rest = rest[:-6]
+        hid_hbm, dg_ref, du_ref, *outs = rest[-7:]
     else:
         hid_hbm, dg_ref, du_ref, out_ref = rest[:-6]
     width = nft_ref.shape[0]
@@ -490,7 +509,6 @@
         sig = 0.5 * jnp.tanh(0.5 * g) + 0.5
         silu = g * sig
         hid[own, :] = (silu * u).astype(BF16)
-        sent.start(hid.at[own, :], hid_hbm.at[own, :])
         du_ref[own, :] = (dh * silu).astype(BF16)
         dg_ref[own, :] = (dh * u * (sig + silu * (1.0 - sig))).astype(BF16)
 
@@ -502,18 +520,20 @@
         made = upcoming
     quarter = width // 4
     for place in range(4):
+        if place == 1:
+            sent.start(hid, hid_hbm)
         own = slice(place * quarter, place * quarter + quarter)
         grads = [dot(nft_ref[own, :], dg_ref[...]), dot(nft_ref[own, :], du_ref[...]), dot(ebt_ref[own, :], hid[...])]
         for j, values in enumerate(grads):
             cols = slice(j * CHUNK, (j + 1) * CHUNK)
             if final:
-                split_store(values + recv_ref[own, cols].astype(F32), cols, 3 * CHUNK, place // 2, place % 2, outs)
+                split_store(values + recv_ref[own, cols].astype(F32), cols, 3 * CHUNK, beside, place // 2, place % 2, outs)
             else:
                 out_ref[own, cols] = values.astype(BF16)
     sent.wait()
 
 
-def ffn(nf, nft, eb, ebt, wg, wu, wd, chunk, recv=None, spare=0):
+def ffn(nf, nft, eb, ebt, wg, wu, wd, chunk, recv=None, base=()):
     count, width = nf.shape
     final = recv is not None
     wide = 3 * CHUNK
@@ -524,15 +544,16 @@
     args = [*on_chip((nf, nft, eb, ebt)), *weights]
     out_shape = [hbm((count, CHUNK), BF16)] + [vmem((count, CHUNK), BF16)] * 2
     if final:
-        args.append(on_chip(recv))
-        out_shape += [vmem((2, width // 4, wide // 2 + spare), BF16)] * 4
+        args += [on_chip(recv), *on_chip(base)]
+        out_shape += [vmem((2, width // 4, wd.shape[0] // CHUNK * wide // 2), BF16)] * 4
     else:
         out_shape.append(vmem((width, wide), BF16))
     return pl.pallas_call(
-        functools.partial(ffn_kernel, final, chunk * CHUNK, blocks),
+        functools.partial(ffn_kernel, final, chunk * CHUNK, chunk * wide // 2, blocks),
         in_specs=[CHIP] * 4 + [ANY] * 3 + [CHIP] * (len(args) - 7),
         out_specs=[ANY] + [CHIP] * (len(out_shape) - 1),
         out_shape=out_shape,
+        input_output_aliases={8 + i: 3 + i for i in range(len(base))},
         scratch_shapes=[pltpu.VMEM((width, CHUNK), BF16)] * 2
         + [
             pltpu.VMEM((CHUNK, width), BF16),
@@ -540,7 +561,7 @@
             pltpu.SemaphoreType.DMA((3,)),
             pltpu.SemaphoreType.DMA((3,)),
         ],
-        compiler_params=params(24),
+        compiler_params=params(14),
         cost_estimate=cost(12 * count * width * CHUNK, 8 * count * width + 12 * width * CHUNK),
         name="ffn_final" if final else "ffn_other",
     )(*args)
@@ -555,8 +576,8 @@
 
 
 def ffn_back_kernel(
-    dp, me_ref, gain_ref, h1_hbm, eb_ref, o_ref, d_refs, wg_hbm, wu_hbm, wo_hbm,
-    dh1_ref, do_ref, dgain_ref, there_ref, here_ref, h1_ref, weights, wo, turn, abt, in_sems,
+    dp, me_ref, gain_hbm, h1_hbm, eb_ref, o_ref, d_refs, wg_hbm, wu_hbm, wo_hbm,
+    dh1_ref, do_ref, dgain_ref, there_ref, here_ref, gain_ref, h1_ref, weights, wo, turn, abt, in_sems,
 ):
     count, width = h1_ref.shape
     cols, half = wo_hbm[0].shape[0], wg_hbm[0].shape[1]
@@ -565,6 +586,7 @@
     wo_in = [arrive.start(w, wo.at[i * cols : (i + 1) * cols, :]) for i, w in enumerate(wo_hbm)]
     blocks = row_blocks(count)
     h1_in = [arrive.start(h1_hbm.at[own, :], h1_ref.at[own, :]) for own in blocks]
+    h1_in.append(arrive.start(gain_hbm, gain_ref))
     per = len(d_refs) // len(w_in)
 
     def product(i):
@@ -580,9 +602,10 @@
     dnf, gain_total = product(0), None
     for c in wo_in:
         c.wait()
+    for c in h1_in:
+        c.wait()
     for i, own in enumerate(blocks):
         upcoming = product(i + 1) if i + 1 < len(blocks) else None
-        h1_in[i].wait()
         d_rows, gain_part = norm_back_rows(h1_ref[own, :], dnf, gain_ref[...][None, :])
         gain_total = gain_part if gain_total is None else gain_total + gain_part
         back = eb_ref[own, :].astype(F32) + d_rows
@@ -605,7 +628,7 @@
     half, cols = wg[0].shape[1], wo[0].shape[0]
     return pl.pallas_call(
         functools.partial(ffn_back_kernel, dp),
-        in_specs=[SCALAR, CHIP, ANY, CHIP, CHIP, [CHIP] * len(d), [ANY] * 2, [ANY] * 2, [ANY] * 2],
+        in_specs=[SCALAR, ANY, ANY, CHIP, CHIP, [CHIP] * len(d), [ANY] * 2, [ANY] * 2, [ANY] * 2],
         out_specs=[CHIP] * 5,
         out_shape=[
             vmem((count, width), F32),
@@ -615,50 +638,26 @@
             vmem((width, cols), BF16),
         ],
         scratch_shapes=[
+            pltpu.VMEM((width,), F32),
             pltpu.VMEM((count, width), F32),
             pltpu.VMEM((4, width, half), BF16),
             pltpu.VMEM((2 * cols, width), BF16),
             pltpu.VMEM((width, ROWS), BF16),
             pltpu.VMEM((width, count), BF16),
-            pltpu.SemaphoreType.DMA((6 + count // ROWS,)),
+            pltpu.SemaphoreType.DMA((7 + count // ROWS,)),
         ],
-        compiler_params=params(26),
+        compiler_params=params(20),
         cost_estimate=cost(4 * count * width * (2 * half + 2 * cols), 20 * count * width + 8 * count * half),
         name="ffn_back",
     )(
-        me, on_chip(gain), off_chip(h1), *on_chip((eb, o)), list(on_chip(d)),
+        me, *off_chip((gain, h1)), *on_chip((eb, o)), list(on_chip(d)),
         [off_chip(wg[0]), wg[1]], [off_chip(wu[0]), wu[1]], [off_chip(wo[0]), wo[1]],
     )
 
 
-def join_kernel(here_ref, recv_ref, *rest):
-    outs = rest[4:8]
-    quarter, cut = here_ref.shape[0] // 4, here_ref.shape[1] // 2
-    spare = slice(outs[0].shape[2] - cut, outs[0].shape[2])
-    for place in range(4):
-        own = slice(place * quarter, place * quarter + quarter)
-        values = here_ref[own, :].astype(F32) + recv_ref[own, :].astype(F32)
-        b0, b1 = place // 2, place % 2
-        (outs[0] if b0 else outs[1])[b1, :, spare] = values[:, :cut].astype(BF16)
-        (outs[2] if b1 else outs[3])[b0, :, spare] = values[:, cut:].astype(BF16)
-
-
-def join(here, recv, pieces):
-    return pl.pallas_call(
-        join_kernel,
-        in_specs=[CHIP] * 2 + [CHIP] * 4,
-        out_specs=[CHIP] * 4,
-        out_shape=[vmem(p.shape, BF16) for p in pieces],
-        input_output_aliases={2 + i: i for i in range(4)},
-        compiler_params=params(16),
-        cost_estimate=cost(here.size, 6 * here.size),
-        name="join",
-    )(*on_chip((here, recv)), *on_chip(pieces))
-
-
 def finish_kernel(
-    items, me_ref, lens_ref, gain_ref, dh1_ref, d_refs, x_hbm, w_hbm, h1_hbm, wd_hbm, hid_hbm,
-    gin_hbm, out_hbm, dgain_ref, weights, x, gin, h1, wd, hid, out, in_sems, out_sems
+    items, me_ref, lens_ref, gain_hbm, dh1_ref, d_refs, x_hbm, w_hbm, h1_hbm, wd_hbm, hid_hbm,
+    gin_hbm, out_hbm, dgain_ref, gain_ref, weights, x, gin, h1, wd, hid, out, in_sems, out_sems
 ):
     arrive, sent = Copies(in_sems), Copies(out_sems)
     cols, per = w_hbm[0].shape[1], 3
@@ -666,7 +665,7 @@
         arrive.start(w, weights.at[i // per, :, (i % per) * cols : (i % per + 1) * cols]) for i, w in enumerate(w_hbm)
     ]
     blocks = row_blocks(x.shape[0])
-    x_in = [arrive.start(x_hbm.at[own, :], x.at[own, :]) for own in blocks]
+    x_in = [arrive.start(x_hbm.at[own, :], x.at[own, :]) for own in blocks] + [arrive.start(gain_hbm, gain_ref)]
     half, size = wd_hbm[0].shape[0], hid_hbm[0].shape[1]
     wd_in = [arrive.start(w, wd.at[i * half : (i + 1) * half, :]) for i, w in enumerate(wd_hbm)]
     row_in = [
@@ -695,11 +694,12 @@
         return dot(hid[blocks[i], :], wd[...])
 
     dna, gain_total, total = product(0), None, None
+    for c in x_in:
+        c.wait()
     for i, own in enumerate(blocks):
         upcoming = product(i + 1) if i + 1 < len(blocks) else None
         if i + 1 == len(blocks):
             total = down(0)
-        x_in[i].wait()
         d_rows, gain_part = norm_back_rows(x[own, :].astype(F32), dna, gain_ref[...][None, :])
         gain_total = gain_part if gain_total is None else gain_total + gain_part
         gin[own, :] = dh1_ref[own, :] + d_rows
@@ -709,7 +709,7 @@
     for i, own in enumerate(blocks):
         upcoming = down(i + 1) if i + 1 < len(blocks) else None
         total = total + h1[own, :]
-        out[own, :] = jnp.where(row_is_valid(me_ref, lens_ref, items, own.start), total, 0.0).astype(BF16)
+        out[own, :] = jnp.where(row_is_valid(me_ref, lens_ref, items, own.start, own.stop - own.start), total, 0.0).astype(BF16)
         sent.start(out.at[own, :], out_hbm.at[own, :])
         total = upcoming
     sent.wait()
@@ -721,10 +721,11 @@
     deep, mine, steps = cols * len(weights), len(weights) // 2, count // ROWS
     return pl.pallas_call(
         functools.partial(finish_kernel, count // SLOTS),
-        in_specs=[SCALAR, SCALAR, CHIP, CHIP, [CHIP] * len(grads), ANY, [ANY] * len(weights), ANY, [ANY] * 2, [ANY] * len(hid)],
+        in_specs=[SCALAR, SCALAR, ANY, CHIP, [CHIP] * len(grads), ANY, [ANY] * len(weights), ANY, [ANY] * 2, [ANY] * len(hid)],
         out_specs=[ANY, ANY, CHIP],
         out_shape=[hbm((count, width), F32), hbm((count, width), BF16), vmem((1, width), F32)],
         scratch_shapes=[
+            pltpu.VMEM((width,), F32),
             pltpu.VMEM((2, width, deep // 2), BF16),
             pltpu.VMEM((count, width), BF16),
             pltpu.VMEM((count, width), F32),
@@ -732,14 +733,14 @@
             pltpu.VMEM((2 * half, width), BF16),
             pltpu.VMEM((count, 2 * half), BF16),
             pltpu.VMEM((count, width), BF16),
-            pltpu.SemaphoreType.DMA((len(weights) + 2 + steps * (2 + len(hid)),)),
+            pltpu.SemaphoreType.DMA((len(weights) + 3 + steps * (2 + len(hid)),)),
             pltpu.SemaphoreType.DMA((2 * steps,)),
         ],
-        compiler_params=params(40),
+        compiler_params=params(36),
         cost_estimate=cost(2 * count * width * (deep + 2 * half), 16 * count * width + 2 * count * (deep + 2 * half)),
         name="finish",
     )(
-        me, lens, *on_chip((gain, dh1)), list(on_chip(grads)), off_chip(x),
+        me, lens, off_chip(gain), on_chip(dh1), list(on_chip(grads)), off_chip(x),
         [*off_chip(weights[:mine]), *weights[mine:]], off_chip(h1), [off_chip(wd[0]), wd[1]], list(off_chip(hid)),
     )
 
@@ -777,11 +778,12 @@
     _, quarter, cut = keep_a.shape
     next_a, next_b = pl.pallas_call(
         second_kernel,
+        in_specs=[CHIP] * 4,
         out_shape=[sds((quarter, cut), BF16)] * 2,
-        compiler_params=params(24),
+        compiler_params=params(8),
         cost_estimate=cost(quarter * cut * 2, quarter * cut * 12),
         name="second_sum",
-    )(keep_a, recv[0], keep_b, recv[1])
+    )(*on_chip((keep_a, recv[0], keep_b, recv[1])))
     return swap_dp(next_a, dp, 2), swap_dp(next_b, dp, 1)
 
 
@@ -793,60 +795,106 @@
     kept, sends = pl.pallas_call(
         third_kernel,
         out_shape=[sds((group, 2 * cut), F32), [sds((group, 2 * cut), BF16)] * (far - 1)],
-        compiler_params=params(24),
+        compiler_params=params(12),
         cost_estimate=cost(quarter * cut * 4, quarter * cut * 16),
         name="third_sum",
     )(keep_a, recv[0], last[0], keep_b, recv[1], last[1])
     return kept, tuple(swap_dp(send, dp, 4 * (z + 1)) for z, send in enumerate(sends))
 
 
-def direct_kernel(keep, recv_refs, keep_ref, send_refs):
+def third_rows_kernel(keep_a, recv_a, last_a, keep_b, recv_b, last_b, keep_ref, send_refs):
     group = keep_ref.shape[0]
+    inner = keep_a.shape[1] // group
     for z in range(len(send_refs) + 1):
-        own = slice(z * group, z * group + group)
-        total = keep[own, :].astype(F32)
-        for recv in recv_refs:
-            total = total + recv[own, :].astype(F32)
+        keep, recv, last = (keep_a, recv_a, last_a) if z < inner else (keep_b, recv_b, last_b)
+        own = slice(z % inner * group, z % inner * group + group)
+        total = keep[0, own, :].astype(F32) + recv[0, own, :].astype(F32) + last[own, :].astype(F32)
         if z:
             send_refs[z - 1][...] = total.astype(BF16)
         else:
             keep_ref[...] = total
 
 
-def direct_swaps(pieces, dp):
-    return tuple(swap_dp(piece, dp, relative) for piece, relative in zip(pieces[1:], (2, 1, 3)))
-
-
-def direct_far_swaps(keep, recv, dp):
-    quarter, cols = keep.shape
+def third_rows_swaps(pieces, recv, last, dp):
+    _, keep_a, _, keep_b = pieces
+    _, rows, cols = keep_a.shape
     far = dp // 4
-    group = quarter // far
+    group = 2 * rows // far
     kept, sends = pl.pallas_call(
-        direct_kernel,
+        third_rows_kernel,
+        in_specs=[CHIP] * 6,
         out_shape=[sds((group, cols), F32), [sds((group, cols), BF16)] * (far - 1)],
-        compiler_params=params(24),
-        cost_estimate=cost(quarter * cols * 4, quarter * cols * 10),
-        name="direct_sum",
-    )(keep, list(recv))
+        compiler_params=params(12),
+        cost_estimate=cost(rows * cols * 8, rows * cols * 20),
+        name="third_rows_sum",
+    )(*on_chip((keep_a, recv[0], last[0], keep_b, recv[1], last[1])))
     return kept, tuple(swap_dp(send, dp, 4 * (z + 1)) for z, send in enumerate(sends))
 
 
+def near_kernel(keep_a, recv_a, last_a, keep_b, recv_b, last_b, keep_ref, send_ref):
+    group, cut = keep_ref.shape[1], keep_a.shape[2]
+    for z in range(4):
+        own = slice(z * group, z * group + group)
+        for cols, keep, recv, last in (
+            (slice(0, cut), keep_a, recv_a, last_a),
+            (slice(cut, 2 * cut), keep_b, recv_b, last_b),
+        ):
+            total = keep[0, own, :].astype(F32) + recv[0, own, :].astype(F32) + last[own, :].astype(F32)
+            (send_ref if z % 2 else keep_ref)[z // 2, :, cols] = total.astype(BF16)
+
+
+def far_kernel(keep, recv, send_ref):
+    send_ref[...] = (keep[1].astype(F32) + recv[1].astype(F32)).astype(BF16)
+
+
+def near_swap(pieces, recv, last, dp):
+    _, keep_a, _, keep_b = pieces
+    _, quarter, cut = keep_a.shape
+    kept, send = pl.pallas_call(
+        near_kernel,
+        in_specs=[CHIP] * 6,
+        out_shape=[sds((2, quarter // 4, 2 * cut), BF16)] * 2,
+        compiler_params=params(12),
+        cost_estimate=cost(quarter * cut * 4, quarter * cut * 16),
+        name="near_sum",
+    )(*on_chip((keep_a, recv[0], last[0], keep_b, recv[1], last[1])))
+    return kept, swap_dp(send, dp, 4)
+
+
+def far_swap(kept, recv, dp):
+    send = pl.pallas_call(
+        far_kernel,
+        in_specs=[CHIP] * 2,
+        out_shape=sds(kept.shape[1:], BF16),
+        compiler_params=params(6),
+        cost_estimate=cost(kept.size, 4 * kept.size),
+        name="far_sum",
+    )(*on_chip((kept, recv)))
+    return swap_dp(send, dp, 8)
+
+
 def last_kernel(kept, far_refs, outs):
-    for p in range(kept.shape[1] // (3 * PAIR)):
-        for j, out in enumerate(outs):
-            own = slice((3 * p + j) * PAIR, (3 * p + j + 1) * PAIR)
-            total = kept[:, own]
-            for far in far_refs:
-                total = total + far[:, own].astype(F32)
-            out[:, p * PAIR : (p + 1) * PAIR] = total
+    *qkv, out = outs
+    cols = out.shape[1]
+
+    def total(own):
+        made = kept[:, own].astype(F32)
+        for far in far_refs:
+            made = made + far[:, own].astype(F32)
+        return made
+
+    for p in range(cols // PAIR):
+        for j, ref in enumerate(qkv):
+            ref[:, p * PAIR : (p + 1) * PAIR] = total(slice((3 * p + j) * PAIR, (3 * p + j + 1) * PAIR))
+    out[...] = total(slice(3 * cols, 4 * cols))
 
 
 def last_sum(kept, far):
     group, cols = kept.shape
     return pl.pallas_call(
         lambda kept, far_refs, *outs: last_kernel(kept, far_refs, outs),
-        out_shape=[sds((group, cols // 3), F32)] * 3,
-        compiler_params=params(16),
+        out_shape=[sds((group, cols // 4), F32)] * 4,
+        compiler_params=params(6),
         name="last_sum",
     )(kept, list(far))
 
@@ -881,13 +929,12 @@
     def other(array):
         return lax.ppermute(array, "mp", [(0, 1), (1, 0)])
 
-    wq, wk, wv, wo, wg, wu, wd = (
-        (w, other(w)) for w in (w_query, w_key, w_value, w_out, w_gate, w_up, w_down)
-    )
+    wq, wk, wv, wo = ((w, other(w)) for w in (w_query, w_key, w_value, w_out))
     tables = tuple(jnp.asarray(t) for t in position_tables(count))
 
     na, nat, eb, ebt = prepare(dp, me, lengths, tokens, cotangent, gain_a)
-    na, wq, wk, wv = fence((na, wq, wk, wv))
+    na, wq, wk, wv, w_gate, w_up, w_down = fence((na, wq, wk, wv, w_gate, w_up, w_down))
+    wg, wu, wd = ((w, other(w)) for w in (w_gate, w_up, w_down))
     nat, ebt = finish_transposed(nat, me, dp), finish_transposed(ebt, me, dp)
     q, k, v, h1, o, lse, nf, nft = front(
         dp, me, na, tables, gain_f, ((wq[0], wk[0], wv[0]), (wq[1], wk[1], wv[1])), wo, tokens
@@ -903,56 +950,54 @@
         made.append(rest)
         back.append(other(there))
     theirs = made
-    made, pieces, recv = [], [], []
+    made, piece = [], ()
     for c in range(chunks):
-        nf, here, theirs, made = fence((nf, back[c], theirs, made))
-        spare = w_out.shape[0] // 2 if c == chunks - 1 else 0
-        *rest, sa, ka, sb, kb = ffn(nf, nft, eb, ebt, wg[0], wu[0], wd[0], c, here, spare)
+        nf, here, theirs, made, piece = fence((nf, back[c], theirs, made, piece))
+        *rest, sa, ka, sb, kb = ffn(nf, nft, eb, ebt, wg[0], wu[0], wd[0], c, here, piece)
         made.append(rest)
-        pieces.append((sa, ka, sb, kb))
-        recv.append(first_swaps(pieces[-1], dp) if c < chunks - 1 else None)
-    h1, recv, made, theirs = fence((h1, recv[:-1], made, theirs))
-    last = [second_swaps(p, r, dp) for p, r in zip(pieces, recv)]
+        piece = (sa, ka, sb, kb)
+    h1, made, theirs, piece = fence((h1, made, theirs, piece))
+    recv = first_swaps(piece, dp)
     parts = made + theirs
     hid = [p[0] for p in parts]
     dh1, do, dgain_f, out_there, out_here = ffn_back(
         dp, me, h1, eb, gain_f, wg, wu, wo, o, [p[1] for p in parts] + [p[2] for p in parts]
     )
-    out_there, out_here, last, do = fence((out_there, out_here, last, do))
-    back_out = other(out_there)
-    third = [third_swaps(p, r, l, dp) for p, r, l in zip(pieces, recv, last)]
-    pieces[-1] = join(out_here, back_out, pieces[-1])
-    recv.append(first_swaps(pieces[-1], dp))
+    out_there, out_here, do = fence((out_there, out_here, do))
+    out_back = other(out_there)
     heads = w_query.shape[1] // PAIR
-    do, pieces = fence((do, pieces))
     *d1, qkv_there = attention_back(q, k, v, do, lse, tables, nat, heads)
-    qkv_there, d1, recv, third, do = fence((qkv_there, d1, recv, third, do))
-    back_qkv = other(qkv_there)
-    last_last = second_swaps(pieces[-1], recv[-1], dp)
-    *d0, keep_q, s1, s2, s3 = attention_back(q, k, v, do, lse, tables, nat, 0, back_qkv)
-    d0, s1, s2, s3, last_last = fence((d0, s1, s2, s3, last_last))
-    recv_q = direct_swaps((keep_q, s1, s2, s3), dp)
-    third.append(third_swaps(pieces[-1], recv[-1], last_last, dp))
+    qkv_there, out_back, d1, recv, do = fence((qkv_there, out_back, d1, recv, do))
+    qkv_back = other(qkv_there)
+    last = second_swaps(piece, recv, dp)
+    *d0, sa, ka, sb, kb = attention_back(q, k, v, do, lse, tables, nat, 0, (qkv_back, out_here, out_back))
+    q_piece = (sa, ka, sb, kb)
+    d0, q_piece, last = fence((d0, q_piece, last))
+    two_steps = dp == 16
+    recv_q = first_swaps(q_piece, dp)
+    kept, near = (near_swap if two_steps else third_swaps)(piece, recv, last, dp)
     grad_input, output, dgain_a = finish(
         me, lengths, tokens, dh1, gain_a, (wq[0], wk[0], wv[0], wq[1], wk[1], wv[1]), (*d0, *d1), h1, wd, hid
     )
-    dgain_a, recv_q, third = fence((dgain_a, recv_q, third))
-    kept_q, far_q = direct_far_swaps(keep_q, recv_q, dp)
+    dgain_a, recv_q, near = fence((dgain_a, recv_q, near))
+    far = far_swap(kept, near, dp) if two_steps else None
+    last_q = second_swaps(q_piece, recv_q, dp)
     gains = jnp.concatenate([dgain_a, dgain_f], 0)
-    gains = gains + other(gains)
-    gains = swap_sum(gains, dp, (1, 2))
-    gains = swap_sum(gains, dp, [1 << i for i in range(2, dp.bit_length() - 1)])
-    gq, gk, gv = last_sum(kept_q, far_q)
-    summed = [total_of(*t) for t in third]
-    wide = 3 * CHUNK
-    ffn_pieces, out_cols = [], []
-    for p in summed:
-        cut = p.shape[1] // 2
-        ffn_pieces.append(jnp.concatenate([p[:, : wide // 2], p[:, cut : cut + wide // 2]], 1))
-        if cut > wide // 2:
-            out_cols = [p[:, wide // 2 : cut], p[:, cut + wide // 2 :]]
-    out_piece = jnp.concatenate(out_cols, 1)
-
+    gains = swap_sum(gains + other(gains), dp, (1,))
+    gains, last_q = fence((gains, last_q))
+    kept_q, far_q = third_rows_swaps(q_piece, recv_q, last_q, dp)
+    gains = swap_sum(gains, dp, (2,))
+    gains, first_q = fence((gains, far_q[0]))
+    far_q = (first_q, *far_q[1:])
+    for bit in range(2, dp.bit_length() - 1):
+        gains = swap_sum(gains, dp, (1 << bit,))
+    total = total_of(kept[0].astype(F32), (near[0], far)) if two_steps else total_of(kept, near)
+    gq, gk, gv, out_piece = last_sum(kept_q, far_q)
+    side, wide = total.shape[1] // 2, 3 * CHUNK // 2
+    ffn_pieces = [
+        jnp.concatenate([total[:, c * wide : (c + 1) * wide], total[:, side + c * wide : side + (c + 1) * wide]], 1)
+        for c in range(chunks)
+    ]
     g_gate, g_up, g_down = (
         jnp.concatenate([p[:, i * CHUNK : (i + 1) * CHUNK] for p in ffn_pieces], 1) for i in range(3)
     )

time: 208 us -> 180 us (0.87)
  starting transfers between devices: 37.2 us -> 24.2 us
  local copies, waits for them, and re-layouts: 9.53 us -> 3.47 us
  Pallas kernels: 131 us -> 125 us
    ppermute x26 -> x17, starting transfers between devices: 34.4 us -> 21.3 us  [swap_dp(): return lax.ppermute(array, 'dp', [(i, i ^ relative) for i in range(dp)])]
    pallas_call x1, Pallas kernels: 22 us -> 15.7 us  [ffn_back(): pl.pallas_call(functools.partial(ffn_back_kernel, dp), in_specs=[SCALAR,...]
    unnamed x42 -> x28, local copies, waits for them, and re-layouts: 8.63 us -> 2.78 us
    pallas_call x11 -> x10, Pallas kernels: 58.5 us -> 56.7 us  [the longest x4 32.2 us: ffn(): pl.pallas_call(functools.partial(ffn_kernel, final, chunk * CHUNK, chunk...]
    ppermute x26 -> x17, waiting for transfers between devices: 18.6 us -> 18.8 us  [swap_dp(): return lax.ppermute(array, 'dp', [(i, i ^ relative) for i in range(dp)])]
  transfers between devices with their start and end apart: 38 -> 29, of which waited for: 13 -> 6; matrix products, arithmetic and copies ran while one was open for 1% -> 1% of each run, Pallas kernels for 59% -> 61%
where the time goes in v2:
time: 180 us; the launch traced here: 177 us
  Pallas kernels  125 us (69%)
  starting transfers between devices  24.2 us (13%)
  waiting for transfers between devices  21.4 us (12%)
  local copies, waits for them, and re-layouts  3.47 us (2%)
    pallas_call x2, Pallas kernels, attention_back(): pl.pallas_call(functools.partial(attention_back_kernel, final, first), in...  32.6 us
    pallas_call x4, Pallas kernels, ffn(): pl.pallas_call(functools.partial(ffn_kernel, final, chunk * CHUNK, chunk...  32.2 us
    pallas_call x1, Pallas kernels, front(): pl.pallas_call(functools.partial(front_kernel, dp), in_specs=[SCALAR, ANY...  23.4 us
    ppermute x17, starting transfers between devices, swap_dp(): return lax.ppermute(array, 'dp', [(i, i ^ relative) for i in range(dp)])  21.3 us
    ppermute x17, waiting for transfers between devices, swap_dp(): return lax.ppermute(array, 'dp', [(i, i ^ relative) for i in range(dp)])  18.8 us
    pallas_call x1, Pallas kernels, ffn_back(): pl.pallas_call(functools.partial(ffn_back_kernel, dp), in_specs=[SCALAR,...  15.7 us
    pallas_call x1, Pallas kernels, finish(): pl.pallas_call(functools.partial(finish_kernel, count // SLOTS), in_specs...  15 us
    pallas_call x1, Pallas kernels, prepare(): pl.pallas_call(functools.partial(prepare_kernel, count // SLOTS, dp), in_...  4.1 us
  transfers between devices with their start and end apart: 29, of which 6 were waited for; matrix products, arithmetic and copies ran while one was open for 1% of the time, Pallas kernels for 61%

profile of v2, /device:TPU:0, one launch (start us, length us, event | category | flops | bytes accessed | tf_op | source)
XLA Modules:
  0.0 177.0 jit_solution(1746368693889471847)
XLA Ops:
  1.8 0.7 copy-done
  2.5 4.1 %prepare.1 = (bf16[1152,768]{1,0:T(8,128)(2,1)S(1)}, bf16[768,1152]{1,0:T(8,128)(2,1)S(1)}, bf16[1152,768]{1,0:T(8,128)(2,1)S(1)}, bf16[768,1152]{1,0:T(8,128)(2,1)S(1)}) custom-call(s32[2]{0:T(128)S(1)} %pad_add_fusion.me_ref, s32[4]{0:T(128)S(1)} %copy-done, f32[768]{0:T(1024)} %gain_hbm.7, bf16[1152,768]{1,0:T(8,128)(2,1)} %x_hbm.5, bf16[1152,768]{1,0:T(8,128)(2,1)} %cot_hbm.1), custom_call_target="tpu_custom_call" | custom-call | flops 8847360 | bytes 10616832 | tf_op jit(solution)/shard_map/prepare/pallas_call | solution.py:161
  7.6 23.4 %front.1 = (bf16[1152,768]{1,0:T(8,128)(2,1)}, bf16[1152,768]{1,0:T(8,128)(2,1)}, bf16[1152,768]{1,0:T(8,128)(2,1)}, f32[1152,768]{1,0:T(8,128)}, bf16[1152,768]...) custom-call(s32[2]{0:T(128)S(1)} %pad_add_fusion.me_ref, ...), custom_call_target="tpu_custom_call" | custom-call | flops 13589544960 | bytes 21233664 | tf_op jit(solution)/shard_map/front/pallas_call | solution.py:305
  31.1 7.4 %ffn_other.2 = (bf16[1152,512]{1,0:T(8,128)(2,1)}, bf16[1152,512]{1,0:T(8,128)(2,1)S(1)}, bf16[1152,512]{1,0:T(8,128)(2,1)S(1)}, bf16[768,1536]{1,0:T(8,128)(2,1)S(1)}) custom-call(bf16[1152,768]{1,0:T(8,128)(2,1)S(1)} %get-tuple-element.207.nf_ref, bf16[768,1152]{1,0:T(8,128)(2,1)S(1)} %get-tuple-element.171.nft_ref, ...), custom_call_target="tpu_custom_call" | custom-call | flops 5435817984 | bytes 11796480 | tf_op jit(solution)/shard_map/ffn_other/pallas_call | solution.py:551
  38.7 7.9 %ffn_other.3 = (bf16[1152,512]{1,0:T(8,128)(2,1)}, bf16[1152,512]{1,0:T(8,128)(2,1)S(1)}, bf16[1152,512]{1,0:T(8,128)(2,1)S(1)}, bf16[768,1536]{1,0:T(8,128)(2,1)S(1)}) custom-call(bf16[1152,768]{1,0:T(8,128)(2,1)S(1)} %get-tuple-element.207.nf_ref, bf16[768,1152]{1,0:T(8,128)(2,1)S(1)} %get-tuple-element.171.nft_ref, ...), custom_call_target="tpu_custom_call" | custom-call | flops 5435817984 | bytes 11796480 | tf_op jit(solution)/shard_map/ffn_other/pallas_call | solution.py:551
  46.7 1.0 copy-done.6
  47.7 1.0 copy-done.8
  49.2 8.2 %ffn_final.2 = (bf16[1152,512]{1,0:T(8,128)(2,1)}, bf16[1152,512]{1,0:T(8,128)(2,1)S(1)}, bf16[1152,512]{1,0:T(8,128)(2,1)S(1)}, bf16[2,192,1536]{2,1,0:T(8,128)...) custom-call(bf16[1152,768]{1,0:T(8,128)(2,1)S(1)} %get-tuple-element, ...), custom_call_target="tpu_custom_call" | custom-call | flops 5435817984 | bytes 11796480 | tf_op jit(solution)/shard_map/ffn_final/pallas_call | solution.py:551
  57.5 8.6 %ffn_final.3 = (bf16[1152,512]{1,0:T(8,128)(2,1)}, bf16[1152,512]{1,0:T(8,128)(2,1)S(1)}, bf16[1152,512]{1,0:T(8,128)(2,1)S(1)}, bf16[2,192,1536]{2,1,0:T(8,128)...) custom-call(bf16[1152,768]{1,0:T(8,128)(2,1)S(1)} %get-tuple-element, ...), custom_call_target="tpu_custom_call", output_to_operand_aliasing={{3}: (8, {}), {4}: (9, {}), {5}: (10, {}), {6}: (11, {})} | custom-call | flops 5435817984 | bytes 11796480 | tf_op jit(solution)/shard_map/ffn_final/pallas_call | solution.py:551
  66.0 2.6 %collective-permute-start.10 = (bf16[2,192,1536]{2,1,0:T(8,128)(2,1)S(1)}, bf16[2,192,1536]{2,1,0:T(8,128)(2,1)S(1)}, u32[]{:S(2)}, u32[]{:S(2)}) collective-permute-start(bf16[2,192,1536]{2,1,0:T(8,128)(2,1)S(1)} %get-tuple-element.251), channel_id=1, source_target_pairs={{0,2},{2,0},{4,6},{6,4},{8,10},{10,8},{12,14},{14,12},{16,18},{18,... | collective-permute-start | bytes 3538952 | tf_op jit(solution)/shard_map/ppermute | solution.py:769
  68.7 1.5 collective-permute-start.11
  70.2 15.7 %ffn_back.1 = (f32[1152,768]{1,0:T(8,128)S(1)}, bf16[1152,768]{1,0:T(8,128)(2,1)S(1)}, f32[1,768]{1,0:T(1,128)S(1)}, bf16[768,384]{1,0:T(8,128)(2,1)S(1)}, bf16[768,384]{1,0:T(8,128)(2,1)S(1)}) custom-call(s32[2]{0:T(128)S(1)} %pad_add_fusion.me_ref, f32[768]{0:T(1024)} %gain_hbm.6, f32[1152,768]{1,0:T(8,128)} %get-tuple-element.226.h1_hbm, ...), custom_call_target="tpu_custom_call" | custom-call | flops 9965666304 | bytes 27131904 | tf_op jit(solution)/shard_map/ffn_back/pallas_call | solution.py:629
  86.0 16.9 %attention_back_other.1 = (bf16[1152,384]{1,0:T(8,128)(2,1)S(1)}, bf16[1152,384]{1,0:T(8,128)(2,1)S(1)}, bf16[1152,384]{1,0:T(8,128)(2,1)S(1)}, bf16[768,1152]{1,0:T(8,128)(2,1)S(1)}) custom-call(bf16[1152,768]{1,0:T(8,128)(2,1)S(1)} %get-tuple-element.253.d_ref, f32[6,4,576]{2,1,0:T(4,128)S(1)} %get-tuple-element.241.lse_ref, ...), custom_call_target="tpu_custom_call" | custom-call | flops 12230590464 | bytes 7077888 | tf_op jit(solution)/shard_map/attention_back_other/pallas_call | solution.py:446
  104.1 2.6 %collective-permute-done.12.rest_0_ = bf16[768,1152]{1,0:T(8,128)(2,1)S(1)} collective-permute-done((bf16[768,1152]{1,0:T(8,128)(2,1)S(1)}, bf16[768,1152]{1,0:T(8,128)(2,1)S(1)}, u32[]{:S(2)}, u32[]{:S(2)}) %collective-permute-start.12) | collective-permute-done | bytes 1769504 | tf_op jit(solution)/shard_map/ppermute | solution.py:930
  106.7 15.6 %attention_back_final.1 = (bf16[1152,384]{1,0:T(8,128)(2,1)S(1)}, bf16[1152,384]{1,0:T(8,128)(2,1)S(1)}, bf16[1152,384]{1,0:T(8,128)(2,1)S(1)}, bf16[2,96,1536]{...) custom-call(bf16[1152,768]{1,0:T(8,128)(2,1)S(1)} %get-tuple-element, ...), custom_call_target="tpu_custom_call" | custom-call | flops 12230590464 | bytes 7077888 | tf_op jit(solution)/shard_map/attention_back_final/pallas_call | solution.py:446
  122.4 0.6 collective-permute-start.15
  123.6 2.0 %collective-permute-start.17 = (bf16[2,48,3072]{2,1,0:T(8,128)(2,1)S(1)}, bf16[2,48,3072]{2,1,0:T(8,128)(2,1)S(1)}, u32[]{:S(2)}, u32[]{:S(2)}) collective-permute-start(bf16[2,48,3072]{2,1,0:T(8,128)(2,1)S(1)} %get-tuple-element.287), channel_id=1, source_target_pairs={{0,8},{2,10},{4,12},{6,14},{8,0},{10,2},{12,4},{14,6},{16,24},{18,... | collective-permute-start | bytes 1769480 | tf_op jit(solution)/shard_map/ppermute | solution.py:769
  125.6 15.0 %finish.1 = (f32[1152,768]{1,0:T(8,128)}, bf16[1152,768]{1,0:T(8,128)(2,1)}, f32[1,768]{1,0:T(1,128)S(1)}) custom-call(s32[2]{0:T(128)S(1)} %pad_add_fusion.me_ref, s32[4]{0:T(128)S(1)} %copy-done.1, f32[768]{0:T(1024)} %gain_hbm.7, f32[1152,768]{1,0:T(8,128)S(1)} %copy-done.3, bf16[1152,384]{1,0:T(8,128)(2,1)S(1)} %get-tuple-element.270.d_refs_0_, ...), custom_call_target="tpu_custom_call" | custom-call | flops 7700742144 | bytes 24182784 | tf_op jit(solution)/shard_map/finish/pallas_call | solution.py:722
  140.8 2.7 %collective-permute-start.28 = (bf16[48,3072]{1,0:T(8,128)(2,1)S(1)}, bf16[48,3072]{1,0:T(8,128)(2,1)S(1)}, u32[]{:S(2)}, u32[]{:S(2)}) collective-permute-start(bf16[48,3072]{1,0:T(8,128)(2,1)S(1)} %far_sum.1), channel_id=1, source_target_pairs={{0,16},{2,18},{4,20},{6,22},{8,24},{10,26},{12,28},{14,30},{16,0},... | collective-permute-start | bytes 884744 | tf_op jit(solution)/shard_map/ppermute | solution.py:769
  143.5 1.5 collective-permute-start.19
  145.2 1.6 collective-permute-start.20
  147.3 10.0 %collective-permute-done.28 = bf16[48,3072]{1,0:T(8,128)(2,1)S(1)} collective-permute-done((bf16[48,3072]{1,0:T(8,128)(2,1)S(1)}, bf16[48,3072]{1,0:T(8,128)(2,1)S(1)}, u32[]{:S(2)}, u32[]{:S(2)}) %collective-permute-start.28) | collective-permute-done | bytes 294944 | tf_op jit(solution)/shard_map/ppermute | solution.py:769
  157.5 1.6 collective-permute-start.22
  159.5 3.2 %collective-permute-start.26 = (bf16[48,1536]{1,0:T(8,128)(2,1)S(1)}, bf16[48,1536]{1,0:T(8,128)(2,1)S(1)}, u32[]{:S(2)}, u32[]{:S(2)}) collective-permute-start(bf16[48,1536]{1,0:T(8,128)(2,1)S(1)} %get-tuple-element.303), channel_id=1, source_target_pairs={{0,16},{2,18},{4,20},{6,22},{8,24},{10,26},{12,28},{14,30},{16,0},... | collective-permute-start | bytes 442376 | tf_op jit(solution)/shard_map/ppermute | solution.py:769
  162.7 1.2 collective-permute-start.27
  163.9 3.3 %collective-permute-done.23.far_refs_0_ = bf16[48,1536]{1,0:T(8,128)(2,1)S(1)} collective-permute-done((bf16[48,1536]{1,0:T(8,128)(2,1)S(1)}, bf16[48,1536]{1,0:T(8,128)(2,1)S(1)}, u32[]{:S(2)}, u32[]{:S(2)}) %collective-permute-start.23) | collective-permute-done | bytes 147488 | tf_op jit(solution)/shard_map/ppermute | solution.py:769
  167.2 0.8 pad_maximum_fusion.1
  168.0 3.5 %collective-permute-done.24 = f32[2,768]{1,0:T(2,128)S(1)} collective-permute-done((f32[2,768]{1,0:T(2,128)S(1)}, f32[2,768]{1,0:T(2,128)S(1)}, u32[]{:S(2)}, u32[]{:S(2)}) %collective-permute-start.24) | collective-permute-done | bytes 6176 | tf_op jit(solution)/shard_map/ppermute | solution.py:769
  171.4 1.1 collective-permute-start.25
  172.6 0.7 fusion
  173.8 0.7 last_sum.1
  174.6 1.4 collective-permute-done.25
  (83 shorter events, 7.2 us)
Async XLA Ops:
  0.6 6.0 %collective-permute-start = (bf16[768,384]{1,0:T(8,128)(2,1)}, bf16[768,384]{1,0:T(8,128)(2,1)S(1)}, u32[]{:S(2)}, u32[]{:S(2)}) collective-permute-start(bf16[768,384]{1,0:T(8,128)(2,1)} %w_hbm_0_), channel_id=1, source_target_pairs={{0,1},{1,0},{2,3},{3,2},{4,5},{5,4},{6,7},{7,6},{8,9},{9,8},{10,11... | collective-permute-start | bytes 1769480 | tf_op jit(solution)/shard_map/ppermute | solution.py:930
  1.2 5.4 %collective-permute-start.1 = (bf16[768,384]{1,0:T(8,128)(2,1)}, bf16[768,384]{1,0:T(8,128)(2,1)S(1)}, u32[]{:S(2)}, u32[]{:S(2)}) collective-permute-start(bf16[768,384]{1,0:T(8,128)(2,1)} %w_hbm_1_), channel_id=1, source_target_pairs={{0,1},{1,0},{2,3},{3,2},{4,5},{5,4},{6,7},{7,6},{8,9},{9,8},{10,11... | collective-permute-start | bytes 1769480 | tf_op jit(solution)/shard_map/ppermute | solution.py:930
  1.2 5.4 %collective-permute-start.2 = (bf16[768,384]{1,0:T(8,128)(2,1)}, bf16[768,384]{1,0:T(8,128)(2,1)S(1)}, u32[]{:S(2)}, u32[]{:S(2)}) collective-permute-start(bf16[768,384]{1,0:T(8,128)(2,1)} %w_hbm_2_), channel_id=1, source_target_pairs={{0,1},{1,0},{2,3},{3,2},{4,5},{5,4},{6,7},{7,6},{8,9},{9,8},{10,11... | collective-permute-start | bytes 1769480 | tf_op jit(solution)/shard_map/ppermute | solution.py:930
  1.7 6.0 %collective-permute-start.3 = (bf16[384,768]{1,0:T(8,128)(2,1)}, bf16[384,768]{1,0:T(8,128)(2,1)S(1)}, u32[]{:S(2)}, u32[]{:S(2)}) collective-permute-start(bf16[384,768]{1,0:T(8,128)(2,1)} %wo_hbm_0_.3), channel_id=1, source_target_pairs={{0,1},{1,0},{2,3},{3,2},{4,5},{5,4},{6,7},{7,6},{8,9},{9,8},{10,11... | collective-permute-start | bytes 1769480 | tf_op jit(solution)/shard_map/ppermute | solution.py:930
  6.6 24.4 %collective-permute-start.4 = (bf16[768,1024]{1,0:T(8,128)(2,1)S(1)}, bf16[768,1024]{1,0:T(8,128)(2,1)S(1)}, u32[]{:S(2)}, u32[]{:S(2)}) collective-permute-start(bf16[768,1024]{1,0:T(8,128)(2,1)S(1)} %copy-done.12), channel_id=1, source_target_pairs={{0,1},{1,0},{2,3},{3,2},{4,5},{5,4},{6,7},{7,6},{8,9},{9,8},{10,11... | collective-permute-start | bytes 4718600 | tf_op jit(solution)/shard_map/ppermute | solution.py:930
  7.1 24.0 %collective-permute-start.5 = (bf16[768,1024]{1,0:T(8,128)(2,1)S(1)}, bf16[768,1024]{1,0:T(8,128)(2,1)S(1)}, u32[]{:S(2)}, u32[]{:S(2)}) collective-permute-start(bf16[768,1024]{1,0:T(8,128)(2,1)S(1)} %copy-done.13), channel_id=1, source_target_pairs={{0,1},{1,0},{2,3},{3,2},{4,5},{5,4},{6,7},{7,6},{8,9},{9,8},{10,11... | collective-permute-start | bytes 4718600 | tf_op jit(solution)/shard_map/ppermute | solution.py:930
  7.2 23.9 %collective-permute-start.6 = (bf16[1024,768]{1,0:T(8,128)(2,1)}, bf16[1024,768]{1,0:T(8,128)(2,1)S(1)}, u32[]{:S(2)}, u32[]{:S(2)}) collective-permute-start(bf16[1024,768]{1,0:T(8,128)(2,1)} %wd_hbm_0_), channel_id=1, source_target_pairs={{0,1},{1,0},{2,3},{3,2},{4,5},{5,4},{6,7},{7,6},{8,9},{9,8},{10,11... | collective-permute-start | bytes 4718600 | tf_op jit(solution)/shard_map/ppermute | solution.py:930
  38.6 10.6 %collective-permute-start.7 = (bf16[768,1536]{1,0:T(8,128)(2,1)S(1)}, bf16[768,1536]{1,0:T(8,128)(2,1)S(1)}, u32[]{:S(2)}, u32[]{:S(2)}) collective-permute-start(bf16[768,1536]{1,0:T(8,128)(2,1)S(1)} %get-tuple-element.181), channel_id=1, source_target_pairs={{0,1},{1,0},{2,3},{3,2},{4,5},{5,4},{6,7},{7,6},{8,9},{9,8},{10,11... | collective-permute-start | bytes 7077896 | tf_op jit(solution)/shard_map/ppermute | solution.py:930
  48.7 8.7 %collective-permute-start.8 = (bf16[768,1536]{1,0:T(8,128)(2,1)S(1)}, bf16[768,1536]{1,0:T(8,128)(2,1)S(1)}, u32[]{:S(2)}, u32[]{:S(2)}) collective-permute-start(bf16[768,1536]{1,0:T(8,128)(2,1)S(1)} %get-tuple-element.189), channel_id=1, source_target_pairs={{0,1},{1,0},{2,3},{3,2},{4,5},{5,4},{6,7},{7,6},{8,9},{9,8},{10,11... | collective-permute-start | bytes 7077896 | tf_op jit(solution)/shard_map/ppermute | solution.py:930
  57.4 12.8 %copy-start.5 = (bf16[1152,512]{1,0:T(8,128)(2,1)S(1)}, bf16[1152,512]{1,0:T(8,128)(2,1)}, u32[]{:S(2)}) copy-start(bf16[1152,512]{1,0:T(8,128)(2,1)} %copy-done.4) | copy-start | bytes 3538948
  57.4 12.8 %copy-start.7 = (bf16[1152,512]{1,0:T(8,128)(2,1)S(1)}, bf16[1152,512]{1,0:T(8,128)(2,1)}, u32[]{:S(2)}) copy-start(bf16[1152,512]{1,0:T(8,128)(2,1)} %copy-done.6) | copy-start | bytes 3538948
  66.0 36.9 %collective-permute-start.10 = (bf16[2,192,1536]{2,1,0:T(8,128)(2,1)S(1)}, bf16[2,192,1536]{2,1,0:T(8,128)(2,1)S(1)}, u32[]{:S(2)}, u32[]{:S(2)}) collective-permute-start(bf16[2,192,1536]{2,1,0:T(8,128)(2,1)S(1)} %get-tuple-element.251), channel_id=1, source_target_pairs={{0,2},{2,0},{4,6},{6,4},{8,10},{10,8},{12,14},{14,12},{16,18},{18,... | collective-permute-start | bytes 3538952 | tf_op jit(solution)/shard_map/ppermute | solution.py:769
  68.7 34.3 %collective-permute-start.11 = (bf16[2,192,1536]{2,1,0:T(8,128)(2,1)S(1)}, bf16[2,192,1536]{2,1,0:T(8,128)(2,1)S(1)}, u32[]{:S(2)}, u32[]{:S(2)}) collective-permute-start(bf16[2,192,1536]{2,1,0:T(8,128)(2,1)S(1)} %get-tuple-element.252), channel_id=1, source_target_pairs={{0,4},{2,6},{4,0},{6,2},{8,12},{10,14},{12,8},{14,10},{16,20},{18,... | collective-permute-start | bytes 3538952 | tf_op jit(solution)/shard_map/ppermute | solution.py:769
  85.9 17.0 %copy-start.2 = (f32[1152,768]{1,0:T(8,128)}, f32[1152,768]{1,0:T(8,128)S(1)}, u32[]{:S(2)}) copy-start(f32[1152,768]{1,0:T(8,128)S(1)} %get-tuple-element.236.dh1_ref) | copy-start | bytes 10616836
  85.9 17.0 %collective-permute-start.9 = (bf16[768,384]{1,0:T(8,128)(2,1)S(1)}, bf16[768,384]{1,0:T(8,128)(2,1)S(1)}, u32[]{:S(2)}, u32[]{:S(2)}) collective-permute-start(bf16[768,384]{1,0:T(8,128)(2,1)S(1)} %get-tuple-element.247), channel_id=1, source_target_pairs={{0,1},{1,0},{2,3},{3,2},{4,5},{5,4},{6,7},{7,6},{8,9},{9,8},{10,11... | collective-permute-start | bytes 1769480 | tf_op jit(solution)/shard_map/ppermute | solution.py:930
  103.0 3.8 %collective-permute-start.12 = (bf16[768,1152]{1,0:T(8,128)(2,1)S(1)}, bf16[768,1152]{1,0:T(8,128)(2,1)S(1)}, u32[]{:S(2)}, u32[]{:S(2)}) collective-permute-start(bf16[768,1152]{1,0:T(8,128)(2,1)S(1)} %get-tuple-element.254), channel_id=1, source_target_pairs={{0,1},{1,0},{2,3},{3,2},{4,5},{5,4},{6,7},{7,6},{8,9},{9,8},{10,11... | collective-permute-start | bytes 5308424 | tf_op jit(solution)/shard_map/ppermute | solution.py:930
  103.3 19.0 %collective-permute-start.13 = (bf16[192,1536]{1,0:T(8,128)(2,1)S(1)}, bf16[192,1536]{1,0:T(8,128)(2,1)S(1)}, u32[]{:S(2)}, u32[]{:S(2)}) collective-permute-start(bf16[192,1536]{1,0:T(8,128)(2,1)S(1)} %get-tuple-element.268), channel_id=1, source_target_pairs={{0,4},{2,6},{4,0},{6,2},{8,12},{10,14},{12,8},{14,10},{16,20},{18,... | collective-permute-start | bytes 1769480 | tf_op jit(solution)/shard_map/ppermute | solution.py:769
  103.9 18.5 %collective-permute-start.14 = (bf16[192,1536]{1,0:T(8,128)(2,1)S(1)}, bf16[192,1536]{1,0:T(8,128)(2,1)S(1)}, u32[]{:S(2)}, u32[]{:S(2)}) collective-permute-start(bf16[192,1536]{1,0:T(8,128)(2,1)S(1)} %get-tuple-element.269), channel_id=1, source_target_pairs={{0,2},{2,0},{4,6},{6,4},{8,10},{10,8},{12,14},{14,12},{16,18},{18,... | collective-permute-start | bytes 1769480 | tf_op jit(solution)/shard_map/ppermute | solution.py:769
  122.4 18.2 %collective-permute-start.15 = (bf16[2,96,1536]{2,1,0:T(8,128)(2,1)S(1)}, bf16[2,96,1536]{2,1,0:T(8,128)(2,1)S(1)}, u32[]{:S(2)}, u32[]{:S(2)}) collective-permute-start(bf16[2,96,1536]{2,1,0:T(8,128)(2,1)S(1)} %get-tuple-element.283), channel_id=1, source_target_pairs={{0,2},{2,0},{4,6},{6,4},{8,10},{10,8},{12,14},{14,12},{16,18},{18,... | collective-permute-start | bytes 1769480 | tf_op jit(solution)/shard_map/ppermute | solution.py:769
  123.0 17.6 %collective-permute-start.16 = (bf16[2,96,1536]{2,1,0:T(8,128)(2,1)S(1)}, bf16[2,96,1536]{2,1,0:T(8,128)(2,1)S(1)}, u32[]{:S(2)}, u32[]{:S(2)}) collective-permute-start(bf16[2,96,1536]{2,1,0:T(8,128)(2,1)S(1)} %get-tuple-element.284), channel_id=1, source_target_pairs={{0,4},{2,6},{4,0},{6,2},{8,12},{10,14},{12,8},{14,10},{16,20},{18,... | collective-permute-start | bytes 1769480 | tf_op jit(solution)/shard_map/ppermute | solution.py:769
  123.6 17.0 %collective-permute-start.17 = (bf16[2,48,3072]{2,1,0:T(8,128)(2,1)S(1)}, bf16[2,48,3072]{2,1,0:T(8,128)(2,1)S(1)}, u32[]{:S(2)}, u32[]{:S(2)}) collective-permute-start(bf16[2,48,3072]{2,1,0:T(8,128)(2,1)S(1)} %get-tuple-element.287), channel_id=1, source_target_pairs={{0,8},{2,10},{4,12},{6,14},{8,0},{10,2},{12,4},{14,6},{16,24},{18,... | collective-permute-start | bytes 1769480 | tf_op jit(solution)/shard_map/ppermute | solution.py:769
  140.7 2.8 %collective-permute-start.18 = (f32[2,768]{1,0:T(2,128)S(1)}, f32[2,768]{1,0:T(2,128)S(1)}, u32[]{:S(2)}, u32[]{:S(2)}) collective-permute-start(f32[2,768]{1,0:T(2,128)S(1)} %pad_maximum_fusion.2), channel_id=1, source_target_pairs={{0,1},{1,0},{2,3},{3,2},{4,5},{5,4},{6,7},{7,6},{8,9},{9,8},{10,11... | collective-permute-start | bytes 18440 | tf_op jit(solution)/shard_map/ppermute | solution.py:930
  140.8 16.5 %collective-permute-start.28 = (bf16[48,3072]{1,0:T(8,128)(2,1)S(1)}, bf16[48,3072]{1,0:T(8,128)(2,1)S(1)}, u32[]{:S(2)}, u32[]{:S(2)}) collective-permute-start(bf16[48,3072]{1,0:T(8,128)(2,1)S(1)} %far_sum.1), channel_id=1, source_target_pairs={{0,16},{2,18},{4,20},{6,22},{8,24},{10,26},{12,28},{14,30},{16,0},... | collective-permute-start | bytes 884744 | tf_op jit(solution)/shard_map/ppermute | solution.py:769
  143.5 3.8 %collective-permute-start.19 = (f32[2,768]{1,0:T(2,128)S(1)}, f32[2,768]{1,0:T(2,128)S(1)}, u32[]{:S(2)}, u32[]{:S(2)}) collective-permute-start(f32[2,768]{1,0:T(2,128)S(1)} %fusion.1), channel_id=1, source_target_pairs={{0,2},{2,0},{4,6},{6,4},{8,10},{10,8},{12,14},{14,12},{16,18},{18,... | collective-permute-start | bytes 18440 | tf_op jit(solution)/shard_map/ppermute | solution.py:769
  145.2 12.3 %collective-permute-start.20 = (bf16[96,1536]{1,0:T(8,128)(2,1)S(1)}, bf16[96,1536]{1,0:T(8,128)(2,1)S(1)}, u32[]{:S(2)}, u32[]{:S(2)}) collective-permute-start(bf16[96,1536]{1,0:T(8,128)(2,1)S(1)} %get-tuple-element.294), channel_id=1, source_target_pairs={{0,4},{2,6},{4,0},{6,2},{8,12},{10,14},{12,8},{14,10},{16,20},{18,... | collective-permute-start | bytes 884744 | tf_op jit(solution)/shard_map/ppermute | solution.py:769
  146.7 10.8 %collective-permute-start.21 = (bf16[96,1536]{1,0:T(8,128)(2,1)S(1)}, bf16[96,1536]{1,0:T(8,128)(2,1)S(1)}, u32[]{:S(2)}, u32[]{:S(2)}) collective-permute-start(bf16[96,1536]{1,0:T(8,128)(2,1)S(1)} %get-tuple-element.295), channel_id=1, source_target_pairs={{0,2},{2,0},{4,6},{6,4},{8,10},{10,8},{12,14},{14,12},{16,18},{18,... | collective-permute-start | bytes 884744 | tf_op jit(solution)/shard_map/ppermute | solution.py:769
  157.5 6.4 %collective-permute-start.22 = (f32[2,768]{1,0:T(2,128)S(1)}, f32[2,768]{1,0:T(2,128)S(1)}, u32[]{:S(2)}, u32[]{:S(2)}) collective-permute-start(f32[2,768]{1,0:T(2,128)S(1)} %fusion.4), channel_id=1, source_target_pairs={{0,4},{2,6},{4,0},{6,2},{8,12},{10,14},{12,8},{14,10},{16,20},{18,... | collective-permute-start | bytes 18440 | tf_op jit(solution)/shard_map/ppermute | solution.py:769
  159.4 7.8 %collective-permute-start.23 = (bf16[48,1536]{1,0:T(8,128)(2,1)S(1)}, bf16[48,1536]{1,0:T(8,128)(2,1)S(1)}, u32[]{:S(2)}, u32[]{:S(2)}) collective-permute-start(bf16[48,1536]{1,0:T(8,128)(2,1)S(1)} %get-tuple-element.299), channel_id=1, source_target_pairs={{0,8},{2,10},{4,12},{6,14},{8,0},{10,2},{12,4},{14,6},{16,24},{18,... | collective-permute-start | bytes 442376 | tf_op jit(solution)/shard_map/ppermute | solution.py:769
  159.5 14.3 %collective-permute-start.26 = (bf16[48,1536]{1,0:T(8,128)(2,1)S(1)}, bf16[48,1536]{1,0:T(8,128)(2,1)S(1)}, u32[]{:S(2)}, u32[]{:S(2)}) collective-permute-start(bf16[48,1536]{1,0:T(8,128)(2,1)S(1)} %get-tuple-element.303), channel_id=1, source_target_pairs={{0,16},{2,18},{4,20},{6,22},{8,24},{10,26},{12,28},{14,30},{16,0},... | collective-permute-start | bytes 442376 | tf_op jit(solution)/shard_map/ppermute | solution.py:769
  162.7 11.1 %collective-permute-start.27 = (bf16[48,1536]{1,0:T(8,128)(2,1)S(1)}, bf16[48,1536]{1,0:T(8,128)(2,1)S(1)}, u32[]{:S(2)}, u32[]{:S(2)}) collective-permute-start(bf16[48,1536]{1,0:T(8,128)(2,1)S(1)} %get-tuple-element.304), channel_id=1, source_target_pairs={{0,24},{2,26},{4,28},{6,30},{8,16},{10,18},{12,20},{14,22},{16,8},... | collective-permute-start | bytes 442376 | tf_op jit(solution)/shard_map/ppermute | solution.py:769
  167.2 4.2 %collective-permute-start.24 = (f32[2,768]{1,0:T(2,128)S(1)}, f32[2,768]{1,0:T(2,128)S(1)}, u32[]{:S(2)}, u32[]{:S(2)}) collective-permute-start(f32[2,768]{1,0:T(2,128)S(1)} %add.26), channel_id=1, source_target_pairs={{0,8},{2,10},{4,12},{6,14},{8,0},{10,2},{12,4},{14,6},{16,24},{18,... | collective-permute-start | bytes 18440 | tf_op jit(solution)/shard_map/ppermute | solution.py:769
  171.4 4.5 %collective-permute-start.25 = (f32[2,768]{1,0:T(2,128)S(1)}, f32[2,768]{1,0:T(2,128)S(1)}, u32[]{:S(2)}, u32[]{:S(2)}) collective-permute-start(f32[2,768]{1,0:T(2,128)S(1)} %add.27), channel_id=1, source_target_pairs={{0,16},{2,18},{4,20},{6,22},{8,24},{10,26},{12,28},{14,30},{16,0},... | collective-permute-start | bytes 18440 | tf_op jit(solution)/shard_map/ppermute | solution.py:769
  (11 other events, 59.1 us)

commit v3 on v2

--- a/solution.py
+++ b/solution.py
@@ -250,34 +250,52 @@
     count, width = na_ref.shape
     items, cols = count // SLOTS, wo_hbm[0].shape[0]
     half = cols // PAIR
+    weights_in = [
+        [arrive.start(w[j], weights.at[j, :, i * cols : (i + 1) * cols]) for i, w in enumerate(w_hbm)] for j in range(3)
+    ]
     early = [arrive.start(cos_hbm, cosine), arrive.start(sin_hbm, sine)]
-    for p in range(2 * half):
-        for j in range(3):
-            source = w_hbm[p // half][j].at[:, (p % half) * PAIR : (p % half + 1) * PAIR]
-            early.append(arrive.start(source, weights.at[:, (3 * p + j) * PAIR : (3 * p + j + 1) * PAIR]))
     late = [arrive.start(w, wo.at[i * cols : (i + 1) * cols, :]) for i, w in enumerate(wo_hbm)]
     late += [arrive.start(x_hbm, x), arrive.start(gain_hbm, gain_ref)]
-    for c in early:
-        c.wait()
+    blocks = row_blocks(count)
+    targets = (q_ref, k_ref, v_ref)
+
+    def project(task):
+        j, own = task
+        return dot(na_ref[own, :], weights[j])
+
+    def place(task, made):
+        j, own = task
+        if j == 2:
+            v_ref[own, :] = made.astype(BF16)
+            return
+        cos_v, sin_v = cosine[own, :], sine[own, :]
+        for start in range(0, width, PAIR):
+            cols_ = slice(start, start + PAIR)
+            turned = made[:, cols_] * cos_v + swap_halves(made[:, cols_]) * sin_v
+            targets[j][own, cols_] = (turned * HEAD**-0.5 if j == 0 else turned).astype(BF16)
+
+    tasks = [(j, own) for j in range(3) for own in blocks]
+    made = None
+    for i in range(len(tasks) + 1):
+        if i % len(blocks) == 0 and i < len(tasks):
+            for c in weights_in[i // len(blocks)]:
+                c.wait()
+        upcoming = project(tasks[i]) if i < len(tasks) else None
+        if made is not None:
+            if i == 1:
+                for c in early:
+                    c.wait()
+            place(tasks[i - 1], made)
+        made = upcoming
+    sent = [copy(source, target, out_sems.at[j]) for j, (source, target) in enumerate(leaving)]
 
     @pl.loop(0, 2 * half)
     def _(pair):
         own_cols = pl.ds(pl.multiple_of(pair * PAIR, PAIR), PAIR)
-        own_weights = weights[:, pl.ds(pl.multiple_of(pair * 3 * PAIR, PAIR), 3 * PAIR)]
-        for own in row_blocks(count):
-            qkv = dot(na_ref[own, :], own_weights)
-            cos_v, sin_v = cosine[own, :], sine[own, :]
-            q, k = qkv[:, :PAIR], qkv[:, PAIR : 2 * PAIR]
-            q_ref[own, own_cols] = ((q * cos_v + swap_halves(q) * sin_v) * HEAD**-0.5).astype(BF16)
-            k_ref[own, own_cols] = (k * cos_v + swap_halves(k) * sin_v).astype(BF16)
-            v_ref[own, own_cols] = qkv[:, 2 * PAIR :].astype(BF16)
-        for j, (source, target) in enumerate(leaving):
-            copy(source.at[:, own_cols], target.at[:, own_cols], out_sems.at[3 * pair + j])
         attend(items, q_ref, k_ref, v_ref, own_cols, o_ref, lse_ref, pair, acc)
 
     for c in late:
         c.wait()
-    blocks = row_blocks(count)
     branch = dot(o_ref[blocks[0], :], wo[...])
     for i, own in enumerate(blocks):
         upcoming = dot(o_ref[blocks[i + 1], :], wo[...]) if i + 1 < len(blocks) else None
@@ -288,13 +306,9 @@
         nf_ref[own, :] = normed
         store_transposed(normed, turn, nft_ref.at[:, own], me_ref, dp)
         branch = upcoming
-        copy(h1_ref.at[own, :], h1_hbm.at[own, :], out_sems.at[6 * half + i])
-    for p in range(2 * half):
-        own_cols = slice(p * PAIR, (p + 1) * PAIR)
-        for j, (source, target) in enumerate(leaving):
-            pltpu.make_async_copy(source.at[:, own_cols], target.at[:, own_cols], out_sems.at[3 * p + j]).wait()
-    for i, own in enumerate(blocks):
-        pltpu.make_async_copy(h1_ref.at[own, :], h1_hbm.at[own, :], out_sems.at[6 * half + i]).wait()
+        sent.append(copy(h1_ref.at[own, :], h1_hbm.at[own, :], out_sems.at[3 + i]))
+    for c in sent:
+        c.wait()
 
 
 def front(dp, me, na, tables, gain, w, wo, x):
@@ -317,14 +331,14 @@
         + [
             pltpu.VMEM((count, width), F32),
             pltpu.VMEM((items, PAIR, SLOTS), F32),
-            pltpu.VMEM((width, 6 * cols), BF16),
+            pltpu.VMEM((3, width, 2 * cols), BF16),
             pltpu.VMEM((2 * cols, width), BF16),
             pltpu.VMEM((count, width), BF16),
             pltpu.VMEM((count, PAIR), F32),
             pltpu.VMEM((count, PAIR), F32),
             pltpu.VMEM((width, ROWS), BF16),
-            pltpu.SemaphoreType.DMA((6 * half + 6,)),
-            pltpu.SemaphoreType.DMA((6 * half + count // ROWS,)),
+            pltpu.SemaphoreType.DMA((12,)),
+            pltpu.SemaphoreType.DMA((3 + count // ROWS,)),
         ],
         compiler_params=params(28),
         cost_estimate=cost(8 * count * width * width + 8 * area * PAIR, 24 * count * width, area),
@@ -668,11 +682,9 @@
     x_in = [arrive.start(x_hbm.at[own, :], x.at[own, :]) for own in blocks] + [arrive.start(gain_hbm, gain_ref)]
     half, size = wd_hbm[0].shape[0], hid_hbm[0].shape[1]
     wd_in = [arrive.start(w, wd.at[i * half : (i + 1) * half, :]) for i, w in enumerate(wd_hbm)]
-    row_in = [
-        [arrive.start(h.at[own, :], hid.at[own, j * size : (j + 1) * size]) for j, h in enumerate(hid_hbm)]
-        + [arrive.start(h1_hbm.at[own, :], h1.at[own, :])]
-        for own in blocks
-    ]
+    own = blocks[0]
+    row_in = [arrive.start(h.at[own, :], hid.at[:, j * size : (j + 1) * size]) for j, h in enumerate(hid_hbm)]
+    row_in.append(arrive.start(h1_hbm.at[own, :], h1))
 
     def product(i):
         total = None
@@ -685,33 +697,24 @@
             total = term if total is None else total + term
         return total
 
-    def down(i):
-        if i == 0:
-            for c in wd_in:
-                c.wait()
-        for c in row_in[i]:
-            c.wait()
-        return dot(hid[blocks[i], :], wd[...])
-
     dna, gain_total, total = product(0), None, None
     for c in x_in:
         c.wait()
     for i, own in enumerate(blocks):
         upcoming = product(i + 1) if i + 1 < len(blocks) else None
         if i + 1 == len(blocks):
-            total = down(0)
+            for c in wd_in + row_in:
+                c.wait()
+            total = h1[...] + dot(hid[...], wd[...])
         d_rows, gain_part = norm_back_rows(x[own, :].astype(F32), dna, gain_ref[...][None, :])
         gain_total = gain_part if gain_total is None else gain_total + gain_part
         gin[own, :] = dh1_ref[own, :] + d_rows
         sent.start(gin.at[own, :], gin_hbm.at[own, :])
         dna = upcoming
     dgain_ref[...] = gain_total
-    for i, own in enumerate(blocks):
-        upcoming = down(i + 1) if i + 1 < len(blocks) else None
-        total = total + h1[own, :]
-        out[own, :] = jnp.where(row_is_valid(me_ref, lens_ref, items, own.start, own.stop - own.start), total, 0.0).astype(BF16)
-        sent.start(out.at[own, :], out_hbm.at[own, :])
-        total = upcoming
+    own = blocks[0]
+    out[...] = jnp.where(row_is_valid(me_ref, lens_ref, items, own.start, own.stop), total, 0.0).astype(BF16)
+    sent.start(out, out_hbm.at[own, :])
     sent.wait()
 
 
@@ -729,20 +732,73 @@
             pltpu.VMEM((2, width, deep // 2), BF16),
             pltpu.VMEM((count, width), BF16),
             pltpu.VMEM((count, width), F32),
-            pltpu.VMEM((count, width), F32),
+            pltpu.VMEM((ROWS, width), F32),
             pltpu.VMEM((2 * half, width), BF16),
-            pltpu.VMEM((count, 2 * half), BF16),
-            pltpu.VMEM((count, width), BF16),
+            pltpu.VMEM((ROWS, 2 * half), BF16),
+            pltpu.VMEM((ROWS, width), BF16),
             pltpu.SemaphoreType.DMA((len(weights) + 3 + steps * (2 + len(hid)),)),
             pltpu.SemaphoreType.DMA((2 * steps,)),
         ],
-        compiler_params=params(36),
+        compiler_params=params(28),
         cost_estimate=cost(2 * count * width * (deep + 2 * half), 16 * count * width + 2 * count * (deep + 2 * half)),
         name="finish",
     )(
         me, lens, off_chip(gain), on_chip(dh1), list(on_chip(grads)), off_chip(x),
         [*off_chip(weights[:mine]), *weights[mine:]], off_chip(h1), [off_chip(wd[0]), wd[1]], list(off_chip(hid)),
     )
+
+
+def output_kernel(items, blocks, me_ref, lens_ref, h1_hbm, wd_hbm, hid_hbm, *rest):
+    out_hbm, h1, wd, hid, out, in_sems, out_sems = rest[-7:]
+    arrive, sent = Copies(in_sems), Copies(out_sems)
+    half, size = wd_hbm[0].shape[0], hid_hbm[0].shape[1]
+    wd_in = [arrive.start(w, wd.at[i * half : (i + 1) * half, :]) for i, w in enumerate(wd_hbm)]
+    row_in = [
+        [arrive.start(h.at[own, :], hid.at[own, j * size : (j + 1) * size]) for j, h in enumerate(hid_hbm)]
+        + [arrive.start(h1_hbm.at[own, :], h1.at[own, :])]
+        for own in blocks
+    ]
+
+    def down(i):
+        for c in (wd_in if i == 0 else []) + row_in[i]:
+            c.wait()
+        return dot(hid[blocks[i], :], wd[...])
+
+    total = down(0)
+    for i, own in enumerate(blocks):
+        upcoming = down(i + 1) if i + 1 < len(blocks) else None
+        total = total + h1[own, :]
+        out[own, :] = jnp.where(row_is_valid(me_ref, lens_ref, items, own.start, own.stop - own.start), total, 0.0).astype(BF16)
+        sent.start(out.at[own, :], out_hbm.at[own, :])
+        total = upcoming
+    sent.wait()
+
+
+def layer_output(me, lens, h1, wd, hid, rows, base=None):
+    count, width = h1.shape
+    half = wd[0].shape[0]
+    blocks = [slice(i, i + ROWS) for i in range(rows.start, rows.stop, ROWS)]
+    args = [me, lens, off_chip(h1), [off_chip(wd[0]), wd[1]], list(off_chip(hid))]
+    if base is not None:
+        args.append(base)
+    return pl.pallas_call(
+        functools.partial(output_kernel, count // SLOTS, blocks),
+        in_specs=[SCALAR, SCALAR, ANY, [ANY] * 2, [ANY] * len(hid)] + [ANY] * (len(args) - 5),
+        out_specs=ANY,
+        out_shape=hbm((count, width), BF16),
+        input_output_aliases={} if base is None else {3 + len(wd) + len(hid): 0},
+        scratch_shapes=[
+            pltpu.VMEM((count, width), F32),
+            pltpu.VMEM((2 * half, width), BF16),
+            pltpu.VMEM((count, 2 * half), BF16),
+            pltpu.VMEM((count, width), BF16),
+            pltpu.SemaphoreType.DMA((2 + len(blocks) * (1 + len(hid)),)),
+            pltpu.SemaphoreType.DMA((len(blocks),)),
+        ],
+        compiler_params=params(22),
+        cost_estimate=cost(2 * count * width * half, 3 * count * width + 2 * count * half),
+        name="layer_output",
+    )(*args)
 
 
 def second_kernel(keep_a, recv_a, keep_b, recv_b, send_a, send_b):
@@ -979,18 +1035,20 @@
     grad_input, output, dgain_a = finish(
         me, lengths, tokens, dh1, gain_a, (wq[0], wk[0], wv[0], wq[1], wk[1], wv[1]), (*d0, *d1), h1, wd, hid
     )
-    dgain_a, recv_q, near = fence((dgain_a, recv_q, near))
+    dgain_a, recv_q, near, h1 = fence((dgain_a, recv_q, near, h1))
     far = far_swap(kept, near, dp) if two_steps else None
     last_q = second_swaps(q_piece, recv_q, dp)
     gains = jnp.concatenate([dgain_a, dgain_f], 0)
     gains = swap_sum(gains + other(gains), dp, (1,))
-    gains, last_q = fence((gains, last_q))
+    output = layer_output(me, lengths, h1, wd, hid, slice(ROWS, count), output)
+    gains, last_q, output = fence((gains, last_q, output))
     kept_q, far_q = third_rows_swaps(q_piece, recv_q, last_q, dp)
     gains = swap_sum(gains, dp, (2,))
-    gains, first_q = fence((gains, far_q[0]))
+    gains, first_q, far = fence((gains, far_q[0], far))
     far_q = (first_q, *far_q[1:])
-    for bit in range(2, dp.bit_length() - 1):
-        gains = swap_sum(gains, dp, (1 << bit,))
+    far_bits = [1 << bit for bit in range(2, dp.bit_length() - 1)]
+    for bits in (far_bits,) if two_steps else ((bit,) for bit in far_bits):
+        gains = swap_sum(gains, dp, bits)
     total = total_of(kept[0].astype(F32), (near[0], far)) if two_steps else total_of(kept, near)
     gq, gk, gv, out_piece = last_sum(kept_q, far_q)
     side, wide = total.shape[1] // 2, 3 * CHUNK // 2

time: 180 us -> 170 us (0.944)
  waiting for transfers between devices: 21.4 us -> 7.14 us
  starting transfers between devices: 24.2 us -> 29.8 us
  local copies, waits for them, and re-layouts: 3.47 us -> 1.37 us
    ppermute x17 -> x18, waiting for transfers between devices: 18.8 us -> 4.75 us  [swap_dp(): return lax.ppermute(array, 'dp', [(i, i ^ relative) for i in range(dp)])]
    pallas_call x0 -> x1, Pallas kernels: none -> 7.16 us  [layer_output(): pl.pallas_call(functools.partial(output_kernel, count // SLOTS, blocks),...]
    ppermute x17 -> x18, starting transfers between devices: 21.3 us -> 26.4 us  [swap_dp(): return lax.ppermute(array, 'dp', [(i, i ^ relative) for i in range(dp)])]
    pallas_call x1, Pallas kernels: 15 us -> 11.7 us  [finish(): pl.pallas_call(functools.partial(finish_kernel, count // SLOTS), in_specs...]
    unnamed x28 -> x12, local copies, waits for them, and re-layouts: 2.78 us -> 0.68 us
  transfers between devices with their start and end apart: 29 -> 30, of which waited for: 6 -> 7; matrix products, arithmetic and copies ran while one was open for 1% -> 1% of each run, Pallas kernels for 61% -> 65%
where the time goes in v3:
time: 170 us; the launch traced here: 167 us
  Pallas kernels  125 us (74%)
  starting transfers between devices  29.8 us (18%)
  waiting for transfers between devices  7.14 us (4%)
    pallas_call x4, Pallas kernels, ffn(): pl.pallas_call(functools.partial(ffn_kernel, final, chunk * CHUNK, chunk...  32.1 us
    pallas_call x2, Pallas kernels, attention_back(): pl.pallas_call(functools.partial(attention_back_kernel, final, first), in...  31.1 us
    ppermute x18, starting transfers between devices, swap_dp(): return lax.ppermute(array, 'dp', [(i, i ^ relative) for i in range(dp)])  26.4 us
    pallas_call x1, Pallas kernels, front(): pl.pallas_call(functools.partial(front_kernel, dp), in_specs=[SCALAR, ANY...  21.8 us
    pallas_call x1, Pallas kernels, ffn_back(): pl.pallas_call(functools.partial(ffn_back_kernel, dp), in_specs=[SCALAR,...  15.6 us
    pallas_call x1, Pallas kernels, finish(): pl.pallas_call(functools.partial(finish_kernel, count // SLOTS), in_specs...  11.7 us
    pallas_call x1, Pallas kernels, layer_output(): pl.pallas_call(functools.partial(output_kernel, count // SLOTS, blocks),...  7.16 us
    ppermute x18, waiting for transfers between devices, swap_dp(): return lax.ppermute(array, 'dp', [(i, i ^ relative) for i in range(dp)])  4.75 us
  transfers between devices with their start and end apart: 30, of which 7 were waited for; matrix products, arithmetic and copies ran while one was open for 1% of the time, Pallas kernels for 65%

profile of v3, /device:TPU:0, one launch (start us, length us, event | category | flops | bytes accessed | tf_op | source)
XLA Modules:
  0.0 166.9 jit_solution(9099448795887597795)
XLA Ops:
  1.8 0.7 copy-done
  2.5 4.1 %prepare.1 = (bf16[1152,768]{1,0:T(8,128)(2,1)S(1)}, bf16[768,1152]{1,0:T(8,128)(2,1)S(1)}, bf16[1152,768]{1,0:T(8,128)(2,1)S(1)}, bf16[768,1152]{1,0:T(8,128)(2,1)S(1)}) custom-call(s32[2]{0:T(128)S(1)} %pad_add_fusion.me_ref, s32[4]{0:T(128)S(1)} %copy-done, f32[768]{0:T(1024)} %gain_hbm.7, bf16[1152,768]{1,0:T(8,128)(2,1)} %x_hbm.5, bf16[1152,768]{1,0:T(8,128)(2,1)} %cot_hbm.1), custom_call_target="tpu_custom_call" | custom-call | flops 8847360 | bytes 10616832 | tf_op jit(solution)/shard_map/prepare/pallas_call | solution.py:161
  7.7 21.8 %front.1 = (bf16[1152,768]{1,0:T(8,128)(2,1)}, bf16[1152,768]{1,0:T(8,128)(2,1)}, bf16[1152,768]{1,0:T(8,128)(2,1)}, f32[1152,768]{1,0:T(8,128)}, bf16[1152,768]...) custom-call(s32[2]{0:T(128)S(1)} %pad_add_fusion.me_ref, ...), custom_call_target="tpu_custom_call" | custom-call | flops 13589544960 | bytes 21233664 | tf_op jit(solution)/shard_map/front/pallas_call | solution.py:319
  29.5 7.9 %ffn_other.2 = (bf16[1152,512]{1,0:T(8,128)(2,1)}, bf16[1152,512]{1,0:T(8,128)(2,1)S(1)}, bf16[1152,512]{1,0:T(8,128)(2,1)S(1)}, bf16[768,1536]{1,0:T(8,128)(2,1)S(1)}) custom-call(bf16[1152,768]{1,0:T(8,128)(2,1)S(1)} %get-tuple-element.210.nf_ref, bf16[768,1152]{1,0:T(8,128)(2,1)S(1)} %get-tuple-element.174.nft_ref, ...), custom_call_target="tpu_custom_call" | custom-call | flops 5435817984 | bytes 11796480 | tf_op jit(solution)/shard_map/ffn_other/pallas_call | solution.py:565
  37.6 7.3 %ffn_other.3 = (bf16[1152,512]{1,0:T(8,128)(2,1)}, bf16[1152,512]{1,0:T(8,128)(2,1)S(1)}, bf16[1152,512]{1,0:T(8,128)(2,1)S(1)}, bf16[768,1536]{1,0:T(8,128)(2,1)S(1)}) custom-call(bf16[1152,768]{1,0:T(8,128)(2,1)S(1)} %get-tuple-element.210.nf_ref, bf16[768,1152]{1,0:T(8,128)(2,1)S(1)} %get-tuple-element.174.nft_ref, ...), custom_call_target="tpu_custom_call" | custom-call | flops 5435817984 | bytes 11796480 | tf_op jit(solution)/shard_map/ffn_other/pallas_call | solution.py:565
  45.4 8.2 %ffn_final.2 = (bf16[1152,512]{1,0:T(8,128)(2,1)}, bf16[1152,512]{1,0:T(8,128)(2,1)S(1)}, bf16[1152,512]{1,0:T(8,128)(2,1)S(1)}, bf16[2,192,1536]{2,1,0:T(8,128)...) custom-call(bf16[1152,768]{1,0:T(8,128)(2,1)S(1)} %get-tuple-element, ...), custom_call_target="tpu_custom_call" | custom-call | flops 5435817984 | bytes 11796480 | tf_op jit(solution)/shard_map/ffn_final/pallas_call | solution.py:565
  53.7 8.7 %ffn_final.3 = (bf16[1152,512]{1,0:T(8,128)(2,1)}, bf16[1152,512]{1,0:T(8,128)(2,1)S(1)}, bf16[1152,512]{1,0:T(8,128)(2,1)S(1)}, bf16[2,192,1536]{2,1,0:T(8,128)...) custom-call(bf16[1152,768]{1,0:T(8,128)(2,1)S(1)} %get-tuple-element, ...), custom_call_target="tpu_custom_call", output_to_operand_aliasing={{3}: (8, {}), {4}: (9, {}), {5}: (10, {}), {6}: (11, {})} | custom-call | flops 5435817984 | bytes 11796480 | tf_op jit(solution)/shard_map/ffn_final/pallas_call | solution.py:565
  62.3 2.6 %collective-permute-start.10 = (bf16[2,192,1536]{2,1,0:T(8,128)(2,1)S(1)}, bf16[2,192,1536]{2,1,0:T(8,128)(2,1)S(1)}, u32[]{:S(2)}, u32[]{:S(2)}) collective-permute-start(bf16[2,192,1536]{2,1,0:T(8,128)(2,1)S(1)} %get-tuple-element.254), channel_id=1, source_target_pairs={{0,2},{2,0},{4,6},{6,4},{8,10},{10,8},{12,14},{14,12},{16,18},{18,... | collective-permute-start | bytes 3538952 | tf_op jit(solution)/shard_map/ppermute | solution.py:825
  65.0 1.5 collective-permute-start.11
  66.5 15.6 %ffn_back.1 = (f32[1152,768]{1,0:T(8,128)S(1)}, bf16[1152,768]{1,0:T(8,128)(2,1)S(1)}, f32[1,768]{1,0:T(1,128)S(1)}, bf16[768,384]{1,0:T(8,128)(2,1)S(1)}, bf16[768,384]{1,0:T(8,128)(2,1)S(1)}) custom-call(s32[2]{0:T(128)S(1)} %pad_add_fusion.me_ref, f32[768]{0:T(1024)} %gain_hbm.6, f32[1152,768]{1,0:T(8,128)} %get-tuple-element.297.h1_hbm, ...), custom_call_target="tpu_custom_call" | custom-call | flops 9965666304 | bytes 27131904 | tf_op jit(solution)/shard_map/ffn_back/pallas_call | solution.py:643
  82.1 15.6 %attention_back_other.1 = (bf16[1152,384]{1,0:T(8,128)(2,1)S(1)}, bf16[1152,384]{1,0:T(8,128)(2,1)S(1)}, bf16[1152,384]{1,0:T(8,128)(2,1)S(1)}, bf16[768,1152]{1,0:T(8,128)(2,1)S(1)}) custom-call(bf16[1152,768]{1,0:T(8,128)(2,1)S(1)} %get-tuple-element.256.d_ref, f32[6,4,576]{2,1,0:T(4,128)S(1)} %get-tuple-element.244.lse_ref, ...), custom_call_target="tpu_custom_call" | custom-call | flops 12230590464 | bytes 7077888 | tf_op jit(solution)/shard_map/attention_back_other/pallas_call | solution.py:460
  99.3 2.4 %collective-permute-done.12.rest_0_ = bf16[768,1152]{1,0:T(8,128)(2,1)S(1)} collective-permute-done((bf16[768,1152]{1,0:T(8,128)(2,1)S(1)}, bf16[768,1152]{1,0:T(8,128)(2,1)S(1)}, u32[]{:S(2)}, u32[]{:S(2)}) %collective-permute-start.12) | collective-permute-done | bytes 1769504 | tf_op jit(solution)/shard_map/ppermute | solution.py:986
  101.7 15.5 %attention_back_final.1 = (bf16[1152,384]{1,0:T(8,128)(2,1)S(1)}, bf16[1152,384]{1,0:T(8,128)(2,1)S(1)}, bf16[1152,384]{1,0:T(8,128)(2,1)S(1)}, bf16[2,96,1536]{...) custom-call(bf16[1152,768]{1,0:T(8,128)(2,1)S(1)} %get-tuple-element, ...), custom_call_target="tpu_custom_call" | custom-call | flops 12230590464 | bytes 7077888 | tf_op jit(solution)/shard_map/attention_back_final/pallas_call | solution.py:460
  117.2 0.6 collective-permute-start.15
  118.8 1.6 collective-permute-start.17
  120.5 11.7 %finish.1 = (f32[1152,768]{1,0:T(8,128)}, bf16[1152,768]{1,0:T(8,128)(2,1)}, f32[1,768]{1,0:T(1,128)S(1)}) custom-call(s32[2]{0:T(128)S(1)} %pad_add_fusion.me_ref, s32[4]{0:T(128)S(1)} %copy-done.1, f32[768]{0:T(1024)} %gain_hbm.7, f32[1152,768]{1,0:T(8,128)S(1)} %get-tuple-element.239.dh1_ref, bf16[1152,384]{1,0:T(8,128)(2,1)S(1)} %get-tuple-element.273.d_refs_0_, ...), custom_call_target="tpu_custom_call" | custom-call | flops 7700742144 | bytes 24182784 | tf_op jit(solution)/shard_map/finish/pallas_call | solution.py:725
  132.2 0.7 collective-permute-done.15.recv_a
  133.1 0.6 collective-permute-done.17.recv
  133.9 2.8 %collective-permute-start.24 = (bf16[48,3072]{1,0:T(8,128)(2,1)S(1)}, bf16[48,3072]{1,0:T(8,128)(2,1)S(1)}, u32[]{:S(2)}, u32[]{:S(2)}) collective-permute-start(bf16[48,3072]{1,0:T(8,128)(2,1)S(1)} %far_sum.1), channel_id=1, source_target_pairs={{0,16},{2,18},{4,20},{6,22},{8,24},{10,26},{12,28},{14,30},{16,0},... | collective-permute-start | bytes 884744 | tf_op jit(solution)/shard_map/ppermute | solution.py:825
  136.8 1.6 collective-permute-start.20
  138.4 1.5 collective-permute-start.21
  139.9 0.6 collective-permute-start.19
  140.6 7.2 %layer_output.1 = bf16[1152,768]{1,0:T(8,128)(2,1)} custom-call(s32[2]{0:T(128)S(1)} %pad_add_fusion.me_ref, s32[4]{0:T(128)S(1)} %copy-done.1, f32[1152,768]{1,0:T(8,128)} %get-tuple-element.297.h1_hbm, bf16[1024,768]{1,0:T(8,128)(2,1)} %wd_hbm_0_.1, bf16[1024,768]{1,0:T(8,128)(2,1)S(1)} %collective-permute-done.6.wd_hbm.wd_hbm_1_, ...), custom_call_target="tpu_custom_call", output_to_operand_aliasing={{}: (9, {})} | custom-call | flops 1811939328 | bytes 5013504 | tf_op jit(solution)/shard_map/layer_output/pallas_call | solution.py:784
  148.0 1.6 collective-permute-start.23
  150.5 2.5 %collective-permute-start.29 = (bf16[48,1536]{1,0:T(8,128)(2,1)S(1)}, bf16[48,1536]{1,0:T(8,128)(2,1)S(1)}, u32[]{:S(2)}, u32[]{:S(2)}) collective-permute-start(bf16[48,1536]{1,0:T(8,128)(2,1)S(1)} %get-tuple-element.311), channel_id=1, source_target_pairs={{0,24},{2,26},{4,28},{6,30},{8,16},{10,18},{12,20},{14,22},{16,8},... | collective-permute-start | bytes 442376 | tf_op jit(solution)/shard_map/ppermute | solution.py:825
  153.3 1.3 collective-permute-done.23.far_refs_0_
  154.6 6.7 %collective-permute-start.27 = (f32[2,768]{1,0:T(2,128)S(1)}, f32[2,768]{1,0:T(2,128)S(1)}, u32[]{:S(2)}, u32[]{:S(2)}) collective-permute-start(f32[2,768]{1,0:T(2,128)S(1)} %add.29), channel_id=1, source_target_pairs={{0,24},{2,26},{4,28},{6,30},{8,16},{10,18},{12,20},{14,22},{16,8},... | collective-permute-start | bytes 18440 | tf_op jit(solution)/shard_map/ppermute | solution.py:825
  162.0 0.8 pad_maximum_fusion.1
  162.8 0.7 fusion
  163.5 0.7 last_sum.1
  164.2 1.6 collective-permute-done.26
  165.8 0.6 slice_reduce_fusion
  (69 shorter events, 8.2 us)
Async XLA Ops:
  0.6 6.0 %collective-permute-start = (bf16[768,384]{1,0:T(8,128)(2,1)}, bf16[768,384]{1,0:T(8,128)(2,1)S(1)}, u32[]{:S(2)}, u32[]{:S(2)}) collective-permute-start(bf16[768,384]{1,0:T(8,128)(2,1)} %w_hbm_0_), channel_id=1, source_target_pairs={{0,1},{1,0},{2,3},{3,2},{4,5},{5,4},{6,7},{7,6},{8,9},{9,8},{10,11... | collective-permute-start | bytes 1769480 | tf_op jit(solution)/shard_map/ppermute | solution.py:986
  1.2 5.5 %collective-permute-start.1 = (bf16[768,384]{1,0:T(8,128)(2,1)}, bf16[768,384]{1,0:T(8,128)(2,1)S(1)}, u32[]{:S(2)}, u32[]{:S(2)}) collective-permute-start(bf16[768,384]{1,0:T(8,128)(2,1)} %w_hbm_1_), channel_id=1, source_target_pairs={{0,1},{1,0},{2,3},{3,2},{4,5},{5,4},{6,7},{7,6},{8,9},{9,8},{10,11... | collective-permute-start | bytes 1769480 | tf_op jit(solution)/shard_map/ppermute | solution.py:986
  1.2 5.4 %collective-permute-start.2 = (bf16[768,384]{1,0:T(8,128)(2,1)}, bf16[768,384]{1,0:T(8,128)(2,1)S(1)}, u32[]{:S(2)}, u32[]{:S(2)}) collective-permute-start(bf16[768,384]{1,0:T(8,128)(2,1)} %w_hbm_2_), channel_id=1, source_target_pairs={{0,1},{1,0},{2,3},{3,2},{4,5},{5,4},{6,7},{7,6},{8,9},{9,8},{10,11... | collective-permute-start | bytes 1769480 | tf_op jit(solution)/shard_map/ppermute | solution.py:986
  1.7 6.0 %collective-permute-start.3 = (bf16[384,768]{1,0:T(8,128)(2,1)}, bf16[384,768]{1,0:T(8,128)(2,1)S(1)}, u32[]{:S(2)}, u32[]{:S(2)}) collective-permute-start(bf16[384,768]{1,0:T(8,128)(2,1)} %wo_hbm_0_.3), channel_id=1, source_target_pairs={{0,1},{1,0},{2,3},{3,2},{4,5},{5,4},{6,7},{7,6},{8,9},{9,8},{10,11... | collective-permute-start | bytes 1769480 | tf_op jit(solution)/shard_map/ppermute | solution.py:986
  6.6 22.8 %collective-permute-start.4 = (bf16[768,1024]{1,0:T(8,128)(2,1)S(1)}, bf16[768,1024]{1,0:T(8,128)(2,1)S(1)}, u32[]{:S(2)}, u32[]{:S(2)}) collective-permute-start(bf16[768,1024]{1,0:T(8,128)(2,1)S(1)} %copy-done.5), channel_id=1, source_target_pairs={{0,1},{1,0},{2,3},{3,2},{4,5},{5,4},{6,7},{7,6},{8,9},{9,8},{10,11... | collective-permute-start | bytes 4718600 | tf_op jit(solution)/shard_map/ppermute | solution.py:986
  7.1 22.4 %collective-permute-start.5 = (bf16[768,1024]{1,0:T(8,128)(2,1)}, bf16[768,1024]{1,0:T(8,128)(2,1)S(1)}, u32[]{:S(2)}, u32[]{:S(2)}) collective-permute-start(bf16[768,1024]{1,0:T(8,128)(2,1)} %wu_hbm_0_), channel_id=1, source_target_pairs={{0,1},{1,0},{2,3},{3,2},{4,5},{5,4},{6,7},{7,6},{8,9},{9,8},{10,11... | collective-permute-start | bytes 4718600 | tf_op jit(solution)/shard_map/ppermute | solution.py:986
  7.2 22.3 %collective-permute-start.6 = (bf16[1024,768]{1,0:T(8,128)(2,1)S(1)}, bf16[1024,768]{1,0:T(8,128)(2,1)S(1)}, u32[]{:S(2)}, u32[]{:S(2)}) collective-permute-start(bf16[1024,768]{1,0:T(8,128)(2,1)S(1)} %copy-done.4), channel_id=1, source_target_pairs={{0,1},{1,0},{2,3},{3,2},{4,5},{5,4},{6,7},{7,6},{8,9},{9,8},{10,11... | collective-permute-start | bytes 4718600 | tf_op jit(solution)/shard_map/ppermute | solution.py:986
  29.5 8.0 %copy-start.2 = (bf16[1152,768]{1,0:T(8,128)(2,1)}, bf16[1152,768]{1,0:T(8,128)(2,1)S(1)}, u32[]{:S(2)}) copy-start(bf16[1152,768]{1,0:T(8,128)(2,1)S(1)} %get-tuple-element.230.o_ref) | copy-start | bytes 5308420
  37.4 7.9 %collective-permute-start.7 = (bf16[768,1536]{1,0:T(8,128)(2,1)S(1)}, bf16[768,1536]{1,0:T(8,128)(2,1)S(1)}, u32[]{:S(2)}, u32[]{:S(2)}) collective-permute-start(bf16[768,1536]{1,0:T(8,128)(2,1)S(1)} %get-tuple-element.184), channel_id=1, source_target_pairs={{0,1},{1,0},{2,3},{3,2},{4,5},{5,4},{6,7},{7,6},{8,9},{9,8},{10,11... | collective-permute-start | bytes 7077896 | tf_op jit(solution)/shard_map/ppermute | solution.py:986
  44.9 8.8 %collective-permute-start.8 = (bf16[768,1536]{1,0:T(8,128)(2,1)S(1)}, bf16[768,1536]{1,0:T(8,128)(2,1)S(1)}, u32[]{:S(2)}, u32[]{:S(2)}) collective-permute-start(bf16[768,1536]{1,0:T(8,128)(2,1)S(1)} %get-tuple-element.192), channel_id=1, source_target_pairs={{0,1},{1,0},{2,3},{3,2},{4,5},{5,4},{6,7},{7,6},{8,9},{9,8},{10,11... | collective-permute-start | bytes 7077896 | tf_op jit(solution)/shard_map/ppermute | solution.py:986
  53.6 12.8 %copy-start.3 = (bf16[1152,768]{1,0:T(8,128)(2,1)S(1)}, bf16[1152,768]{1,0:T(8,128)(2,1)}, u32[]{:S(2)}) copy-start(bf16[1152,768]{1,0:T(8,128)(2,1)} %copy-done.2) | copy-start | bytes 5308420
  62.3 35.4 %collective-permute-start.10 = (bf16[2,192,1536]{2,1,0:T(8,128)(2,1)S(1)}, bf16[2,192,1536]{2,1,0:T(8,128)(2,1)S(1)}, u32[]{:S(2)}, u32[]{:S(2)}) collective-permute-start(bf16[2,192,1536]{2,1,0:T(8,128)(2,1)S(1)} %get-tuple-element.254), channel_id=1, source_target_pairs={{0,2},{2,0},{4,6},{6,4},{8,10},{10,8},{12,14},{14,12},{16,18},{18,... | collective-permute-start | bytes 3538952 | tf_op jit(solution)/shard_map/ppermute | solution.py:825
  65.0 32.8 %collective-permute-start.11 = (bf16[2,192,1536]{2,1,0:T(8,128)(2,1)S(1)}, bf16[2,192,1536]{2,1,0:T(8,128)(2,1)S(1)}, u32[]{:S(2)}, u32[]{:S(2)}) collective-permute-start(bf16[2,192,1536]{2,1,0:T(8,128)(2,1)S(1)} %get-tuple-element.255), channel_id=1, source_target_pairs={{0,4},{2,6},{4,0},{6,2},{8,12},{10,14},{12,8},{14,10},{16,20},{18,... | collective-permute-start | bytes 3538952 | tf_op jit(solution)/shard_map/ppermute | solution.py:825
  82.1 15.7 %collective-permute-start.9 = (bf16[768,384]{1,0:T(8,128)(2,1)S(1)}, bf16[768,384]{1,0:T(8,128)(2,1)S(1)}, u32[]{:S(2)}, u32[]{:S(2)}) collective-permute-start(bf16[768,384]{1,0:T(8,128)(2,1)S(1)} %get-tuple-element.250), channel_id=1, source_target_pairs={{0,1},{1,0},{2,3},{3,2},{4,5},{5,4},{6,7},{7,6},{8,9},{9,8},{10,11... | collective-permute-start | bytes 1769480 | tf_op jit(solution)/shard_map/ppermute | solution.py:986
  97.8 3.9 %collective-permute-start.12 = (bf16[768,1152]{1,0:T(8,128)(2,1)S(1)}, bf16[768,1152]{1,0:T(8,128)(2,1)S(1)}, u32[]{:S(2)}, u32[]{:S(2)}) collective-permute-start(bf16[768,1152]{1,0:T(8,128)(2,1)S(1)} %get-tuple-element.257), channel_id=1, source_target_pairs={{0,1},{1,0},{2,3},{3,2},{4,5},{5,4},{6,7},{7,6},{8,9},{9,8},{10,11... | collective-permute-start | bytes 5308424 | tf_op jit(solution)/shard_map/ppermute | solution.py:986
  98.6 18.6 %collective-permute-start.13 = (bf16[192,1536]{1,0:T(8,128)(2,1)S(1)}, bf16[192,1536]{1,0:T(8,128)(2,1)S(1)}, u32[]{:S(2)}, u32[]{:S(2)}) collective-permute-start(bf16[192,1536]{1,0:T(8,128)(2,1)S(1)} %get-tuple-element.271), channel_id=1, source_target_pairs={{0,4},{2,6},{4,0},{6,2},{8,12},{10,14},{12,8},{14,10},{16,20},{18,... | collective-permute-start | bytes 1769480 | tf_op jit(solution)/shard_map/ppermute | solution.py:825
  99.2 18.0 %collective-permute-start.14 = (bf16[192,1536]{1,0:T(8,128)(2,1)S(1)}, bf16[192,1536]{1,0:T(8,128)(2,1)S(1)}, u32[]{:S(2)}, u32[]{:S(2)}) collective-permute-start(bf16[192,1536]{1,0:T(8,128)(2,1)S(1)} %get-tuple-element.272), channel_id=1, source_target_pairs={{0,2},{2,0},{4,6},{6,4},{8,10},{10,8},{12,14},{14,12},{16,18},{18,... | collective-permute-start | bytes 1769480 | tf_op jit(solution)/shard_map/ppermute | solution.py:825
  117.2 15.7 %collective-permute-start.15 = (bf16[2,96,1536]{2,1,0:T(8,128)(2,1)S(1)}, bf16[2,96,1536]{2,1,0:T(8,128)(2,1)S(1)}, u32[]{:S(2)}, u32[]{:S(2)}) collective-permute-start(bf16[2,96,1536]{2,1,0:T(8,128)(2,1)S(1)} %get-tuple-element.284), channel_id=1, source_target_pairs={{0,2},{2,0},{4,6},{6,4},{8,10},{10,8},{12,14},{14,12},{16,18},{18,... | collective-permute-start | bytes 1769480 | tf_op jit(solution)/shard_map/ppermute | solution.py:825
  117.8 15.3 %collective-permute-start.16 = (bf16[2,96,1536]{2,1,0:T(8,128)(2,1)S(1)}, bf16[2,96,1536]{2,1,0:T(8,128)(2,1)S(1)}, u32[]{:S(2)}, u32[]{:S(2)}) collective-permute-start(bf16[2,96,1536]{2,1,0:T(8,128)(2,1)S(1)} %get-tuple-element.285), channel_id=1, source_target_pairs={{0,4},{2,6},{4,0},{6,2},{8,12},{10,14},{12,8},{14,10},{16,20},{18,... | collective-permute-start | bytes 1769480 | tf_op jit(solution)/shard_map/ppermute | solution.py:825
  118.8 14.9 %collective-permute-start.17 = (bf16[2,48,3072]{2,1,0:T(8,128)(2,1)S(1)}, bf16[2,48,3072]{2,1,0:T(8,128)(2,1)S(1)}, u32[]{:S(2)}, u32[]{:S(2)}) collective-permute-start(bf16[2,48,3072]{2,1,0:T(8,128)(2,1)S(1)} %get-tuple-element.288), channel_id=1, source_target_pairs={{0,8},{2,10},{4,12},{6,14},{8,0},{10,2},{12,4},{14,6},{16,24},{18,... | collective-permute-start | bytes 1769480 | tf_op jit(solution)/shard_map/ppermute | solution.py:825
  133.7 6.2 %collective-permute-start.18 = (f32[2,768]{1,0:T(2,128)S(1)}, f32[2,768]{1,0:T(2,128)S(1)}, u32[]{:S(2)}, u32[]{:S(2)}) collective-permute-start(f32[2,768]{1,0:T(2,128)S(1)} %pad_maximum_fusion.2), channel_id=1, source_target_pairs={{0,1},{1,0},{2,3},{3,2},{4,5},{5,4},{6,7},{7,6},{8,9},{9,8},{10,11... | collective-permute-start | bytes 18440 | tf_op jit(solution)/shard_map/ppermute | solution.py:986
  133.9 19.4 %collective-permute-start.24 = (bf16[48,3072]{1,0:T(8,128)(2,1)S(1)}, bf16[48,3072]{1,0:T(8,128)(2,1)S(1)}, u32[]{:S(2)}, u32[]{:S(2)}) collective-permute-start(bf16[48,3072]{1,0:T(8,128)(2,1)S(1)} %far_sum.1), channel_id=1, source_target_pairs={{0,16},{2,18},{4,20},{6,22},{8,24},{10,26},{12,28},{14,30},{16,0},... | collective-permute-start | bytes 884744 | tf_op jit(solution)/shard_map/ppermute | solution.py:825
  136.8 10.9 %collective-permute-start.20 = (bf16[96,1536]{1,0:T(8,128)(2,1)S(1)}, bf16[96,1536]{1,0:T(8,128)(2,1)S(1)}, u32[]{:S(2)}, u32[]{:S(2)}) collective-permute-start(bf16[96,1536]{1,0:T(8,128)(2,1)S(1)} %get-tuple-element.295), channel_id=1, source_target_pairs={{0,4},{2,6},{4,0},{6,2},{8,12},{10,14},{12,8},{14,10},{16,20},{18,... | collective-permute-start | bytes 884744 | tf_op jit(solution)/shard_map/ppermute | solution.py:825
  138.4 9.3 %collective-permute-start.21 = (bf16[96,1536]{1,0:T(8,128)(2,1)S(1)}, bf16[96,1536]{1,0:T(8,128)(2,1)S(1)}, u32[]{:S(2)}, u32[]{:S(2)}) collective-permute-start(bf16[96,1536]{1,0:T(8,128)(2,1)S(1)} %get-tuple-element.296), channel_id=1, source_target_pairs={{0,2},{2,0},{4,6},{6,4},{8,10},{10,8},{12,14},{14,12},{16,18},{18,... | collective-permute-start | bytes 884744 | tf_op jit(solution)/shard_map/ppermute | solution.py:825
  139.9 7.8 %collective-permute-start.19 = (f32[2,768]{1,0:T(2,128)S(1)}, f32[2,768]{1,0:T(2,128)S(1)}, u32[]{:S(2)}, u32[]{:S(2)}) collective-permute-start(f32[2,768]{1,0:T(2,128)S(1)} %fusion.1), channel_id=1, source_target_pairs={{0,2},{2,0},{4,6},{6,4},{8,10},{10,8},{12,14},{14,12},{16,18},{18,... | collective-permute-start | bytes 18440 | tf_op jit(solution)/shard_map/ppermute | solution.py:825
  148.0 6.6 %collective-permute-start.23 = (bf16[48,1536]{1,0:T(8,128)(2,1)S(1)}, bf16[48,1536]{1,0:T(8,128)(2,1)S(1)}, u32[]{:S(2)}, u32[]{:S(2)}) collective-permute-start(bf16[48,1536]{1,0:T(8,128)(2,1)S(1)} %get-tuple-element.304), channel_id=1, source_target_pairs={{0,8},{2,10},{4,12},{6,14},{8,0},{10,2},{12,4},{14,6},{16,24},{18,... | collective-permute-start | bytes 442376 | tf_op jit(solution)/shard_map/ppermute | solution.py:825
  149.6 3.6 %collective-permute-start.22 = (f32[2,768]{1,0:T(2,128)S(1)}, f32[2,768]{1,0:T(2,128)S(1)}, u32[]{:S(2)}, u32[]{:S(2)}) collective-permute-start(f32[2,768]{1,0:T(2,128)S(1)} %fusion.4), channel_id=1, source_target_pairs={{0,4},{2,6},{4,0},{6,2},{8,12},{10,14},{12,8},{14,10},{16,20},{18,... | collective-permute-start | bytes 18440 | tf_op jit(solution)/shard_map/ppermute | solution.py:825
  150.1 13.4 %collective-permute-start.28 = (bf16[48,1536]{1,0:T(8,128)(2,1)S(1)}, bf16[48,1536]{1,0:T(8,128)(2,1)S(1)}, u32[]{:S(2)}, u32[]{:S(2)}) collective-permute-start(bf16[48,1536]{1,0:T(8,128)(2,1)S(1)} %get-tuple-element.310), channel_id=1, source_target_pairs={{0,16},{2,18},{4,20},{6,22},{8,24},{10,26},{12,28},{14,30},{16,0},... | collective-permute-start | bytes 442376 | tf_op jit(solution)/shard_map/ppermute | solution.py:825
  150.5 13.0 %collective-permute-start.29 = (bf16[48,1536]{1,0:T(8,128)(2,1)S(1)}, bf16[48,1536]{1,0:T(8,128)(2,1)S(1)}, u32[]{:S(2)}, u32[]{:S(2)}) collective-permute-start(bf16[48,1536]{1,0:T(8,128)(2,1)S(1)} %get-tuple-element.311), channel_id=1, source_target_pairs={{0,24},{2,26},{4,28},{6,30},{8,16},{10,18},{12,20},{14,22},{16,8},... | collective-permute-start | bytes 442376 | tf_op jit(solution)/shard_map/ppermute | solution.py:825
  154.6 9.7 %collective-permute-start.27 = (f32[2,768]{1,0:T(2,128)S(1)}, f32[2,768]{1,0:T(2,128)S(1)}, u32[]{:S(2)}, u32[]{:S(2)}) collective-permute-start(f32[2,768]{1,0:T(2,128)S(1)} %add.29), channel_id=1, source_target_pairs={{0,24},{2,26},{4,28},{6,30},{8,16},{10,18},{12,20},{14,22},{16,8},... | collective-permute-start | bytes 18440 | tf_op jit(solution)/shard_map/ppermute | solution.py:825
  161.3 4.5 %collective-permute-start.26 = (f32[2,768]{1,0:T(2,128)S(1)}, f32[2,768]{1,0:T(2,128)S(1)}, u32[]{:S(2)}, u32[]{:S(2)}) collective-permute-start(f32[2,768]{1,0:T(2,128)S(1)} %add.29), channel_id=1, source_target_pairs={{0,16},{2,18},{4,20},{6,22},{8,24},{10,26},{12,28},{14,30},{16,0},... | collective-permute-start | bytes 18440 | tf_op jit(solution)/shard_map/ppermute | solution.py:825
  161.3 4.5 %collective-permute-start.25 = (f32[2,768]{1,0:T(2,128)S(1)}, f32[2,768]{1,0:T(2,128)S(1)}, u32[]{:S(2)}, u32[]{:S(2)}) collective-permute-start(f32[2,768]{1,0:T(2,128)S(1)} %add.29), channel_id=1, source_target_pairs={{0,8},{2,10},{4,12},{6,14},{8,0},{10,2},{12,4},{14,6},{16,24},{18,... | collective-permute-start | bytes 18440 | tf_op jit(solution)/shard_map/ppermute | solution.py:825
  (4 other events, 12.8 us)

commit v4 on v3

--- a/solution.py
+++ b/solution.py
@@ -1044,8 +1044,7 @@
     gains, last_q, output = fence((gains, last_q, output))
     kept_q, far_q = third_rows_swaps(q_piece, recv_q, last_q, dp)
     gains = swap_sum(gains, dp, (2,))
-    gains, first_q, far = fence((gains, far_q[0], far))
-    far_q = (first_q, *far_q[1:])
+    gains, far = fence((gains, far))
     far_bits = [1 << bit for bit in range(2, dp.bit_length() - 1)]
     for bits in (far_bits,) if two_steps else ((bit,) for bit in far_bits):
         gains = swap_sum(gains, dp, bits)

time: 170 us -> 169 us (level)
  starting transfers between devices: 29.8 us -> 27.4 us
    ppermute x18, starting transfers between devices: 26.4 us -> 23.9 us  [swap_dp(): return lax.ppermute(array, 'dp', [(i, i ^ relative) for i in range(dp)])]
  transfers between devices with their start and end apart: 30 -> 30, of which waited for: 7 -> 6; matrix products, arithmetic and copies ran while one was open for 1% -> 1% of each run, Pallas kernels for 65% -> 65%
where the time goes in v4:
time: 169 us; the launch traced here: 166 us
  Pallas kernels  125 us (74%)
  starting transfers between devices  27.4 us (16%)
  waiting for transfers between devices  8.52 us (5%)
    pallas_call x4, Pallas kernels, ffn(): pl.pallas_call(functools.partial(ffn_kernel, final, chunk * CHUNK, chunk...  32.1 us
    pallas_call x2, Pallas kernels, attention_back(): pl.pallas_call(functools.partial(attention_back_kernel, final, first), in...  31.1 us
    ppermute x18, starting transfers between devices, swap_dp(): return lax.ppermute(array, 'dp', [(i, i ^ relative) for i in range(dp)])  23.9 us
    pallas_call x1, Pallas kernels, front(): pl.pallas_call(functools.partial(front_kernel, dp), in_specs=[SCALAR, ANY...  21.8 us
    pallas_call x1, Pallas kernels, ffn_back(): pl.pallas_call(functools.partial(ffn_back_kernel, dp), in_specs=[SCALAR,...  15.6 us
    pallas_call x1, Pallas kernels, finish(): pl.pallas_call(functools.partial(finish_kernel, count // SLOTS), in_specs...  11.7 us
    pallas_call x1, Pallas kernels, layer_output(): pl.pallas_call(functools.partial(output_kernel, count // SLOTS, blocks),...  7.16 us
    ppermute x18, waiting for transfers between devices, swap_dp(): return lax.ppermute(array, 'dp', [(i, i ^ relative) for i in range(dp)])  6.14 us
  transfers between devices with their start and end apart: 30, of which 6 were waited for; matrix products, arithmetic and copies ran while one was open for 1% of the time, Pallas kernels for 65%

profile of v4, /device:TPU:0, one launch (start us, length us, event | category | flops | bytes accessed | tf_op | source)
XLA Modules:
  0.0 165.8 jit_solution(7349606634405524494)
XLA Ops:
  1.8 0.7 copy-done
  2.5 4.1 %prepare.1 = (bf16[1152,768]{1,0:T(8,128)(2,1)S(1)}, bf16[768,1152]{1,0:T(8,128)(2,1)S(1)}, bf16[1152,768]{1,0:T(8,128)(2,1)S(1)}, bf16[768,1152]{1,0:T(8,128)(2,1)S(1)}) custom-call(s32[2]{0:T(128)S(1)} %pad_add_fusion.me_ref, s32[4]{0:T(128)S(1)} %copy-done, f32[768]{0:T(1024)} %gain_hbm.7, bf16[1152,768]{1,0:T(8,128)(2,1)} %x_hbm.5, bf16[1152,768]{1,0:T(8,128)(2,1)} %cot_hbm.1), custom_call_target="tpu_custom_call" | custom-call | flops 8847360 | bytes 10616832 | tf_op jit(solution)/shard_map/prepare/pallas_call | solution.py:161
  7.7 21.8 %front.1 = (bf16[1152,768]{1,0:T(8,128)(2,1)}, bf16[1152,768]{1,0:T(8,128)(2,1)}, bf16[1152,768]{1,0:T(8,128)(2,1)}, f32[1152,768]{1,0:T(8,128)}, bf16[1152,768]...) custom-call(s32[2]{0:T(128)S(1)} %pad_add_fusion.me_ref, ...), custom_call_target="tpu_custom_call" | custom-call | flops 13589544960 | bytes 21233664 | tf_op jit(solution)/shard_map/front/pallas_call | solution.py:319
  29.5 7.9 %ffn_other.2 = (bf16[1152,512]{1,0:T(8,128)(2,1)}, bf16[1152,512]{1,0:T(8,128)(2,1)S(1)}, bf16[1152,512]{1,0:T(8,128)(2,1)S(1)}, bf16[768,1536]{1,0:T(8,128)(2,1)S(1)}) custom-call(bf16[1152,768]{1,0:T(8,128)(2,1)S(1)} %get-tuple-element.209.nf_ref, bf16[768,1152]{1,0:T(8,128)(2,1)S(1)} %get-tuple-element.173.nft_ref, ...), custom_call_target="tpu_custom_call" | custom-call | flops 5435817984 | bytes 11796480 | tf_op jit(solution)/shard_map/ffn_other/pallas_call | solution.py:565
  37.6 7.3 %ffn_other.3 = (bf16[1152,512]{1,0:T(8,128)(2,1)}, bf16[1152,512]{1,0:T(8,128)(2,1)S(1)}, bf16[1152,512]{1,0:T(8,128)(2,1)S(1)}, bf16[768,1536]{1,0:T(8,128)(2,1)S(1)}) custom-call(bf16[1152,768]{1,0:T(8,128)(2,1)S(1)} %get-tuple-element.209.nf_ref, bf16[768,1152]{1,0:T(8,128)(2,1)S(1)} %get-tuple-element.173.nft_ref, ...), custom_call_target="tpu_custom_call" | custom-call | flops 5435817984 | bytes 11796480 | tf_op jit(solution)/shard_map/ffn_other/pallas_call | solution.py:565
  45.4 8.2 %ffn_final.2 = (bf16[1152,512]{1,0:T(8,128)(2,1)}, bf16[1152,512]{1,0:T(8,128)(2,1)S(1)}, bf16[1152,512]{1,0:T(8,128)(2,1)S(1)}, bf16[2,192,1536]{2,1,0:T(8,128)...) custom-call(bf16[1152,768]{1,0:T(8,128)(2,1)S(1)} %get-tuple-element, ...), custom_call_target="tpu_custom_call" | custom-call | flops 5435817984 | bytes 11796480 | tf_op jit(solution)/shard_map/ffn_final/pallas_call | solution.py:565
  53.7 8.7 %ffn_final.3 = (bf16[1152,512]{1,0:T(8,128)(2,1)}, bf16[1152,512]{1,0:T(8,128)(2,1)S(1)}, bf16[1152,512]{1,0:T(8,128)(2,1)S(1)}, bf16[2,192,1536]{2,1,0:T(8,128)...) custom-call(bf16[1152,768]{1,0:T(8,128)(2,1)S(1)} %get-tuple-element, ...), custom_call_target="tpu_custom_call", output_to_operand_aliasing={{3}: (8, {}), {4}: (9, {}), {5}: (10, {}), {6}: (11, {})} | custom-call | flops 5435817984 | bytes 11796480 | tf_op jit(solution)/shard_map/ffn_final/pallas_call | solution.py:565
  62.3 2.6 %collective-permute-start.10 = (bf16[2,192,1536]{2,1,0:T(8,128)(2,1)S(1)}, bf16[2,192,1536]{2,1,0:T(8,128)(2,1)S(1)}, u32[]{:S(2)}, u32[]{:S(2)}) collective-permute-start(bf16[2,192,1536]{2,1,0:T(8,128)(2,1)S(1)} %get-tuple-element.253), channel_id=1, source_target_pairs={{0,2},{2,0},{4,6},{6,4},{8,10},{10,8},{12,14},{14,12},{16,18},{18,... | collective-permute-start | bytes 3538952 | tf_op jit(solution)/shard_map/ppermute | solution.py:825
  65.0 1.5 collective-permute-start.11
  66.5 15.6 %ffn_back.1 = (f32[1152,768]{1,0:T(8,128)S(1)}, bf16[1152,768]{1,0:T(8,128)(2,1)S(1)}, f32[1,768]{1,0:T(1,128)S(1)}, bf16[768,384]{1,0:T(8,128)(2,1)S(1)}, bf16[768,384]{1,0:T(8,128)(2,1)S(1)}) custom-call(s32[2]{0:T(128)S(1)} %pad_add_fusion.me_ref, f32[768]{0:T(1024)} %gain_hbm.6, f32[1152,768]{1,0:T(8,128)} %get-tuple-element.296.h1_hbm, ...), custom_call_target="tpu_custom_call" | custom-call | flops 9965666304 | bytes 27131904 | tf_op jit(solution)/shard_map/ffn_back/pallas_call | solution.py:643
  82.1 15.6 %attention_back_other.1 = (bf16[1152,384]{1,0:T(8,128)(2,1)S(1)}, bf16[1152,384]{1,0:T(8,128)(2,1)S(1)}, bf16[1152,384]{1,0:T(8,128)(2,1)S(1)}, bf16[768,1152]{1,0:T(8,128)(2,1)S(1)}) custom-call(bf16[1152,768]{1,0:T(8,128)(2,1)S(1)} %get-tuple-element.255.d_ref, f32[6,4,576]{2,1,0:T(4,128)S(1)} %get-tuple-element.243.lse_ref, ...), custom_call_target="tpu_custom_call" | custom-call | flops 12230590464 | bytes 7077888 | tf_op jit(solution)/shard_map/attention_back_other/pallas_call | solution.py:460
  99.3 2.4 %collective-permute-done.12.rest_0_ = bf16[768,1152]{1,0:T(8,128)(2,1)S(1)} collective-permute-done((bf16[768,1152]{1,0:T(8,128)(2,1)S(1)}, bf16[768,1152]{1,0:T(8,128)(2,1)S(1)}, u32[]{:S(2)}, u32[]{:S(2)}) %collective-permute-start.12) | collective-permute-done | bytes 1769504 | tf_op jit(solution)/shard_map/ppermute | solution.py:986
  101.7 15.5 %attention_back_final.1 = (bf16[1152,384]{1,0:T(8,128)(2,1)S(1)}, bf16[1152,384]{1,0:T(8,128)(2,1)S(1)}, bf16[1152,384]{1,0:T(8,128)(2,1)S(1)}, bf16[2,96,1536]{...) custom-call(bf16[1152,768]{1,0:T(8,128)(2,1)S(1)} %get-tuple-element, ...), custom_call_target="tpu_custom_call" | custom-call | flops 12230590464 | bytes 7077888 | tf_op jit(solution)/shard_map/attention_back_final/pallas_call | solution.py:460
  117.2 0.6 collective-permute-start.15
  118.8 1.6 collective-permute-start.17
  120.5 11.7 %finish.1 = (f32[1152,768]{1,0:T(8,128)}, bf16[1152,768]{1,0:T(8,128)(2,1)}, f32[1,768]{1,0:T(1,128)S(1)}) custom-call(s32[2]{0:T(128)S(1)} %pad_add_fusion.me_ref, s32[4]{0:T(128)S(1)} %copy-done.1, f32[768]{0:T(1024)} %gain_hbm.7, f32[1152,768]{1,0:T(8,128)S(1)} %get-tuple-element.238.dh1_ref, bf16[1152,384]{1,0:T(8,128)(2,1)S(1)} %get-tuple-element.272.d_refs_0_, ...), custom_call_target="tpu_custom_call" | custom-call | flops 7700742144 | bytes 24182784 | tf_op jit(solution)/shard_map/finish/pallas_call | solution.py:725
  132.2 0.7 collective-permute-done.15.recv_a
  133.9 2.8 %collective-permute-start.23 = (bf16[48,3072]{1,0:T(8,128)(2,1)S(1)}, bf16[48,3072]{1,0:T(8,128)(2,1)S(1)}, u32[]{:S(2)}, u32[]{:S(2)}) collective-permute-start(bf16[48,3072]{1,0:T(8,128)(2,1)S(1)} %far_sum.1), channel_id=1, source_target_pairs={{0,16},{2,18},{4,20},{6,22},{8,24},{10,26},{12,28},{14,30},{16,0},... | collective-permute-start | bytes 884744 | tf_op jit(solution)/shard_map/ppermute | solution.py:825
  136.8 1.6 collective-permute-start.20
  138.4 1.5 collective-permute-start.21
  139.9 0.6 collective-permute-start.19
  140.6 7.2 %layer_output.1 = bf16[1152,768]{1,0:T(8,128)(2,1)} custom-call(s32[2]{0:T(128)S(1)} %pad_add_fusion.me_ref, s32[4]{0:T(128)S(1)} %copy-done.1, f32[1152,768]{1,0:T(8,128)} %get-tuple-element.296.h1_hbm, bf16[1024,768]{1,0:T(8,128)(2,1)} %wd_hbm_0_.1, bf16[1024,768]{1,0:T(8,128)(2,1)S(1)} %collective-permute-done.6.wd_hbm.wd_hbm_1_, ...), custom_call_target="tpu_custom_call", output_to_operand_aliasing={{}: (9, {})} | custom-call | flops 1811939328 | bytes 5013504 | tf_op jit(solution)/shard_map/layer_output/pallas_call | solution.py:784
  148.5 1.7 collective-permute-start.27
  150.5 0.9 collective-permute-done.22
  151.5 2.9 %collective-permute-start.26 = (f32[2,768]{1,0:T(2,128)S(1)}, f32[2,768]{1,0:T(2,128)S(1)}, u32[]{:S(2)}, u32[]{:S(2)}) collective-permute-start(f32[2,768]{1,0:T(2,128)S(1)} %add.29), channel_id=1, source_target_pairs={{0,24},{2,26},{4,28},{6,30},{8,16},{10,18},{12,20},{14,22},{16,8},... | collective-permute-start | bytes 18440 | tf_op jit(solution)/shard_map/ppermute | solution.py:825
  154.6 1.3 collective-permute-start.24
  156.1 0.8 pad_maximum_fusion.1
  156.9 0.7 fusion
  157.6 2.8 %collective-permute-start.29 = (bf16[48,1536]{1,0:T(8,128)(2,1)S(1)}, bf16[48,1536]{1,0:T(8,128)(2,1)S(1)}, u32[]{:S(2)}, u32[]{:S(2)}) collective-permute-start(bf16[48,1536]{1,0:T(8,128)(2,1)S(1)} %get-tuple-element.309), channel_id=1, source_target_pairs={{0,24},{2,26},{4,28},{6,30},{8,16},{10,18},{12,20},{14,22},{16,8},... | collective-permute-start | bytes 442376 | tf_op jit(solution)/shard_map/ppermute | solution.py:825
  160.4 0.6 slice_reduce_fusion
  161.1 3.6 %collective-permute-done.29.far_refs_2_ = bf16[48,1536]{1,0:T(8,128)(2,1)S(1)} collective-permute-done((bf16[48,1536]{1,0:T(8,128)(2,1)S(1)}, bf16[48,1536]{1,0:T(8,128)(2,1)S(1)}, u32[]{:S(2)}, u32[]{:S(2)}) %collective-permute-start.29) | collective-permute-done | bytes 147488 | tf_op jit(solution)/shard_map/ppermute | solution.py:825
  164.7 0.7 last_sum.1
  (69 shorter events, 8.2 us)
Async XLA Ops:
  0.6 6.0 %collective-permute-start = (bf16[768,384]{1,0:T(8,128)(2,1)}, bf16[768,384]{1,0:T(8,128)(2,1)S(1)}, u32[]{:S(2)}, u32[]{:S(2)}) collective-permute-start(bf16[768,384]{1,0:T(8,128)(2,1)} %w_hbm_0_), channel_id=1, source_target_pairs={{0,1},{1,0},{2,3},{3,2},{4,5},{5,4},{6,7},{7,6},{8,9},{9,8},{10,11... | collective-permute-start | bytes 1769480 | tf_op jit(solution)/shard_map/ppermute | solution.py:986
  1.2 5.5 %collective-permute-start.1 = (bf16[768,384]{1,0:T(8,128)(2,1)}, bf16[768,384]{1,0:T(8,128)(2,1)S(1)}, u32[]{:S(2)}, u32[]{:S(2)}) collective-permute-start(bf16[768,384]{1,0:T(8,128)(2,1)} %w_hbm_1_), channel_id=1, source_target_pairs={{0,1},{1,0},{2,3},{3,2},{4,5},{5,4},{6,7},{7,6},{8,9},{9,8},{10,11... | collective-permute-start | bytes 1769480 | tf_op jit(solution)/shard_map/ppermute | solution.py:986
  1.2 5.4 %collective-permute-start.2 = (bf16[768,384]{1,0:T(8,128)(2,1)}, bf16[768,384]{1,0:T(8,128)(2,1)S(1)}, u32[]{:S(2)}, u32[]{:S(2)}) collective-permute-start(bf16[768,384]{1,0:T(8,128)(2,1)} %w_hbm_2_), channel_id=1, source_target_pairs={{0,1},{1,0},{2,3},{3,2},{4,5},{5,4},{6,7},{7,6},{8,9},{9,8},{10,11... | collective-permute-start | bytes 1769480 | tf_op jit(solution)/shard_map/ppermute | solution.py:986
  1.7 6.0 %collective-permute-start.3 = (bf16[384,768]{1,0:T(8,128)(2,1)}, bf16[384,768]{1,0:T(8,128)(2,1)S(1)}, u32[]{:S(2)}, u32[]{:S(2)}) collective-permute-start(bf16[384,768]{1,0:T(8,128)(2,1)} %wo_hbm_0_.3), channel_id=1, source_target_pairs={{0,1},{1,0},{2,3},{3,2},{4,5},{5,4},{6,7},{7,6},{8,9},{9,8},{10,11... | collective-permute-start | bytes 1769480 | tf_op jit(solution)/shard_map/ppermute | solution.py:986
  6.6 22.8 %collective-permute-start.4 = (bf16[768,1024]{1,0:T(8,128)(2,1)S(1)}, bf16[768,1024]{1,0:T(8,128)(2,1)S(1)}, u32[]{:S(2)}, u32[]{:S(2)}) collective-permute-start(bf16[768,1024]{1,0:T(8,128)(2,1)S(1)} %copy-done.5), channel_id=1, source_target_pairs={{0,1},{1,0},{2,3},{3,2},{4,5},{5,4},{6,7},{7,6},{8,9},{9,8},{10,11... | collective-permute-start | bytes 4718600 | tf_op jit(solution)/shard_map/ppermute | solution.py:986
  7.1 22.4 %collective-permute-start.5 = (bf16[768,1024]{1,0:T(8,128)(2,1)}, bf16[768,1024]{1,0:T(8,128)(2,1)S(1)}, u32[]{:S(2)}, u32[]{:S(2)}) collective-permute-start(bf16[768,1024]{1,0:T(8,128)(2,1)} %wu_hbm_0_), channel_id=1, source_target_pairs={{0,1},{1,0},{2,3},{3,2},{4,5},{5,4},{6,7},{7,6},{8,9},{9,8},{10,11... | collective-permute-start | bytes 4718600 | tf_op jit(solution)/shard_map/ppermute | solution.py:986
  7.2 22.3 %collective-permute-start.6 = (bf16[1024,768]{1,0:T(8,128)(2,1)S(1)}, bf16[1024,768]{1,0:T(8,128)(2,1)S(1)}, u32[]{:S(2)}, u32[]{:S(2)}) collective-permute-start(bf16[1024,768]{1,0:T(8,128)(2,1)S(1)} %copy-done.4), channel_id=1, source_target_pairs={{0,1},{1,0},{2,3},{3,2},{4,5},{5,4},{6,7},{7,6},{8,9},{9,8},{10,11... | collective-permute-start | bytes 4718600 | tf_op jit(solution)/shard_map/ppermute | solution.py:986
  29.5 8.0 %copy-start.2 = (bf16[1152,768]{1,0:T(8,128)(2,1)}, bf16[1152,768]{1,0:T(8,128)(2,1)S(1)}, u32[]{:S(2)}) copy-start(bf16[1152,768]{1,0:T(8,128)(2,1)S(1)} %get-tuple-element.229.o_ref) | copy-start | bytes 5308420
  37.4 7.9 %collective-permute-start.7 = (bf16[768,1536]{1,0:T(8,128)(2,1)S(1)}, bf16[768,1536]{1,0:T(8,128)(2,1)S(1)}, u32[]{:S(2)}, u32[]{:S(2)}) collective-permute-start(bf16[768,1536]{1,0:T(8,128)(2,1)S(1)} %get-tuple-element.183), channel_id=1, source_target_pairs={{0,1},{1,0},{2,3},{3,2},{4,5},{5,4},{6,7},{7,6},{8,9},{9,8},{10,11... | collective-permute-start | bytes 7077896 | tf_op jit(solution)/shard_map/ppermute | solution.py:986
  44.9 8.8 %collective-permute-start.8 = (bf16[768,1536]{1,0:T(8,128)(2,1)S(1)}, bf16[768,1536]{1,0:T(8,128)(2,1)S(1)}, u32[]{:S(2)}, u32[]{:S(2)}) collective-permute-start(bf16[768,1536]{1,0:T(8,128)(2,1)S(1)} %get-tuple-element.191), channel_id=1, source_target_pairs={{0,1},{1,0},{2,3},{3,2},{4,5},{5,4},{6,7},{7,6},{8,9},{9,8},{10,11... | collective-permute-start | bytes 7077896 | tf_op jit(solution)/shard_map/ppermute | solution.py:986
  53.6 12.8 %copy-start.3 = (bf16[1152,768]{1,0:T(8,128)(2,1)S(1)}, bf16[1152,768]{1,0:T(8,128)(2,1)}, u32[]{:S(2)}) copy-start(bf16[1152,768]{1,0:T(8,128)(2,1)} %copy-done.2) | copy-start | bytes 5308420
  62.3 35.4 %collective-permute-start.10 = (bf16[2,192,1536]{2,1,0:T(8,128)(2,1)S(1)}, bf16[2,192,1536]{2,1,0:T(8,128)(2,1)S(1)}, u32[]{:S(2)}, u32[]{:S(2)}) collective-permute-start(bf16[2,192,1536]{2,1,0:T(8,128)(2,1)S(1)} %get-tuple-element.253), channel_id=1, source_target_pairs={{0,2},{2,0},{4,6},{6,4},{8,10},{10,8},{12,14},{14,12},{16,18},{18,... | collective-permute-start | bytes 3538952 | tf_op jit(solution)/shard_map/ppermute | solution.py:825
  65.0 32.8 %collective-permute-start.11 = (bf16[2,192,1536]{2,1,0:T(8,128)(2,1)S(1)}, bf16[2,192,1536]{2,1,0:T(8,128)(2,1)S(1)}, u32[]{:S(2)}, u32[]{:S(2)}) collective-permute-start(bf16[2,192,1536]{2,1,0:T(8,128)(2,1)S(1)} %get-tuple-element.254), channel_id=1, source_target_pairs={{0,4},{2,6},{4,0},{6,2},{8,12},{10,14},{12,8},{14,10},{16,20},{18,... | collective-permute-start | bytes 3538952 | tf_op jit(solution)/shard_map/ppermute | solution.py:825
  82.1 15.7 %collective-permute-start.9 = (bf16[768,384]{1,0:T(8,128)(2,1)S(1)}, bf16[768,384]{1,0:T(8,128)(2,1)S(1)}, u32[]{:S(2)}, u32[]{:S(2)}) collective-permute-start(bf16[768,384]{1,0:T(8,128)(2,1)S(1)} %get-tuple-element.249), channel_id=1, source_target_pairs={{0,1},{1,0},{2,3},{3,2},{4,5},{5,4},{6,7},{7,6},{8,9},{9,8},{10,11... | collective-permute-start | bytes 1769480 | tf_op jit(solution)/shard_map/ppermute | solution.py:986
  97.8 3.9 %collective-permute-start.12 = (bf16[768,1152]{1,0:T(8,128)(2,1)S(1)}, bf16[768,1152]{1,0:T(8,128)(2,1)S(1)}, u32[]{:S(2)}, u32[]{:S(2)}) collective-permute-start(bf16[768,1152]{1,0:T(8,128)(2,1)S(1)} %get-tuple-element.256), channel_id=1, source_target_pairs={{0,1},{1,0},{2,3},{3,2},{4,5},{5,4},{6,7},{7,6},{8,9},{9,8},{10,11... | collective-permute-start | bytes 5308424 | tf_op jit(solution)/shard_map/ppermute | solution.py:986
  98.6 18.6 %collective-permute-start.13 = (bf16[192,1536]{1,0:T(8,128)(2,1)S(1)}, bf16[192,1536]{1,0:T(8,128)(2,1)S(1)}, u32[]{:S(2)}, u32[]{:S(2)}) collective-permute-start(bf16[192,1536]{1,0:T(8,128)(2,1)S(1)} %get-tuple-element.270), channel_id=1, source_target_pairs={{0,4},{2,6},{4,0},{6,2},{8,12},{10,14},{12,8},{14,10},{16,20},{18,... | collective-permute-start | bytes 1769480 | tf_op jit(solution)/shard_map/ppermute | solution.py:825
  99.2 18.0 %collective-permute-start.14 = (bf16[192,1536]{1,0:T(8,128)(2,1)S(1)}, bf16[192,1536]{1,0:T(8,128)(2,1)S(1)}, u32[]{:S(2)}, u32[]{:S(2)}) collective-permute-start(bf16[192,1536]{1,0:T(8,128)(2,1)S(1)} %get-tuple-element.271), channel_id=1, source_target_pairs={{0,2},{2,0},{4,6},{6,4},{8,10},{10,8},{12,14},{14,12},{16,18},{18,... | collective-permute-start | bytes 1769480 | tf_op jit(solution)/shard_map/ppermute | solution.py:825
  117.2 15.7 %collective-permute-start.15 = (bf16[2,96,1536]{2,1,0:T(8,128)(2,1)S(1)}, bf16[2,96,1536]{2,1,0:T(8,128)(2,1)S(1)}, u32[]{:S(2)}, u32[]{:S(2)}) collective-permute-start(bf16[2,96,1536]{2,1,0:T(8,128)(2,1)S(1)} %get-tuple-element.283), channel_id=1, source_target_pairs={{0,2},{2,0},{4,6},{6,4},{8,10},{10,8},{12,14},{14,12},{16,18},{18,... | collective-permute-start | bytes 1769480 | tf_op jit(solution)/shard_map/ppermute | solution.py:825
  117.8 15.3 %collective-permute-start.16 = (bf16[2,96,1536]{2,1,0:T(8,128)(2,1)S(1)}, bf16[2,96,1536]{2,1,0:T(8,128)(2,1)S(1)}, u32[]{:S(2)}, u32[]{:S(2)}) collective-permute-start(bf16[2,96,1536]{2,1,0:T(8,128)(2,1)S(1)} %get-tuple-element.284), channel_id=1, source_target_pairs={{0,4},{2,6},{4,0},{6,2},{8,12},{10,14},{12,8},{14,10},{16,20},{18,... | collective-permute-start | bytes 1769480 | tf_op jit(solution)/shard_map/ppermute | solution.py:825
  118.8 14.9 %collective-permute-start.17 = (bf16[2,48,3072]{2,1,0:T(8,128)(2,1)S(1)}, bf16[2,48,3072]{2,1,0:T(8,128)(2,1)S(1)}, u32[]{:S(2)}, u32[]{:S(2)}) collective-permute-start(bf16[2,48,3072]{2,1,0:T(8,128)(2,1)S(1)} %get-tuple-element.287), channel_id=1, source_target_pairs={{0,8},{2,10},{4,12},{6,14},{8,0},{10,2},{12,4},{14,6},{16,24},{18,... | collective-permute-start | bytes 1769480 | tf_op jit(solution)/shard_map/ppermute | solution.py:825
  133.7 6.2 %collective-permute-start.18 = (f32[2,768]{1,0:T(2,128)S(1)}, f32[2,768]{1,0:T(2,128)S(1)}, u32[]{:S(2)}, u32[]{:S(2)}) collective-permute-start(f32[2,768]{1,0:T(2,128)S(1)} %pad_maximum_fusion.2), channel_id=1, source_target_pairs={{0,1},{1,0},{2,3},{3,2},{4,5},{5,4},{6,7},{7,6},{8,9},{9,8},{10,11... | collective-permute-start | bytes 18440 | tf_op jit(solution)/shard_map/ppermute | solution.py:986
  133.9 17.6 %collective-permute-start.23 = (bf16[48,3072]{1,0:T(8,128)(2,1)S(1)}, bf16[48,3072]{1,0:T(8,128)(2,1)S(1)}, u32[]{:S(2)}, u32[]{:S(2)}) collective-permute-start(bf16[48,3072]{1,0:T(8,128)(2,1)S(1)} %far_sum.1), channel_id=1, source_target_pairs={{0,16},{2,18},{4,20},{6,22},{8,24},{10,26},{12,28},{14,30},{16,0},... | collective-permute-start | bytes 884744 | tf_op jit(solution)/shard_map/ppermute | solution.py:825
  136.8 10.9 %collective-permute-start.20 = (bf16[96,1536]{1,0:T(8,128)(2,1)S(1)}, bf16[96,1536]{1,0:T(8,128)(2,1)S(1)}, u32[]{:S(2)}, u32[]{:S(2)}) collective-permute-start(bf16[96,1536]{1,0:T(8,128)(2,1)S(1)} %get-tuple-element.294), channel_id=1, source_target_pairs={{0,4},{2,6},{4,0},{6,2},{8,12},{10,14},{12,8},{14,10},{16,20},{18,... | collective-permute-start | bytes 884744 | tf_op jit(solution)/shard_map/ppermute | solution.py:825
  138.4 9.3 %collective-permute-start.21 = (bf16[96,1536]{1,0:T(8,128)(2,1)S(1)}, bf16[96,1536]{1,0:T(8,128)(2,1)S(1)}, u32[]{:S(2)}, u32[]{:S(2)}) collective-permute-start(bf16[96,1536]{1,0:T(8,128)(2,1)S(1)} %get-tuple-element.295), channel_id=1, source_target_pairs={{0,2},{2,0},{4,6},{6,4},{8,10},{10,8},{12,14},{14,12},{16,18},{18,... | collective-permute-start | bytes 884744 | tf_op jit(solution)/shard_map/ppermute | solution.py:825
  139.9 7.8 %collective-permute-start.19 = (f32[2,768]{1,0:T(2,128)S(1)}, f32[2,768]{1,0:T(2,128)S(1)}, u32[]{:S(2)}, u32[]{:S(2)}) collective-permute-start(f32[2,768]{1,0:T(2,128)S(1)} %fusion.1), channel_id=1, source_target_pairs={{0,2},{2,0},{4,6},{6,4},{8,10},{10,8},{12,14},{14,12},{16,18},{18,... | collective-permute-start | bytes 18440 | tf_op jit(solution)/shard_map/ppermute | solution.py:825
  147.8 3.7 %collective-permute-start.22 = (f32[2,768]{1,0:T(2,128)S(1)}, f32[2,768]{1,0:T(2,128)S(1)}, u32[]{:S(2)}, u32[]{:S(2)}) collective-permute-start(f32[2,768]{1,0:T(2,128)S(1)} %fusion.4), channel_id=1, source_target_pairs={{0,4},{2,6},{4,0},{6,2},{8,12},{10,14},{12,8},{14,10},{16,20},{18,... | collective-permute-start | bytes 18440 | tf_op jit(solution)/shard_map/ppermute | solution.py:825
  148.5 12.5 %collective-permute-start.27 = (bf16[48,1536]{1,0:T(8,128)(2,1)S(1)}, bf16[48,1536]{1,0:T(8,128)(2,1)S(1)}, u32[]{:S(2)}, u32[]{:S(2)}) collective-permute-start(bf16[48,1536]{1,0:T(8,128)(2,1)S(1)} %get-tuple-element.307), channel_id=1, source_target_pairs={{0,8},{2,10},{4,12},{6,14},{8,0},{10,2},{12,4},{14,6},{16,24},{18,... | collective-permute-start | bytes 442376 | tf_op jit(solution)/shard_map/ppermute | solution.py:825
  150.2 10.9 %collective-permute-start.28 = (bf16[48,1536]{1,0:T(8,128)(2,1)S(1)}, bf16[48,1536]{1,0:T(8,128)(2,1)S(1)}, u32[]{:S(2)}, u32[]{:S(2)}) collective-permute-start(bf16[48,1536]{1,0:T(8,128)(2,1)S(1)} %get-tuple-element.308), channel_id=1, source_target_pairs={{0,16},{2,18},{4,20},{6,22},{8,24},{10,26},{12,28},{14,30},{16,0},... | collective-permute-start | bytes 442376 | tf_op jit(solution)/shard_map/ppermute | solution.py:825
  151.5 6.1 %collective-permute-start.26 = (f32[2,768]{1,0:T(2,128)S(1)}, f32[2,768]{1,0:T(2,128)S(1)}, u32[]{:S(2)}, u32[]{:S(2)}) collective-permute-start(f32[2,768]{1,0:T(2,128)S(1)} %add.29), channel_id=1, source_target_pairs={{0,24},{2,26},{4,28},{6,30},{8,16},{10,18},{12,20},{14,22},{16,8},... | collective-permute-start | bytes 18440 | tf_op jit(solution)/shard_map/ppermute | solution.py:825
  154.4 6.1 %collective-permute-start.25 = (f32[2,768]{1,0:T(2,128)S(1)}, f32[2,768]{1,0:T(2,128)S(1)}, u32[]{:S(2)}, u32[]{:S(2)}) collective-permute-start(f32[2,768]{1,0:T(2,128)S(1)} %add.29), channel_id=1, source_target_pairs={{0,16},{2,18},{4,20},{6,22},{8,24},{10,26},{12,28},{14,30},{16,0},... | collective-permute-start | bytes 18440 | tf_op jit(solution)/shard_map/ppermute | solution.py:825
  154.6 5.8 %collective-permute-start.24 = (f32[2,768]{1,0:T(2,128)S(1)}, f32[2,768]{1,0:T(2,128)S(1)}, u32[]{:S(2)}, u32[]{:S(2)}) collective-permute-start(f32[2,768]{1,0:T(2,128)S(1)} %add.29), channel_id=1, source_target_pairs={{0,8},{2,10},{4,12},{6,14},{8,0},{10,2},{12,4},{14,6},{16,24},{18,... | collective-permute-start | bytes 18440 | tf_op jit(solution)/shard_map/ppermute | solution.py:825
  157.6 7.1 %collective-permute-start.29 = (bf16[48,1536]{1,0:T(8,128)(2,1)S(1)}, bf16[48,1536]{1,0:T(8,128)(2,1)S(1)}, u32[]{:S(2)}, u32[]{:S(2)}) collective-permute-start(bf16[48,1536]{1,0:T(8,128)(2,1)S(1)} %get-tuple-element.309), channel_id=1, source_target_pairs={{0,24},{2,26},{4,28},{6,30},{8,16},{10,18},{12,20},{14,22},{16,8},... | collective-permute-start | bytes 442376 | tf_op jit(solution)/shard_map/ppermute | solution.py:825
  (4 other events, 12.8 us)
